TPU v7x, 32 devices: a whole 2x2x4 slice. The times are simulated.
32 devices in a mesh: groups: 2 (over x), seq: 16 (over z, y, core).
Axes of the slice: x: 2, y: 2, z: 4, core: 2. Of those that a mesh axis runs over, the one named last changes fastest.
Arguments:
- features: bfloat16 [4, 16384, 384], P('groups', 'seq'), parts along dimension 0, may hold values from -6 to 6
- first_expand: bfloat16 [768, 1536], replicated, may hold values from -0.21875 to 0.21875
- first_contract: bfloat16 [1536, 768], replicated, may hold values from -0.15625 to 0.15625
- first_gain: float32 [1536], replicated, may hold values from 0.25 to 1.75
- first_shift: float32 [1536], replicated, may hold values from -3 to 3
- first_keep: float32 [768], replicated, may hold values from -1 to 2
- first_bias: float32 [768], replicated, may hold values from -2 to 2
- second_expand: bfloat16 [768, 1536], replicated, may hold values from -0.21875 to 0.21875
- second_contract: bfloat16 [1536, 768], replicated, may hold values from -0.15625 to 0.15625
- second_gain: float32 [1536], replicated, may hold values from 0.25 to 1.75
- second_shift: float32 [1536], replicated, may hold values from -3 to 3
- second_keep: float32 [768], replicated, may hold values from -1 to 2
- second_bias: float32 [768], replicated, may hold values from -2 to 2
Outputs:
- mixed: bfloat16 [4, 16384, 384], P('groups', 'seq'), parts along dimension 0
There are 2 independent parts, one for each index of `groups`. A program takes and returns all parts, laid end to end along the dimension named above; an argument that names none is the same for every part. Nothing has to cross between parts.
All inputs are finite; a program needn't handle non-finite values.
Results may differ from a plain program's by a relative error of at most 0.0057.
Values may be sent and summed in bfloat16 or wider, within the bound.
No kernel may reach another device: no remote copies, remote signals or barrier semaphores. Data moves between devices by JAX's collectives and lax.ppermute only.
A program may use at most 64 MiB of HBM per device.

v0:
```python
import jax
import jax.numpy as jnp
from jax import lax
from jax.sharding import PartitionSpec as P


def swapped(value, axis, stride):
    mask = 2**stride
    pairs = [(source, source ^ mask) for source in range(lax.axis_size(axis))]
    return lax.ppermute(value, axis, pairs)


def switch_unit(pairs, expand, contract, gain, shift, keep, bias):
    width = pairs.shape[-1]
    flat = pairs.reshape(-1, width)
    hidden = jnp.dot(flat, expand, preferred_element_type=jnp.float32)
    center = hidden - jnp.mean(hidden, axis=-1, keepdims=True)
    spread = jnp.mean(center * center, axis=-1, keepdims=True)
    normed = center * lax.rsqrt(spread + 1e-05) * gain + shift
    active = jax.nn.gelu(normed).astype(jnp.bfloat16)
    result = (
        jax.nn.sigmoid(keep) * flat.astype(jnp.float32)
        + jnp.dot(active, contract, preferred_element_type=jnp.float32)
        + bias
    )
    return result.astype(jnp.bfloat16).reshape(pairs.shape)


def per_device(
    features,
    first_expand,
    first_contract,
    first_gain,
    first_shift,
    first_keep,
    first_bias,
    second_expand,
    second_contract,
    second_gain,
    second_shift,
    second_keep,
    second_bias,
):
    first_params = (first_expand, first_contract, first_gain, first_shift, first_keep, first_bias)
    second_params = (
        second_expand,
        second_contract,
        second_gain,
        second_shift,
        second_keep,
        second_bias,
    )
    width = features.shape[-1]
    rows_here = features.shape[1]
    devices = lax.axis_size("seq")
    slots = rows_here // devices
    current = features
    other = swapped(current, "seq", 3)
    upper = lax.axis_index("seq") // 8 % 2 == 1
    lower_rows = jnp.where(upper, other, current)
    upper_rows = jnp.where(upper, current, other)
    result = switch_unit(jnp.concatenate([lower_rows, upper_rows], axis=-1), *first_params)
    current = jnp.where(upper, result[..., width:], result[..., :width])
    received = lax.all_to_all(
        current.reshape(2, slots, devices, width), "seq", split_axis=2, concat_axis=2, tiled=True
    )
    pairs = received.reshape(2, rows_here // 2, 2 * width)
    result = switch_unit(pairs, *second_params)
    return result.reshape(2, rows_here, width)


def solution(mesh):
    return jax.shard_map(
        per_device,
        mesh=mesh,
        in_specs=(
            P("groups", "seq", None),
            P(),
            P(),
            P(),
            P(),
            P(),
            P(),
            P(),
            P(),
            P(),
            P(),
            P(),
            P(),
        ),
        out_specs=P("groups", "seq", None),
        check_vma=False,
    )
```

profile of v0, /device:TPU:13, one launch (start us, length us, event | category | flops | bytes accessed | tf_op | source)
XLA Modules:
  0.0 160.4 jit_solution(7510748348630885469)
XLA Ops:
  0.0 0.0 copy-start
  0.0 2.3 %collective-permute-start = (bf16[2,1024,384]{2,1,0:T(8,128)(2,1)}, bf16[2,1024,384]{2,1,0:T(8,128)(2,1)}, u32[]{:S(2)}, u32[]{:S(2)}) collective-permute-start(bf16[2,1024,384]{2,1,0:T(8,128)(2,1)} %param.13), channel_id=1, source_target_pairs={{0,8},{1,9},{2,10},{3,11},{4,12},{5,13},{6,14},{7,15},{8,0},{9,1},... | collective-permute-start | bytes 4718600 | tf_op jit(solution)/shard_map/ppermute | solution.py:10
  2.3 0.7 add_divide_fusion
  3.0 67.3 %collective-permute-done = bf16[2,1024,384]{2,1,0:T(8,128)(2,1)} collective-permute-done((bf16[2,1024,384]{2,1,0:T(8,128)(2,1)}, bf16[2,1024,384]{2,1,0:T(8,128)(2,1)}, u32[]{:S(2)}, u32[]{:S(2)}) %collective-permute-start) | collective-permute-done | bytes 1572896 | tf_op jit(solution)/shard_map/ppermute | solution.py:10
  70.3 2.2 %broadcast_select_fusion.1 = (bf16[2,1024,384]{2,1,0:T(8,128)(2,1)S(1)}, bf16[2,1024,384]{2,1,0:T(8,128)(2,1)S(1)}) fusion(bf16[2,1024,384]{2,1,0:T(8,128)(2,1)} %collective-permute-done, bf16[2,1024,384]{2,1,0:T(8,128)(2,1)} %param.13, pred[]{:T(512)S(6)} %eq.5), kind=kLoop, calls=%fused_computation.27 | loop fusion | flops 1572864 | bytes 6291457 | tf_op jit(solution)/shard_map/jit(_where)/select_n | solution.py:60
  72.5 0.3 pad_maximum_fusion
  72.8 0.0 copy-done
  72.8 5.3 %fusion.32 = (f32[2048]{0:T(1024)S(1)}, f32[2048,1536]{0,1:T(8,128)S(1)}) fusion(bf16[2048,768]{1,0:T(8,128)(2,1)S(1)} %bitcast.12, bf16[768,1536]{1,0:T(8,128)(2,1)S(1)} %copy-done), kind=kOutput, calls=%fused_computation.42 | convolution fusion | flops 4834981888 | bytes 18096128 | tf_op jit(solution)/shard_map/dot_general | solution.py:16
  78.1 0.0 copy-start.4
  78.2 0.0 copy-start.5
  78.2 0.0 copy-start.8
  78.2 1.3 multiply_reduce_fusion
  79.5 0.0 copy-done.4
  79.5 0.0 copy-done.5
  79.5 11.5 %add_convert_fusion = bf16[2048,768]{1,0:T(8,128)(2,1)S(1)} fusion(bf16[2048,768]{1,0:T(8,128)(2,1)S(1)} %bitcast.13, f32[768]{0:T(1024)S(1)} %copy-done.8, f32[768]{0:T(1024)S(1)} %add_divide_fusion, bf16[1536,768]{1,0:T(8,128)(2,1)} %param.15, f32[2048,1536]{0,1:T(8,128)S(1)} %get-tuple-element.8, f32[1536]{0:T(1024)S(1)} %copy-done.4, ...), kind=kOutput, calls=%fused_computation.20 | convolution fusion | flops 4880596992 | bytes 21268480 | tf_op jit(solution)/shard_map/dot_general | solution.py:23
  91.1 0.0 copy-start.2
  91.1 0.2 slice_select_fusion
  91.3 1.5 copy.15
  92.8 7.2 %all-to-all-start = ((bf16[2,64,16,384]{3,1,0,2:T(8,128)(2,1)}), bf16[2,64,16,384]{3,1,0,2:T(8,128)(2,1)}, u32[]{:S(2)}, u32[]{:S(2)}) async-start(bf16[2,64,16,384]{3,1,0,2:T(8,128)(2,1)} %copy.15), calls=%async_computation | async-start | bytes 3145728 | tf_op jit(solution)/shard_map/all_to_all | solution.py:64
  100.0 36.3 %all-to-all-done = bf16[2,64,16,384]{3,1,0,2:T(8,128)(2,1)} async-done(((bf16[2,64,16,384]{3,1,0,2:T(8,128)(2,1)}), bf16[2,64,16,384]{3,1,0,2:T(8,128)(2,1)}, u32[]{:S(2)}, u32[]{:S(2)}) %all-to-all-start) | async-done | bytes 1572896 | tf_op jit(solution)/shard_map/all_to_all | solution.py:64
  136.3 3.5 %copy.16 = bf16[2,64,16,384]{3,2,1,0:T(8,128)(2,1)} copy(bf16[2,64,16,384]{3,1,0,2:T(8,128)(2,1)} %all-to-all-done) | data formatting | bytes 3145728 | tf_op jit(solution)/shard_map/all_to_all | solution.py:64
  139.7 3.6 %reshape_reshape.6 = bf16[1024,768]{1,0:T(8,128)(2,1)} reshape(bf16[2,64,16,384]{3,2,1,0:T(8,128)(2,1)} %copy.16) | data formatting | bytes 3145728 | tf_op jit(solution)/shard_map/reshape;reshape | solution.py:15
  143.4 4.8 %fusion.33 = (f32[1024]{0:T(1024)S(1)}, f32[1024,1536]{1,0:T(8,128)S(1)}) fusion(bf16[1024,768]{1,0:T(8,128)(2,1)} %reshape_reshape.6, bf16[768,1536]{1,0:T(8,128)(2,1)} %param.20), kind=kOutput, calls=%fused_computation.43 | convolution fusion | flops 2417490944 | bytes 10227712 | tf_op jit(solution)/shard_map/dot_general | solution.py:16
  148.2 0.0 copy-start.3
  148.2 0.0 copy-start.6
  148.2 0.0 copy-start.7
  148.2 0.0 copy-start.9
  148.3 0.8 multiply_reduce_fusion.1
  149.0 0.6 copy-done.1
  149.6 0.7 copy-done.3
  150.3 6.4 %add_convert_fusion.1 = bf16[1024,768]{1,0:T(8,128)(2,1)} fusion(bf16[1024,768]{1,0:T(8,128)(2,1)S(1)} %copy-done.1, f32[768]{0:T(1024)S(1)} %copy-done.9, f32[768]{0:T(1024)S(1)} %add_divide_fusion.1, bf16[1536,768]{1,0:T(8,128)(2,1)S(1)} %copy-done.3, f32[1024,1536]{1,0:T(8,128)S(1)} %get-tuple-element.10, f32[1536]{0:T(1024)S(1)} %copy-done.6, ...), kind=kOutput, calls=%fused_computation.23 | convolution fusion | flops 2440298496 | bytes 11823104 | tf_op jit(solution)/shard_map/dot_general | solution.py:23
  156.7 3.6 %reshape_reshape.7 = bf16[2,1024,384]{2,1,0:T(8,128)(2,1)} reshape(bf16[1024,768]{1,0:T(8,128)(2,1)} %add_convert_fusion.1) | data formatting | bytes 3145728 | tf_op jit(solution)/shard_map/reshape;reshape | solution.py:69
  (11 shorter events, 0.0 us)
Async XLA Ops:
  0.0 72.8 %copy-start = (bf16[768,1536]{1,0:T(8,128)(2,1)S(1)}, bf16[768,1536]{1,0:T(8,128)(2,1)}, u32[]{:S(2)}) copy-start(bf16[768,1536]{1,0:T(8,128)(2,1)} %param.14) | copy-start | bytes 7077892
  0.0 70.3 %collective-permute-start = (bf16[2,1024,384]{2,1,0:T(8,128)(2,1)}, bf16[2,1024,384]{2,1,0:T(8,128)(2,1)}, u32[]{:S(2)}, u32[]{:S(2)}) collective-permute-start(bf16[2,1024,384]{2,1,0:T(8,128)(2,1)} %param.13), channel_id=1, source_target_pairs={{0,8},{1,9},{2,10},{3,11},{4,12},{5,13},{6,14},{7,15},{8,0},{9,1},... | collective-permute-start | bytes 4718600 | tf_op jit(solution)/shard_map/ppermute | solution.py:10
  78.1 1.4 copy-start.4
  78.2 1.4 copy-start.5
  78.2 1.4 copy-start.8
  91.1 8.9 %copy-start.2 = (f32[768]{0:T(1024)S(1)}, f32[768]{0:T(1024)}, u32[]{:S(2)}) copy-start(f32[768]{0:T(1024)} %param.24) | copy-start | bytes 9220
  92.8 43.5 %all-to-all-start = ((bf16[2,64,16,384]{3,1,0,2:T(8,128)(2,1)}), bf16[2,64,16,384]{3,1,0,2:T(8,128)(2,1)}, u32[]{:S(2)}, u32[]{:S(2)}) async-start(bf16[2,64,16,384]{3,1,0,2:T(8,128)(2,1)} %copy.15), calls=%async_computation | async-start | bytes 3145728 | tf_op jit(solution)/shard_map/all_to_all | solution.py:64
  148.2 1.4 copy-start.1
  148.2 2.1 %copy-start.3 = (bf16[1536,768]{1,0:T(8,128)(2,1)S(1)}, bf16[1536,768]{1,0:T(8,128)(2,1)}, u32[]{:S(2)}) copy-start(bf16[1536,768]{1,0:T(8,128)(2,1)} %param.21) | copy-start | bytes 7077892
  148.2 2.1 %copy-start.6 = (f32[1536]{0:T(1024)S(1)}, f32[1536]{0:T(1024)}, u32[]{:S(2)}) copy-start(f32[1536]{0:T(1024)} %param.23) | copy-start | bytes 18436
  148.2 2.1 %copy-start.7 = (f32[1536]{0:T(1024)S(1)}, f32[1536]{0:T(1024)}, u32[]{:S(2)}) copy-start(f32[1536]{0:T(1024)} %param.22) | copy-start | bytes 18436
  148.2 2.1 %copy-start.9 = (f32[768]{0:T(1024)S(1)}, f32[768]{0:T(1024)}, u32[]{:S(2)}) copy-start(f32[768]{0:T(1024)} %param.25) | copy-start | bytes 9220
where the time goes:
time: 161 us; the launch traced here: 160 us
  waiting for transfers between devices  104 us (65%)
  matrix products  28.1 us (17%)
  local copies, waits for them, and re-layouts  13.6 us (8%)
  starting transfers between devices  9.47 us (6%)
  other arithmetic  5.4 us (3%)
    ppermute x1, waiting for transfers between devices, swapped(): return lax.ppermute(value, axis, pairs)  67.3 us
    all_to_all x1, waiting for transfers between devices, per_device(): lax.all_to_all(current.reshape(2, slots, devices, width), 'seq', split_ax...  36.3 us
    dot_general x2, matrix products, switch_unit(): jnp.dot(active, contract, preferred_element_type=jnp.float32)  17.9 us
    dot_general x2, matrix products, switch_unit(): hidden = jnp.dot(flat, expand, preferred_element_type=jnp.float32)  10.2 us
    all_to_all x1, starting transfers between devices, per_device(): lax.all_to_all(current.reshape(2, slots, devices, width), 'seq', split_ax...  7.16 us
    another operation x1, local copies, waits for them, and re-layouts, switch_unit(): flat = pairs.reshape(-1, width)  3.64 us
    another operation x1, local copies, waits for them, and re-layouts, per_device(): return result.reshape(2, rows_here, width)  3.62 us
    all_to_all x1, local copies, waits for them, and re-layouts, per_device(): lax.all_to_all(current.reshape(2, slots, devices, width), 'seq', split_ax...  3.47 us
  transfers between devices with their start and end apart: 2, of which 2 were waited for; matrix products, arithmetic and copies ran while one was open for 0% of the time, Pallas kernels for 0%

commit v1 on v0

v1 whole, which is shorter than its diff:
```python
import jax
import jax.numpy as jnp
from jax import lax
from jax.sharding import PartitionSpec as P

REACH = 8


def switch_unit(flat, expand, contract, gain, shift, keep, bias):
    hidden = jnp.dot(flat, expand, preferred_element_type=jnp.float32)
    center = hidden - jnp.mean(hidden, axis=-1, keepdims=True)
    spread = jnp.mean(center * center, axis=-1, keepdims=True)
    normed = center * lax.rsqrt(spread + 1e-05) * gain + shift
    active = jax.nn.gelu(normed).astype(jnp.bfloat16)
    result = (
        jax.nn.sigmoid(keep) * flat.astype(jnp.float32)
        + jnp.dot(active, contract, preferred_element_type=jnp.float32)
        + bias
    )
    return result.astype(jnp.bfloat16)


def per_device(features, *params):
    first_params, second_params = params[:6], params[6:]
    streams, rows_here, width = features.shape
    devices = lax.axis_size("seq")
    slots = rows_here // devices
    outgoing = features.reshape(streams, slots, devices, width).transpose(2, 0, 1, 3)
    outgoing = outgoing.reshape(devices, streams * slots, width)
    received = lax.all_to_all(outgoing, "seq", split_axis=0, concat_axis=0, tiled=True)
    clusters = devices // (2 * REACH)
    halves = received.reshape(clusters, 2, REACH, streams * slots, width)
    pairs = jnp.concatenate([halves[:, 0], halves[:, 1]], axis=-1).reshape(-1, 2 * width)
    mid = switch_unit(pairs, *first_params)
    mid = mid.reshape(clusters, REACH // 2, 2, streams * slots, 2, width)
    pairs = mid.transpose(0, 4, 1, 3, 2, 5).reshape(-1, 2 * width)
    result = switch_unit(pairs, *second_params)
    result = result.reshape(devices // 2, streams, slots, 2, width)
    return result.transpose(1, 2, 0, 3, 4).reshape(streams, rows_here, width)


def solution(mesh):
    return jax.shard_map(
        per_device,
        mesh=mesh,
        in_specs=(P("groups", "seq", None),) + (P(),) * 12,
        out_specs=P("groups", "seq", None),
        check_vma=False,
    )
```

time: 161 us -> 90 us (0.56)
  the two profiles are of different devices: /device:TPU:13 before, /device:TPU:15 now
where the time goes in v1:
time: 90 us; the launch traced here: 89.5 us
  waiting for transfers between devices  36.2 us (40%)
  local copies, waits for them, and re-layouts  26.9 us (30%)
  matrix products  18.1 us (20%)
  starting transfers between devices  6.55 us (7%)
  other arithmetic  1.56 us (2%)
    all_to_all x1, waiting for transfers between devices, per_device(): lax.all_to_all(outgoing, 'seq', split_axis=0, concat_axis=0, tiled=True)  36.2 us
    dot_general x2, matrix products, switch_unit(): jnp.dot(active, contract, preferred_element_type=jnp.float32)  12.7 us
    all_to_all x1, starting transfers between devices, per_device(): lax.all_to_all(outgoing, 'seq', split_axis=0, concat_axis=0, tiled=True)  6.55 us
    dot_general x2, matrix products, switch_unit(): hidden = jnp.dot(flat, expand, preferred_element_type=jnp.float32)  5.37 us
    reshape x1, local copies, waits for them, and re-layouts, per_device(): return result.transpose(1, 2, 0, 3, 4).reshape(streams, rows_here, width)  4.64 us
    reshape x1, local copies, waits for them, and re-layouts, per_device(): result = result.reshape(devices // 2, streams, slots, 2, width)  4.38 us
    reshape x1, local copies, waits for them, and re-layouts, per_device(): mid = mid.reshape(clusters, REACH // 2, 2, streams * slots, 2, width)  4.38 us
    transpose x1, local copies, waits for them, and re-layouts, per_device(): return result.transpose(1, 2, 0, 3, 4).reshape(streams, rows_here, width)  3.63 us
  transfers between devices with their start and end apart: 1, of which 1 were waited for; matrix products, arithmetic and copies ran while one was open for 0% of the time, Pallas kernels for 0%

profile of v1, /device:TPU:15, one launch (start us, length us, event | category | flops | bytes accessed | tf_op | source)
XLA Modules:
  0.0 89.5 jit_solution(18123404356349040169)
XLA Ops:
  0.0 0.0 copy-start
  0.0 3.1 %copy.14 = bf16[16,128,384]{2,1,0:T(8,128)(2,1)} copy(bf16[16,128,384]{2,0,1:T(8,128)(2,1)} %bitcast.21) | data formatting | bytes 3145728 | tf_op jit(solution)/shard_map/reshape | solution.py:29
  3.1 6.6 %all-to-all-start = ((bf16[16,128,384]{2,1,0:T(8,128)(2,1)}), bf16[16,128,384]{2,1,0:T(8,128)(2,1)}, u32[]{:S(2)}, u32[]{:S(2)}) async-start(bf16[16,128,384]{2,1,0:T(8,128)(2,1)} %copy.14), calls=%async_computation | async-start | bytes 3145728 | tf_op jit(solution)/shard_map/all_to_all | solution.py:30
  9.6 0.0 copy-done.1
  9.7 0.0 copy-done.2
  9.7 36.2 %all-to-all-done = bf16[16,128,384]{2,1,0:T(8,128)(2,1)} async-done(((bf16[16,128,384]{2,1,0:T(8,128)(2,1)}), bf16[16,128,384]{2,1,0:T(8,128)(2,1)}, u32[]{:S(2)}, u32[]{:S(2)}) %all-to-all-start) | async-done | bytes 1572896 | tf_op jit(solution)/shard_map/all_to_all | solution.py:30
  45.9 1.6 %fusion.34 = (bf16[1,1,8,128,384]{4,3,2,1,0:T(8,128)(2,1)S(1)}, bf16[1,1,8,128,384]{4,3,2,1,0:T(8,128)(2,1)S(1)}) fusion(bf16[1,2,8,128,384]{4,3,2,1,0:T(8,128)(2,1)} %bitcast.3), kind=kLoop, calls=%fused_computation.41 | loop fusion | bytes 3145728 | tf_op jit(solution)/shard_map/slice | solution.py:33
  47.5 0.0 copy-done
  47.5 2.7 %fusion.35 = (f32[1024]{0:T(1024)S(1)}, f32[1024,1536]{1,0:T(8,128)S(1)}) fusion(bf16[768,1536]{1,0:T(8,128)(2,1)S(1)} %copy-done, bf16[1024,384]{1,0:T(8,128)(2,1)S(1)} %bitcast.26, bf16[1024,384]{1,0:T(8,128)(2,1)S(1)} %bitcast.24), kind=kOutput, calls=%fused_computation.42 | convolution fusion | flops 2420636672 | bytes 10227712 | tf_op jit(solution)/shard_map/dot_general | solution.py:10
  50.2 0.0 copy-start.3
  50.2 0.0 copy-start.6
  50.2 0.0 copy-start.7
  50.2 0.0 copy-start.10
  50.2 0.8 multiply_reduce_fusion.1
  51.0 0.8 copy-done.3
  51.9 0.0 copy-done.7
  51.9 6.4 %add_convert_fusion.1 = bf16[1024,768]{1,0:T(8,128)(2,1)} fusion(f32[768]{0:T(1024)S(1)} %copy-done.10, f32[768]{0:T(1024)S(1)} %add_divide_fusion, bf16[1536,768]{1,0:T(8,128)(2,1)S(1)} %copy-done.3, f32[1024,1536]{1,0:T(8,128)S(1)} %get-tuple-element.8, f32[1536]{0:T(1024)S(1)} %copy-done.6, f32[1536]{0:T(1024)S(1)} %copy-done.7, ...), kind=kOutput, calls=%fused_computation.21 | convolution fusion | flops 2442657792 | bytes 11823104 | tf_op jit(solution)/shard_map/dot_general | solution.py:17
  58.3 4.4 %reshape.61 = bf16[1,4,2,128,2,384]{5,4,3,2,1,0:T(2,128)(2,1)} reshape(bf16[1024,768]{1,0:T(8,128)(2,1)} %add_convert_fusion.1) | data formatting | bytes 3145728 | tf_op jit(solution)/shard_map/reshape | solution.py:35
  62.6 3.2 %copy.15 = bf16[1,2,4,128,2,384]{5,4,3,2,1,0:T(2,128)(2,1)S(1)} copy(bf16[1,2,4,128,2,384]{5,1,3,4,2,0:T(2,128)(2,1)} %bitcast.18) | data formatting | bytes 3145728 | tf_op jit(solution)/shard_map/transpose | solution.py:36
  65.8 0.3 copy.17
  66.1 0.0 copy-done.4
  66.1 2.7 %fusion.36 = (f32[1024]{0:T(1024)S(1)}, f32[1024,1536]{1,0:T(8,128)S(1)}) fusion(bf16[1024,768]{1,0:T(8,128)(2,1)S(1)} %bitcast.22, bf16[768,1536]{1,0:T(8,128)(2,1)S(1)} %copy-done.4), kind=kOutput, calls=%fused_computation.43 | convolution fusion | flops 2417490944 | bytes 10227712 | tf_op jit(solution)/shard_map/dot_general | solution.py:10
  68.8 0.0 copy-start.5
  68.8 0.0 copy-start.8
  68.9 0.0 copy-start.9
  68.9 0.0 copy-start.11
  68.9 0.8 multiply_reduce_fusion
  69.7 0.8 copy-done.5
  70.5 6.4 %add_convert_fusion = bf16[1024,768]{1,0:T(8,128)(2,1)} fusion(bf16[1024,768]{1,0:T(8,128)(2,1)S(1)} %bitcast.23, f32[768]{0:T(1024)S(1)} %copy-done.11, f32[768]{0:T(1024)S(1)} %add_divide_fusion.1, bf16[1536,768]{1,0:T(8,128)(2,1)S(1)} %copy-done.5, f32[1024,1536]{1,0:T(8,128)S(1)} %get-tuple-element.10, f32[1536]{0:T(1024)S(1)} %copy-done.8, ...), kind=kOutput, calls=%fused_computation.20 | convolution fusion | flops 2440298496 | bytes 11823104 | tf_op jit(solution)/shard_map/dot_general | solution.py:17
  76.9 4.4 %reshape.63 = bf16[8,2,64,2,384]{4,3,2,1,0:T(2,128)(2,1)} reshape(bf16[1024,768]{1,0:T(8,128)(2,1)} %add_convert_fusion) | data formatting | bytes 3145728 | tf_op jit(solution)/shard_map/reshape | solution.py:38
  81.3 3.6 %copy.16 = bf16[2,64,8,2,384]{4,3,2,1,0:T(2,128)(2,1)} copy(bf16[2,64,8,2,384]{4,3,1,0,2:T(2,128)(2,1)} %bitcast.20) | data formatting | bytes 3145728 | tf_op jit(solution)/shard_map/transpose | solution.py:39
  84.9 4.6 %reshape.64 = bf16[2,1024,384]{2,1,0:T(8,128)(2,1)} reshape(bf16[2,64,8,2,384]{4,3,2,1,0:T(2,128)(2,1)} %copy.16) | data formatting | bytes 3145728 | tf_op jit(solution)/shard_map/reshape | solution.py:39
  (14 shorter events, 0.1 us)
Async XLA Ops:
  0.0 47.5 %copy-start = (bf16[768,1536]{1,0:T(8,128)(2,1)S(1)}, bf16[768,1536]{1,0:T(8,128)(2,1)}, u32[]{:S(2)}) copy-start(bf16[768,1536]{1,0:T(8,128)(2,1)} %param.14) | copy-start | bytes 7077892
  0.0 9.6 %copy-start.1 = (f32[768]{0:T(1024)S(1)}, f32[768]{0:T(1024)}, u32[]{:S(2)}) copy-start(f32[768]{0:T(1024)} %param.18) | copy-start | bytes 9220
  0.0 9.7 %copy-start.2 = (f32[768]{0:T(1024)S(1)}, f32[768]{0:T(1024)}, u32[]{:S(2)}) copy-start(f32[768]{0:T(1024)} %param.24) | copy-start | bytes 9220
  3.1 42.8 %all-to-all-start = ((bf16[16,128,384]{2,1,0:T(8,128)(2,1)}), bf16[16,128,384]{2,1,0:T(8,128)(2,1)}, u32[]{:S(2)}, u32[]{:S(2)}) async-start(bf16[16,128,384]{2,1,0:T(8,128)(2,1)} %copy.14), calls=%async_computation | async-start | bytes 3145728 | tf_op jit(solution)/shard_map/all_to_all | solution.py:30
  50.2 1.7 %copy-start.3 = (bf16[1536,768]{1,0:T(8,128)(2,1)S(1)}, bf16[1536,768]{1,0:T(8,128)(2,1)}, u32[]{:S(2)}) copy-start(bf16[1536,768]{1,0:T(8,128)(2,1)} %param.15) | copy-start | bytes 7077892
  50.2 1.7 %copy-start.6 = (f32[1536]{0:T(1024)S(1)}, f32[1536]{0:T(1024)}, u32[]{:S(2)}) copy-start(f32[1536]{0:T(1024)} %param.17) | copy-start | bytes 18436
  50.2 1.6 %copy-start.7 = (f32[1536]{0:T(1024)S(1)}, f32[1536]{0:T(1024)}, u32[]{:S(2)}) copy-start(f32[1536]{0:T(1024)} %param.16) | copy-start | bytes 18436
  50.2 1.6 %copy-start.10 = (f32[768]{0:T(1024)S(1)}, f32[768]{0:T(1024)}, u32[]{:S(2)}) copy-start(f32[768]{0:T(1024)} %param.19) | copy-start | bytes 9220
  62.6 3.5 %copy-start.4 = (bf16[768,1536]{1,0:T(8,128)(2,1)S(1)}, bf16[768,1536]{1,0:T(8,128)(2,1)}, u32[]{:S(2)}) copy-start(bf16[768,1536]{1,0:T(8,128)(2,1)} %param.20) | copy-start | bytes 7077892
  68.8 1.7 %copy-start.5 = (bf16[1536,768]{1,0:T(8,128)(2,1)S(1)}, bf16[1536,768]{1,0:T(8,128)(2,1)}, u32[]{:S(2)}) copy-start(bf16[1536,768]{1,0:T(8,128)(2,1)} %param.21) | copy-start | bytes 7077892
  68.8 1.7 %copy-start.8 = (f32[1536]{0:T(1024)S(1)}, f32[1536]{0:T(1024)}, u32[]{:S(2)}) copy-start(f32[1536]{0:T(1024)} %param.23) | copy-start | bytes 18436
  68.9 1.6 %copy-start.9 = (f32[1536]{0:T(1024)S(1)}, f32[1536]{0:T(1024)}, u32[]{:S(2)}) copy-start(f32[1536]{0:T(1024)} %param.22) | copy-start | bytes 18436
  68.9 1.6 %copy-start.11 = (f32[768]{0:T(1024)S(1)}, f32[768]{0:T(1024)}, u32[]{:S(2)}) copy-start(f32[768]{0:T(1024)} %param.25) | copy-start | bytes 9220

commit v2 on v1

v2 whole, which is shorter than its diff:
```python
import functools

import jax
import jax.numpy as jnp
from jax import lax
from jax.experimental import pallas as pl
from jax.experimental.pallas import tpu as pltpu
from jax.sharding import PartitionSpec as P

REACH = 8
MIB = 1 << 20


def gelu(n):
    root = 0.7978845608028654
    half = 0.5 * n
    return half + half * jnp.tanh(n * (root + (root * 0.044715) * (n * n)))


def switch_rows(s, expand, contract, wide, narrow):
    hidden = jnp.dot(s, expand, preferred_element_type=jnp.float32)
    center = hidden - jnp.mean(hidden, axis=-1, keepdims=True)
    spread = jnp.mean(center * center, axis=-1, keepdims=True)
    normed = center * lax.rsqrt(spread + 1e-05) * wide[0:1] + wide[1:2]
    active = gelu(normed).astype(jnp.bfloat16)
    result = (
        narrow[0:1] * s.astype(jnp.float32)
        + jnp.dot(active, contract, preferred_element_type=jnp.float32)
        + narrow[1:2]
    )
    return result.astype(jnp.bfloat16)


def iota2(shape, dim):
    return lax.broadcasted_iota(jnp.int32, shape, dim)


def one_hot(hit):
    return jnp.where(hit, 1.0, 0.0).astype(jnp.bfloat16)


def sort_kernel(shards, x_ref, *outs):
    me = lax.axis_index("seq")
    tile = shards * shards
    row, col = iota2((tile, tile), 0), iota2((tile, tile), 1)
    pick = one_hot((col // shards == row % shards) & (col % shards == ((row // shards) ^ me)))
    streams, rows, _ = x_ref.shape
    for s in range(streams):
        for t in range(rows // tile):
            y = jnp.dot(pick, x_ref[s, t * tile : (t + 1) * tile], preferred_element_type=jnp.float32)
            y = y.astype(jnp.bfloat16)
            at = s * (rows // shards) + t * shards
            for mask in range(shards):
                outs[mask][at : at + shards] = y[mask * shards : (mask + 1) * shards]


def sort_rows(features, shards):
    streams, rows, width = features.shape
    block = jax.ShapeDtypeStruct((streams * rows // shards, width), features.dtype)
    return pl.pallas_call(
        functools.partial(sort_kernel, shards),
        out_shape=[block] * shards,
        in_specs=[pl.BlockSpec(memory_space=pltpu.VMEM)],
        out_specs=[pl.BlockSpec(memory_space=pltpu.VMEM)] * shards,
        compiler_params=pltpu.CompilerParams(vmem_limit_bytes=16 * MIB),
        cost_estimate=pl.CostEstimate(flops=10**9, bytes_accessed=2 * features.size * 2, transcendentals=0),
        name="sort_rows",
    )(features)


def group_blocks(refs, roles, first, second):
    me = lax.axis_index("seq")
    core, upper = me & 1, (me // REACH) & 1
    for i, ref in enumerate(refs):
        roles[(upper ^ (i // 2)) * 2 + (core ^ (i % 2))] = ref[...]
    first = [ref[...] for ref in first]
    second = [ref[...] for ref in second]
    width = roles.shape[-1]
    mids = [
        switch_rows(jnp.concatenate([roles[c], roles[2 + c]], axis=-1), *first) for c in range(2)
    ]
    ends = []
    for half in range(2):
        part = slice(half * width, (half + 1) * width)
        o = switch_rows(jnp.concatenate([mids[0][:, part], mids[1][:, part]], axis=-1), *second)
        ends += [o[:, :width], o[:, width:]]
    return ends


def group_kernel(*refs):
    blocks, first, second, out, roles = refs[:4], refs[4:8], refs[8:12], refs[12], refs[13]
    for i, end in enumerate(group_blocks(blocks, roles, first, second)):
        out[i] = end


def last_kernel(shards, groups, *refs):
    blocks, first, second = refs[:4], refs[4:8], refs[8:12]
    done, out, roles = refs[12 : 12 + groups - 1], refs[12 + groups - 1], refs[12 + groups]
    ends = group_blocks(blocks, roles, first, second)
    me = lax.axis_index("seq")
    near = (me & (REACH - 1)) >> 1
    tile = shards * shards
    row, col = iota2((tile, tile), 0), iota2((tile, tile), 1)
    group, half, core = col // (4 * shards), (col // (2 * shards)) % 2, (col // shards) % 2
    source = half * REACH + ((group ^ near) * 2 + core)
    place = one_hot((row // shards == col % shards) & (row % shards == source))
    streams, rows, _ = out.shape
    for s in range(streams):
        for t in range(rows // tile):
            at = s * (rows // shards) + t * shards
            parts = [d[i, at : at + shards] for d in done for i in range(4)]
            parts += [end[at : at + shards] for end in ends]
            y = jnp.dot(place, jnp.concatenate(parts, axis=0), preferred_element_type=jnp.float32)
            out[s, t * tile : (t + 1) * tile] = y.astype(jnp.bfloat16)


def run_group(kernel, blocks, params, extra, out_shape, name):
    rows, width = blocks[0].shape
    args = (*blocks, *params, *extra)
    hidden = params[0].shape[1]
    return pl.pallas_call(
        kernel,
        out_shape=out_shape,
        in_specs=[pl.BlockSpec(memory_space=pltpu.VMEM)] * len(args),
        out_specs=pl.BlockSpec(memory_space=pltpu.VMEM),
        scratch_shapes=[pltpu.VMEM((4, rows, width), jnp.bfloat16)],
        compiler_params=pltpu.CompilerParams(vmem_limit_bytes=32 * MIB),
        cost_estimate=pl.CostEstimate(
            flops=2 * 2 * rows * 4 * 2 * width * hidden,
            bytes_accessed=sum(a.size * a.dtype.itemsize for a in args),
            transcendentals=4 * rows * hidden,
        ),
        name=name,
    )(*args)


def packed(params):
    expand, contract, gain, shift, keep, bias = params
    return expand, contract, jnp.stack([gain, shift]), jnp.stack([jax.nn.sigmoid(keep), bias])


def exchanged(features, params, shards):
    sent = sort_rows(features, shards)
    groups = REACH // 2
    waves = [[REACH], [REACH + 1, 1]]
    for g in range(1, groups):
        waves += [[REACH + 2 * g, 2 * g], [REACH + 2 * g + 1, 2 * g + 1]]
    window = 4
    got, ends = {0: sent[0]}, []
    for i, wave in enumerate(waves):
        ops = [sent[mask] for mask in wave]
        if i >= window:
            before = waves[i - window]
            hold = [got[mask] for mask in before]
            extra = []
            held = lax.optimization_barrier((*ops, *hold, *extra))
            ops = list(held[: len(ops)])
            for mask, value in zip(before, held[len(ops) :]):
                got[mask] = value
        for mask, op in zip(wave, ops):
            pairs = [(d, d ^ mask) for d in range(shards)]
            got[mask] = lax.ppermute(op, "seq", pairs)
    for g in range(groups):
        blocks = [got[2 * g], got[2 * g + 1], got[REACH + 2 * g], got[REACH + 2 * g + 1]]
        if g < groups - 1:
            shape = jax.ShapeDtypeStruct((4, *blocks[0].shape), features.dtype)
            ends.append(run_group(group_kernel, blocks, params, (), shape, "switch_group"))
        else:
            kernel = functools.partial(last_kernel, shards, groups)
            shape = jax.ShapeDtypeStruct(features.shape, features.dtype)
            return run_group(kernel, blocks, params, tuple(ends), shape, "switch_last")


def switch_unit(flat, expand, contract, wide, narrow):
    return switch_rows(flat, expand, contract, wide, narrow)


def gathered(features, first, second):
    streams, rows_here, width = features.shape
    devices = lax.axis_size("seq")
    slots = rows_here // devices
    outgoing = features.reshape(streams, slots, devices, width).transpose(2, 0, 1, 3)
    outgoing = outgoing.reshape(devices, streams * slots, width)
    received = lax.all_to_all(outgoing, "seq", split_axis=0, concat_axis=0, tiled=True)
    clusters = devices // (2 * REACH)
    halves = received.reshape(clusters, 2, REACH, streams * slots, width)
    pairs = jnp.concatenate([halves[:, 0], halves[:, 1]], axis=-1).reshape(-1, 2 * width)
    mid = switch_unit(pairs, *first)
    mid = mid.reshape(clusters, REACH // 2, 2, streams * slots, 2, width)
    pairs = mid.transpose(0, 4, 1, 3, 2, 5).reshape(-1, 2 * width)
    result = switch_unit(pairs, *second)
    result = result.reshape(devices // 2, streams, slots, 2, width)
    return result.transpose(1, 2, 0, 3, 4).reshape(streams, rows_here, width)


def per_device(features, *params):
    first, second = packed(params[:6]), packed(params[6:])
    shards = lax.axis_size("seq")
    if shards == 2 * REACH and features.shape[1] % (shards * shards) == 0:
        return exchanged(features, (*first, *second), shards)
    return gathered(features, first, second)


def solution(mesh):
    return jax.shard_map(
        per_device,
        mesh=mesh,
        in_specs=(P("groups", "seq", None),) + (P(),) * 12,
        out_specs=P("groups", "seq", None),
        check_vma=False,
    )
```

time: 90 us -> 60.6 us (0.67)
  the two profiles are of different devices: /device:TPU:15 before, /device:TPU:0 now
where the time goes in v2:
time: 60.6 us; the launch traced here: 60.4 us
  starting transfers between devices  25.6 us (42%)
  Pallas kernels  21 us (35%)
  waiting for transfers between devices  7.01 us (12%)
  local copies, waits for them, and re-layouts  6.48 us (11%)
    ppermute x15, starting transfers between devices, exchanged(): got[mask] = lax.ppermute(op, 'seq', pairs)  25.6 us
    pallas_call x4, Pallas kernels, run_group(): pl.pallas_call(kernel, out_shape=out_shape, in_specs=[pl.BlockSpec(memory...  20.3 us
    ppermute x15, waiting for transfers between devices, exchanged(): got[mask] = lax.ppermute(op, 'seq', pairs)  7.01 us
    unnamed x28, local copies, waits for them, and re-layouts  6.44 us
  transfers between devices with their start and end apart: 15, of which 4 were waited for; matrix products, arithmetic and copies ran while one was open for 0% of the time, Pallas kernels for 23%

profile of v2, /device:TPU:0, one launch (start us, length us, event | category | flops | bytes accessed | tf_op | source)
XLA Modules:
  0.0 60.4 jit_solution(190222308924121721)
XLA Ops:
  0.0 1.4 %copy-done.5 = bf16[2,1024,384]{2,1,0:T(8,128)(2,1)S(1)} copy-done((bf16[2,1024,384]{2,1,0:T(8,128)(2,1)S(1)}, bf16[2,1024,384]{2,1,0:T(8,128)(2,1)}, u32[]{:S(2)}) %copy-start.5) | copy-done | bytes 1572888
  1.5 0.7 %sort_rows.1 = (bf16[128,384]{1,0:T(8,128)(2,1)S(1)}, bf16[128,384]{1,0:T(8,128)(2,1)S(1)}, bf16[128,384]{1,0:T(8,128)(2,1)S(1)}, bf16[128,384]{1,0:T(8,128)(2,1...) custom-call(bf16[2,1024,384]{2,1,0:T(8,128)(2,1)S(1)} %copy-done.5), custom_call_target="tpu_custom_call" | custom-call | flops 1000000000 | bytes 3145728 | tf_op jit(solution)/shard_map/sort_rows/pallas_call | solution.py:60
  2.2 5.1 %collective-permute-start = (bf16[128,384]{1,0:T(8,128)(2,1)S(1)}, bf16[128,384]{1,0:T(8,128)(2,1)S(1)}, u32[]{:S(2)}, u32[]{:S(2)}) collective-permute-start(bf16[128,384]{1,0:T(8,128)(2,1)S(1)} %get-tuple-element.38), channel_id=1, source_target_pairs={{0,10},{1,11},{2,8},{3,9},{4,14},{5,15},{6,12},{7,13},{8,2},{9,3},... | collective-permute-start | bytes 294920 | tf_op jit(solution)/shard_map/ppermute | solution.py:162
  7.2 0.5 collective-permute-start.1
  7.8 0.2 collective-permute-start.3
  7.9 1.1 %collective-permute-start.4 = (bf16[128,384]{1,0:T(8,128)(2,1)S(1)}, bf16[128,384]{1,0:T(8,128)(2,1)S(1)}, u32[]{:S(2)}, u32[]{:S(2)}) collective-permute-start(bf16[128,384]{1,0:T(8,128)(2,1)S(1)} %get-tuple-element.44), channel_id=1, source_target_pairs={{0,3},{1,2},{2,1},{3,0},{4,7},{5,6},{6,5},{7,4},{8,11},{9,10},{10,... | collective-permute-start | bytes 294920 | tf_op jit(solution)/shard_map/ppermute | solution.py:162
  9.1 2.3 %collective-permute-start.8 = (bf16[128,384]{1,0:T(8,128)(2,1)S(1)}, bf16[128,384]{1,0:T(8,128)(2,1)S(1)}, u32[]{:S(2)}, u32[]{:S(2)}) collective-permute-start(bf16[128,384]{1,0:T(8,128)(2,1)S(1)} %get-tuple-element.51), channel_id=1, source_target_pairs={{0,9},{1,8},{2,11},{3,10},{4,13},{5,12},{6,15},{7,14},{8,1},{9,0},... | collective-permute-start | bytes 294920 | tf_op jit(solution)/shard_map/ppermute | solution.py:162
  11.6 0.7 %collective-permute-done.refs_2_ = bf16[128,384]{1,0:T(8,128)(2,1)S(1)} collective-permute-done((bf16[128,384]{1,0:T(8,128)(2,1)S(1)}, bf16[128,384]{1,0:T(8,128)(2,1)S(1)}, u32[]{:S(2)}, u32[]{:S(2)}) %collective-permute-start) | collective-permute-done | bytes 98336 | tf_op jit(solution)/shard_map/ppermute | solution.py:162
  12.2 0.0 collective-permute-start.9
  12.3 2.5 %collective-permute-done.1.refs_0_ = bf16[128,384]{1,0:T(8,128)(2,1)S(1)} collective-permute-done((bf16[128,384]{1,0:T(8,128)(2,1)S(1)}, bf16[128,384]{1,0:T(8,128)(2,1)S(1)}, u32[]{:S(2)}, u32[]{:S(2)}) %collective-permute-start.1) | collective-permute-done | bytes 98336 | tf_op jit(solution)/shard_map/ppermute | solution.py:162
  14.8 2.2 %collective-permute-start.10 = (bf16[128,384]{1,0:T(8,128)(2,1)S(1)}, bf16[128,384]{1,0:T(8,128)(2,1)S(1)}, u32[]{:S(2)}, u32[]{:S(2)}) collective-permute-start(bf16[128,384]{1,0:T(8,128)(2,1)S(1)} %get-tuple-element.56), channel_id=1, source_target_pairs={{0,8},{1,9},{2,10},{3,11},{4,12},{5,13},{6,14},{7,15},{8,0},{9,1},... | collective-permute-start | bytes 294920 | tf_op jit(solution)/shard_map/ppermute | solution.py:162
  17.0 1.9 %collective-permute-done.3.refs_3_ = bf16[128,384]{1,0:T(8,128)(2,1)S(1)} collective-permute-done((bf16[128,384]{1,0:T(8,128)(2,1)S(1)}, bf16[128,384]{1,0:T(8,128)(2,1)S(1)}, u32[]{:S(2)}, u32[]{:S(2)}) %collective-permute-start.3) | collective-permute-done | bytes 98336 | tf_op jit(solution)/shard_map/ppermute | solution.py:162
  18.9 3.7 %collective-permute-start.2 = (bf16[128,384]{1,0:T(8,128)(2,1)S(1)}, bf16[128,384]{1,0:T(8,128)(2,1)S(1)}, u32[]{:S(2)}, u32[]{:S(2)}) collective-permute-start(bf16[128,384]{1,0:T(8,128)(2,1)S(1)} %get-tuple-element.40), channel_id=1, source_target_pairs={{0,6},{1,7},{2,4},{3,5},{4,2},{5,3},{6,0},{7,1},{8,14},{9,15},{10,... | collective-permute-start | bytes 294920 | tf_op jit(solution)/shard_map/ppermute | solution.py:162
  22.6 0.0 collective-permute-done.9.refs_1_
  22.6 0.4 collective-permute-start.12
  23.0 3.7 %collective-permute-start.14 = (bf16[128,384]{1,0:T(8,128)(2,1)S(1)}, bf16[128,384]{1,0:T(8,128)(2,1)S(1)}, u32[]{:S(2)}, u32[]{:S(2)}) collective-permute-start(bf16[128,384]{1,0:T(8,128)(2,1)S(1)} %get-tuple-element.66), channel_id=1, source_target_pairs={{0,13},{1,12},{2,15},{3,14},{4,9},{5,8},{6,11},{7,10},{8,5},{9,4},... | collective-permute-start | bytes 294920 | tf_op jit(solution)/shard_map/ppermute | solution.py:162
  26.7 0.0 collective-permute-done.10.refs_2_
  26.7 0.3 collective-permute-start.11
  27.0 1.4 %collective-permute-start.13 = (bf16[128,384]{1,0:T(8,128)(2,1)S(1)}, bf16[128,384]{1,0:T(8,128)(2,1)S(1)}, u32[]{:S(2)}, u32[]{:S(2)}) collective-permute-start(bf16[128,384]{1,0:T(8,128)(2,1)S(1)} %get-tuple-element.65), channel_id=1, source_target_pairs={{0,12},{1,13},{2,14},{3,15},{4,8},{5,9},{6,10},{7,11},{8,4},{9,5},... | collective-permute-start | bytes 294920 | tf_op jit(solution)/shard_map/ppermute | solution.py:162
  28.4 1.7 %copy-done.1 = bf16[1536,768]{1,0:T(8,128)(2,1)S(1)} copy-done((bf16[1536,768]{1,0:T(8,128)(2,1)S(1)}, bf16[1536,768]{1,0:T(8,128)(2,1)}, u32[]{:S(2)}) %copy-start.1) | copy-done | bytes 2359320
  30.1 1.7 %copy-done.2 = bf16[768,1536]{1,0:T(8,128)(2,1)S(1)} copy-done((bf16[768,1536]{1,0:T(8,128)(2,1)S(1)}, bf16[768,1536]{1,0:T(8,128)(2,1)}, u32[]{:S(2)}) %copy-start.2) | copy-done | bytes 2359320
  31.7 1.7 %copy-done.4 = bf16[1536,768]{1,0:T(8,128)(2,1)S(1)} copy-done((bf16[1536,768]{1,0:T(8,128)(2,1)S(1)}, bf16[1536,768]{1,0:T(8,128)(2,1)}, u32[]{:S(2)}) %copy-start.4) | copy-done | bytes 2359320
  33.4 4.6 %switch_group.3.refs_12_ = bf16[4,128,384]{2,1,0:T(8,128)(2,1)S(1)} custom-call(bf16[128,384]{1,0:T(8,128)(2,1)S(1)} %get-tuple-element.48.refs_0_, bf16[128,384]{1,0:T(8,128)(2,1)S(1)} %collective-permute-done.9.refs_1_, bf16[128,384]{1,0:T(8,128)(2,1)S(1)} %collective-permute-done.10.refs_2_, bf16[128,384]{1,0:T(8,128)(2,1)S(1)} %collective-permute-done.8.refs_3_, ...), custom_call_target="tpu_custom_call" | custom-call | flops 2415919104 | bytes 9867264 | tf_op jit(solution)/shard_map/switch_group/pallas_call | solution.py:121
  38.0 4.6 %switch_group.4.refs_13_ = bf16[4,128,384]{2,1,0:T(8,128)(2,1)S(1)} custom-call(bf16[128,384]{1,0:T(8,128)(2,1)S(1)} %collective-permute-done.1.refs_0_, bf16[128,384]{1,0:T(8,128)(2,1)S(1)} %collective-permute-done.4.refs_1_, bf16[128,384]{1,0:T(8,128)(2,1)S(1)} %collective-permute-done.refs_2_, bf16[128,384]{1,0:T(8,128)(2,1)S(1)} %collective-permute-done.3.refs_3_, ...), custom_call_target="tpu_custom_call" | custom-call | flops 2415919104 | bytes 9867264 | tf_op jit(solution)/shard_map/switch_group/pallas_call | solution.py:121
  42.5 0.0 collective-permute-done.12.refs_1_
  42.6 2.4 %collective-permute-start.6 = (bf16[128,384]{1,0:T(8,128)(2,1)S(1)}, bf16[128,384]{1,0:T(8,128)(2,1)S(1)}, u32[]{:S(2)}, u32[]{:S(2)}) collective-permute-start(bf16[128,384]{1,0:T(8,128)(2,1)S(1)} %get-tuple-element.46), channel_id=1, source_target_pairs={{0,14},{1,15},{2,12},{3,13},{4,10},{5,11},{6,8},{7,9},{8,6},{9,7},... | collective-permute-start | bytes 294920 | tf_op jit(solution)/shard_map/ppermute | solution.py:162
  45.0 0.0 collective-permute-done.14.refs_3_
  45.0 0.0 collective-permute-start.5
  45.0 2.2 %collective-permute-start.7 = (bf16[128,384]{1,0:T(8,128)(2,1)S(1)}, bf16[128,384]{1,0:T(8,128)(2,1)S(1)}, u32[]{:S(2)}, u32[]{:S(2)}) collective-permute-start(bf16[128,384]{1,0:T(8,128)(2,1)S(1)} %get-tuple-element.47), channel_id=1, source_target_pairs={{0,15},{1,14},{2,13},{3,12},{4,11},{5,10},{6,9},{7,8},{8,7},{9,6},... | collective-permute-start | bytes 294920 | tf_op jit(solution)/shard_map/ppermute | solution.py:162
  47.3 4.8 %switch_group.5.refs_14_ = bf16[4,128,384]{2,1,0:T(8,128)(2,1)S(1)} custom-call(bf16[128,384]{1,0:T(8,128)(2,1)S(1)} %collective-permute-done.11.refs_0_, bf16[128,384]{1,0:T(8,128)(2,1)S(1)} %collective-permute-done.12.refs_1_, bf16[128,384]{1,0:T(8,128)(2,1)S(1)} %collective-permute-done.13.refs_2_, bf16[128,384]{1,0:T(8,128)(2,1)S(1)} %collective-permute-done.14.refs_3_, ...), custom_call_target="tpu_custom_call" | custom-call | flops 2415919104 | bytes 9867264 | tf_op jit(solution)/shard_map/switch_group/pallas_call | solution.py:121
  52.0 1.9 %collective-permute-done.5.refs_1_ = bf16[128,384]{1,0:T(8,128)(2,1)S(1)} collective-permute-done((bf16[128,384]{1,0:T(8,128)(2,1)S(1)}, bf16[128,384]{1,0:T(8,128)(2,1)S(1)}, u32[]{:S(2)}, u32[]{:S(2)}) %collective-permute-start.5) | collective-permute-done | bytes 98336 | tf_op jit(solution)/shard_map/ppermute | solution.py:162
  54.0 6.4 %switch_last.1 = bf16[2,1024,384]{2,1,0:T(8,128)(2,1)} custom-call(bf16[128,384]{1,0:T(8,128)(2,1)S(1)} %collective-permute-done.2.refs_0_, bf16[128,384]{1,0:T(8,128)(2,1)S(1)} %collective-permute-done.5.refs_1_, bf16[128,384]{1,0:T(8,128)(2,1)S(1)} %collective-permute-done.6.refs_2_, bf16[128,384]{1,0:T(8,128)(2,1)S(1)} %collective-permute-done.7.refs_3_, ...), custom_call_target="tpu_custom_call" | custom-call | flops 2415919104 | bytes 11046912 | tf_op jit(solution)/shard_map/switch_last/pallas_call | solution.py:121
  (43 shorter events, 0.2 us)
Async XLA Ops:
  0.0 1.4 %copy-start.5 = (bf16[2,1024,384]{2,1,0:T(8,128)(2,1)S(1)}, bf16[2,1024,384]{2,1,0:T(8,128)(2,1)}, u32[]{:S(2)}) copy-start(bf16[2,1024,384]{2,1,0:T(8,128)(2,1)} %x_ref.1) | copy-start | bytes 4718596
  1.4 10.0 %copy-start.12 = (f32[768]{0:T(1024)S(1)}, f32[768]{0:T(1024)}, u32[]{:S(2)}) copy-start(f32[768]{0:T(1024)} %param.18) | copy-start | bytes 9220
  1.4 10.0 %copy-start.6 = (f32[1536]{0:T(1024)S(1)}, f32[1536]{0:T(1024)}, u32[]{:S(2)}) copy-start(f32[1536]{0:T(1024)} %param.16) | copy-start | bytes 18436
  1.4 10.0 %copy-start.7 = (f32[1536]{0:T(1024)S(1)}, f32[1536]{0:T(1024)}, u32[]{:S(2)}) copy-start(f32[1536]{0:T(1024)} %param.17) | copy-start | bytes 18436
  1.4 10.0 %copy-start.8 = (f32[1536]{0:T(1024)S(1)}, f32[1536]{0:T(1024)}, u32[]{:S(2)}) copy-start(f32[1536]{0:T(1024)} %param.22) | copy-start | bytes 18436
  1.4 10.0 %copy-start.9 = (f32[1536]{0:T(1024)S(1)}, f32[1536]{0:T(1024)}, u32[]{:S(2)}) copy-start(f32[1536]{0:T(1024)} %param.23) | copy-start | bytes 18436
  1.4 10.1 %copy-start.13 = (f32[768]{0:T(1024)S(1)}, f32[768]{0:T(1024)}, u32[]{:S(2)}) copy-start(f32[768]{0:T(1024)} %param.24) | copy-start | bytes 9220
  1.4 10.1 %copy-start.10 = (f32[768]{0:T(1024)S(1)}, f32[768]{0:T(1024)}, u32[]{:S(2)}) copy-start(f32[768]{0:T(1024)} %param.19) | copy-start | bytes 9220
  1.4 10.1 %copy-start.11 = (f32[768]{0:T(1024)S(1)}, f32[768]{0:T(1024)}, u32[]{:S(2)}) copy-start(f32[768]{0:T(1024)} %param.25) | copy-start | bytes 9220
  1.5 26.9 %copy-start = (bf16[768,1536]{1,0:T(8,128)(2,1)S(1)}, bf16[768,1536]{1,0:T(8,128)(2,1)}, u32[]{:S(2)}) copy-start(bf16[768,1536]{1,0:T(8,128)(2,1)} %refs_4_.7) | copy-start | bytes 7077892
  2.2 10.1 %collective-permute-start = (bf16[128,384]{1,0:T(8,128)(2,1)S(1)}, bf16[128,384]{1,0:T(8,128)(2,1)S(1)}, u32[]{:S(2)}, u32[]{:S(2)}) collective-permute-start(bf16[128,384]{1,0:T(8,128)(2,1)S(1)} %get-tuple-element.38), channel_id=1, source_target_pairs={{0,10},{1,11},{2,8},{3,9},{4,14},{5,15},{6,12},{7,13},{8,2},{9,3},... | collective-permute-start | bytes 294920 | tf_op jit(solution)/shard_map/ppermute | solution.py:162
  7.2 7.5 %collective-permute-start.1 = (bf16[128,384]{1,0:T(8,128)(2,1)S(1)}, bf16[128,384]{1,0:T(8,128)(2,1)S(1)}, u32[]{:S(2)}, u32[]{:S(2)}) collective-permute-start(bf16[128,384]{1,0:T(8,128)(2,1)S(1)} %get-tuple-element.39), channel_id=1, source_target_pairs={{0,2},{1,3},{2,0},{3,1},{4,6},{5,7},{6,4},{7,5},{8,10},{9,11},{10,... | collective-permute-start | bytes 294920 | tf_op jit(solution)/shard_map/ppermute | solution.py:162
  7.8 11.2 %collective-permute-start.3 = (bf16[128,384]{1,0:T(8,128)(2,1)S(1)}, bf16[128,384]{1,0:T(8,128)(2,1)S(1)}, u32[]{:S(2)}, u32[]{:S(2)}) collective-permute-start(bf16[128,384]{1,0:T(8,128)(2,1)S(1)} %get-tuple-element.43), channel_id=1, source_target_pairs={{0,11},{1,10},{2,9},{3,8},{4,15},{5,14},{6,13},{7,12},{8,3},{9,2},... | collective-permute-start | bytes 294920 | tf_op jit(solution)/shard_map/ppermute | solution.py:162
  7.9 14.7 %collective-permute-start.4 = (bf16[128,384]{1,0:T(8,128)(2,1)S(1)}, bf16[128,384]{1,0:T(8,128)(2,1)S(1)}, u32[]{:S(2)}, u32[]{:S(2)}) collective-permute-start(bf16[128,384]{1,0:T(8,128)(2,1)S(1)} %get-tuple-element.44), channel_id=1, source_target_pairs={{0,3},{1,2},{2,1},{3,0},{4,7},{5,6},{6,5},{7,4},{8,11},{9,10},{10,... | collective-permute-start | bytes 294920 | tf_op jit(solution)/shard_map/ppermute | solution.py:162
  9.1 13.5 %collective-permute-start.8 = (bf16[128,384]{1,0:T(8,128)(2,1)S(1)}, bf16[128,384]{1,0:T(8,128)(2,1)S(1)}, u32[]{:S(2)}, u32[]{:S(2)}) collective-permute-start(bf16[128,384]{1,0:T(8,128)(2,1)S(1)} %get-tuple-element.51), channel_id=1, source_target_pairs={{0,9},{1,8},{2,11},{3,10},{4,13},{5,12},{6,15},{7,14},{8,1},{9,0},... | collective-permute-start | bytes 294920 | tf_op jit(solution)/shard_map/ppermute | solution.py:162
  12.2 10.4 %collective-permute-start.9 = (bf16[128,384]{1,0:T(8,128)(2,1)S(1)}, bf16[128,384]{1,0:T(8,128)(2,1)S(1)}, u32[]{:S(2)}, u32[]{:S(2)}) collective-permute-start(bf16[128,384]{1,0:T(8,128)(2,1)S(1)} %get-tuple-element.52), channel_id=1, source_target_pairs={{0,1},{1,0},{2,3},{3,2},{4,5},{5,4},{6,7},{7,6},{8,9},{9,8},{10,11... | collective-permute-start | bytes 294920 | tf_op jit(solution)/shard_map/ppermute | solution.py:162
  14.8 12.0 %collective-permute-start.10 = (bf16[128,384]{1,0:T(8,128)(2,1)S(1)}, bf16[128,384]{1,0:T(8,128)(2,1)S(1)}, u32[]{:S(2)}, u32[]{:S(2)}) collective-permute-start(bf16[128,384]{1,0:T(8,128)(2,1)S(1)} %get-tuple-element.56), channel_id=1, source_target_pairs={{0,8},{1,9},{2,10},{3,11},{4,12},{5,13},{6,14},{7,15},{8,0},{9,1},... | collective-permute-start | bytes 294920 | tf_op jit(solution)/shard_map/ppermute | solution.py:162
  18.9 33.1 %collective-permute-start.2 = (bf16[128,384]{1,0:T(8,128)(2,1)S(1)}, bf16[128,384]{1,0:T(8,128)(2,1)S(1)}, u32[]{:S(2)}, u32[]{:S(2)}) collective-permute-start(bf16[128,384]{1,0:T(8,128)(2,1)S(1)} %get-tuple-element.40), channel_id=1, source_target_pairs={{0,6},{1,7},{2,4},{3,5},{4,2},{5,3},{6,0},{7,1},{8,14},{9,15},{10,... | collective-permute-start | bytes 294920 | tf_op jit(solution)/shard_map/ppermute | solution.py:162
  22.6 19.9 %collective-permute-start.12 = (bf16[128,384]{1,0:T(8,128)(2,1)S(1)}, bf16[128,384]{1,0:T(8,128)(2,1)S(1)}, u32[]{:S(2)}, u32[]{:S(2)}) collective-permute-start(bf16[128,384]{1,0:T(8,128)(2,1)S(1)} %get-tuple-element.64), channel_id=1, source_target_pairs={{0,5},{1,4},{2,7},{3,6},{4,1},{5,0},{6,3},{7,2},{8,13},{9,12},{10,... | collective-permute-start | bytes 294920 | tf_op jit(solution)/shard_map/ppermute | solution.py:162
  23.0 22.0 %collective-permute-start.14 = (bf16[128,384]{1,0:T(8,128)(2,1)S(1)}, bf16[128,384]{1,0:T(8,128)(2,1)S(1)}, u32[]{:S(2)}, u32[]{:S(2)}) collective-permute-start(bf16[128,384]{1,0:T(8,128)(2,1)S(1)} %get-tuple-element.66), channel_id=1, source_target_pairs={{0,13},{1,12},{2,15},{3,14},{4,9},{5,8},{6,11},{7,10},{8,5},{9,4},... | collective-permute-start | bytes 294920 | tf_op jit(solution)/shard_map/ppermute | solution.py:162
  26.7 18.3 %collective-permute-start.11 = (bf16[128,384]{1,0:T(8,128)(2,1)S(1)}, bf16[128,384]{1,0:T(8,128)(2,1)S(1)}, u32[]{:S(2)}, u32[]{:S(2)}) collective-permute-start(bf16[128,384]{1,0:T(8,128)(2,1)S(1)} %get-tuple-element.63), channel_id=1, source_target_pairs={{0,4},{1,5},{2,6},{3,7},{4,0},{5,1},{6,2},{7,3},{8,12},{9,13},{10,... | collective-permute-start | bytes 294920 | tf_op jit(solution)/shard_map/ppermute | solution.py:162
  27.0 20.2 %collective-permute-start.13 = (bf16[128,384]{1,0:T(8,128)(2,1)S(1)}, bf16[128,384]{1,0:T(8,128)(2,1)S(1)}, u32[]{:S(2)}, u32[]{:S(2)}) collective-permute-start(bf16[128,384]{1,0:T(8,128)(2,1)S(1)} %get-tuple-element.65), channel_id=1, source_target_pairs={{0,12},{1,13},{2,14},{3,15},{4,8},{5,9},{6,10},{7,11},{8,4},{9,5},... | collective-permute-start | bytes 294920 | tf_op jit(solution)/shard_map/ppermute | solution.py:162
  28.4 1.7 %copy-start.1 = (bf16[1536,768]{1,0:T(8,128)(2,1)S(1)}, bf16[1536,768]{1,0:T(8,128)(2,1)}, u32[]{:S(2)}) copy-start(bf16[1536,768]{1,0:T(8,128)(2,1)} %refs_5_.7) | copy-start | bytes 7077892
  30.1 1.7 %copy-start.2 = (bf16[768,1536]{1,0:T(8,128)(2,1)S(1)}, bf16[768,1536]{1,0:T(8,128)(2,1)}, u32[]{:S(2)}) copy-start(bf16[768,1536]{1,0:T(8,128)(2,1)} %refs_8_.7) | copy-start | bytes 7077892
  31.7 1.7 %copy-start.4 = (bf16[1536,768]{1,0:T(8,128)(2,1)S(1)}, bf16[1536,768]{1,0:T(8,128)(2,1)}, u32[]{:S(2)}) copy-start(bf16[1536,768]{1,0:T(8,128)(2,1)} %refs_9_.7) | copy-start | bytes 7077892
  33.4 4.6 %copy-start.3 = (bf16[768,1536]{1,0:T(8,128)(2,1)S(1)}, bf16[768,1536]{1,0:T(8,128)(2,1)}, u32[]{:S(2)}) copy-start(bf16[768,1536]{1,0:T(8,128)(2,1)} %refs_8_.7) | copy-start | bytes 7077892
  42.6 9.5 %collective-permute-start.6 = (bf16[128,384]{1,0:T(8,128)(2,1)S(1)}, bf16[128,384]{1,0:T(8,128)(2,1)S(1)}, u32[]{:S(2)}, u32[]{:S(2)}) collective-permute-start(bf16[128,384]{1,0:T(8,128)(2,1)S(1)} %get-tuple-element.46), channel_id=1, source_target_pairs={{0,14},{1,15},{2,12},{3,13},{4,10},{5,11},{6,8},{7,9},{8,6},{9,7},... | collective-permute-start | bytes 294920 | tf_op jit(solution)/shard_map/ppermute | solution.py:162
  45.0 9.0 %collective-permute-start.5 = (bf16[128,384]{1,0:T(8,128)(2,1)S(1)}, bf16[128,384]{1,0:T(8,128)(2,1)S(1)}, u32[]{:S(2)}, u32[]{:S(2)}) collective-permute-start(bf16[128,384]{1,0:T(8,128)(2,1)S(1)} %get-tuple-element.45), channel_id=1, source_target_pairs={{0,7},{1,6},{2,5},{3,4},{4,3},{5,2},{6,1},{7,0},{8,15},{9,14},{10,... | collective-permute-start | bytes 294920 | tf_op jit(solution)/shard_map/ppermute | solution.py:162
  45.0 9.0 %collective-permute-start.7 = (bf16[128,384]{1,0:T(8,128)(2,1)S(1)}, bf16[128,384]{1,0:T(8,128)(2,1)S(1)}, u32[]{:S(2)}, u32[]{:S(2)}) collective-permute-start(bf16[128,384]{1,0:T(8,128)(2,1)S(1)} %get-tuple-element.47), channel_id=1, source_target_pairs={{0,15},{1,14},{2,13},{3,12},{4,11},{5,10},{6,9},{7,8},{8,7},{9,6},... | collective-permute-start | bytes 294920 | tf_op jit(solution)/shard_map/ppermute | solution.py:162

commit v3 on v2

v3 whole, which is shorter than its diff:
```python
import functools

import jax
import jax.numpy as jnp
from jax import lax
from jax.experimental import pallas as pl
from jax.experimental.pallas import tpu as pltpu
from jax.sharding import PartitionSpec as P

REACH = 8
WEIGH = (0, 0, 1)
MIB = 1 << 20


def gelu(n):
    root = 0.7978845608028654
    half = 0.5 * n
    return half + half * jnp.tanh(n * (root + (root * 0.044715) * (n * n)))


def switch_rows(s, expand, contract, gain, shift, keep, bias):
    hidden = jnp.dot(s, expand, preferred_element_type=jnp.float32)
    center = hidden - jnp.mean(hidden, axis=-1, keepdims=True)
    spread = jnp.mean(center * center, axis=-1, keepdims=True)
    normed = center * lax.rsqrt(spread + 1e-05) * gain[None] + shift[None]
    active = gelu(normed).astype(jnp.bfloat16)
    result = (
        jax.nn.sigmoid(keep[None]) * s.astype(jnp.float32)
        + jnp.dot(active, contract, preferred_element_type=jnp.float32)
        + bias[None]
    )
    return result.astype(jnp.bfloat16)


def iota2(shape, dim):
    return lax.broadcasted_iota(jnp.int32, shape, dim)


def one_hot(hit):
    return jnp.where(hit, 1.0, 0.0).astype(jnp.bfloat16)


def sort_kernel(shards, x_ref, straight, mate, ahead, first, second):
    me = lax.axis_index("seq")
    tile = shards * shards
    streams, rows, _ = x_ref.shape
    row, col = iota2((tile, tile), 0), iota2((tile, tile), 1)
    pick = one_hot((col // shards == row % shards) & (col % shards == ((row // shards) ^ me)))
    for s in range(streams):
        for t in range(rows // tile):
            y = jnp.dot(pick, x_ref[s, t * tile : (t + 1) * tile], preferred_element_type=jnp.float32)
            y = y.astype(jnp.bfloat16)
            at = s * (rows // shards) + t * shards
            for mask in range(shards):
                part = y[mask * shards : (mask + 1) * shards]
                if mask == 0:
                    straight[at : at + shards] = part
                elif mask == REACH:
                    first[at : at + shards] = part
                elif mask == REACH + 1:
                    second[at : at + shards] = part
                elif mask % 2:
                    mate[mask_slot(mask), at : at + shards] = part
                else:
                    ahead[mask_slot(mask) - 1, at : at + shards] = part


def mask_slot(mask):
    chip = mask // 2
    return chip if chip < REACH // 2 else chip - 1


def sort_rows(features, shards):
    streams, rows, width = features.shape
    count = streams * rows // shards
    block = jax.ShapeDtypeStruct((count, width), features.dtype)
    mate = jax.ShapeDtypeStruct((REACH - 1, count, width), features.dtype)
    ahead = jax.ShapeDtypeStruct((REACH - 2, count, width), features.dtype)
    return pl.pallas_call(
        functools.partial(sort_kernel, shards),
        out_shape=[block, mate, ahead, block, block],
        in_specs=[pl.BlockSpec(memory_space=pltpu.VMEM)],
        out_specs=[pl.BlockSpec(memory_space=pltpu.VMEM)] * 5,
        compiler_params=pltpu.CompilerParams(vmem_limit_bytes=16 * MIB),
        cost_estimate=pl.CostEstimate(flops=3 * 10**10, bytes_accessed=2 * features.size * 2, transcendentals=0),
        name="sort_rows",
    )(features)


def join_kernel(straight, mate, ahead, *outs):
    count = straight.shape[0]
    for i, out in enumerate(outs):
        out[:count] = straight[...] if i == 0 else ahead[i - 1]
        out[count:] = mate[i]


def join_rows(straight, mate, ahead):
    count, width = straight.shape
    pair = jax.ShapeDtypeStruct((2 * count, width), straight.dtype)
    return pl.pallas_call(
        join_kernel,
        out_shape=[pair] * (REACH - 1),
        in_specs=[pl.BlockSpec(memory_space=pltpu.VMEM)] * 3,
        out_specs=[pl.BlockSpec(memory_space=pltpu.VMEM)] * (REACH - 1),
        compiler_params=pltpu.CompilerParams(vmem_limit_bytes=16 * MIB),
        cost_estimate=pl.CostEstimate(flops=0, bytes_accessed=4 * mate.size * 2, transcendentals=0),
        name="join_rows",
    )(straight, mate, ahead)


def group_blocks(refs, roles, first, second):
    me = lax.axis_index("seq")
    core, upper = me & 1, (me // REACH) & 1
    count = roles.shape[1]
    parts = [(ref, at) for ref in refs for at in range(0, ref.shape[0], count)]
    for i, (ref, at) in enumerate(parts):
        roles[(upper ^ (i // 2)) * 2 + (core ^ (i % 2))] = ref[at : at + count]
    first = [ref[...] for ref in first]
    second = [ref[...] for ref in second]
    width = roles.shape[-1]
    mids = [
        switch_rows(jnp.concatenate([roles[c], roles[2 + c]], axis=-1), *first) for c in range(2)
    ]
    ends = []
    for half in range(2):
        part = slice(half * width, (half + 1) * width)
        o = switch_rows(jnp.concatenate([mids[0][:, part], mids[1][:, part]], axis=-1), *second)
        ends += [o[:, :width], o[:, width:]]
    return ends


def group_kernel(blocks, *refs):
    first, second, out, roles = refs[blocks : blocks + 6], refs[blocks + 6 : blocks + 12], refs[-2], refs[-1]
    for i, end in enumerate(group_blocks(refs[:blocks], roles, first, second)):
        out[i] = end


def last_kernel(blocks, shards, *refs):
    first, second = refs[blocks : blocks + 6], refs[blocks + 6 : blocks + 12]
    done, out, roles = refs[blocks + 12 : -2], refs[-2], refs[-1]
    ends = group_blocks(refs[:blocks], roles, first, second)
    me = lax.axis_index("seq")
    near = (me & (REACH - 1)) >> 1
    tile = shards * shards
    row, col = iota2((tile, tile), 0), iota2((tile, tile), 1)
    group, half, core = col // (4 * shards), (col // (2 * shards)) % 2, (col // shards) % 2
    source = half * REACH + ((group ^ near) * 2 + core)
    place = one_hot((row // shards == col % shards) & (row % shards == source))
    streams, rows, _ = out.shape
    for s in range(streams):
        for t in range(rows // tile):
            at = s * (rows // shards) + t * shards
            parts = [d[i, at : at + shards] for d in done for i in range(4)]
            parts += [end[at : at + shards] for end in ends]
            y = jnp.dot(place, jnp.concatenate(parts, axis=0), preferred_element_type=jnp.float32)
            out[s, t * tile : (t + 1) * tile] = y.astype(jnp.bfloat16)


def run_group(kernel, blocks, count, params, extra, out_shape, name, weigh=1):
    width = blocks[0].shape[-1]
    args = (*blocks, *params, *extra)
    hidden = params[0].shape[1]
    return pl.pallas_call(
        functools.partial(kernel, len(blocks)),
        out_shape=out_shape,
        in_specs=[pl.BlockSpec(memory_space=pltpu.VMEM)] * len(args),
        out_specs=pl.BlockSpec(memory_space=pltpu.VMEM),
        scratch_shapes=[pltpu.VMEM((4, count, width), jnp.bfloat16)],
        compiler_params=pltpu.CompilerParams(vmem_limit_bytes=32 * MIB),
        cost_estimate=pl.CostEstimate(
            flops=weigh * 2 * 2 * count * 4 * 2 * width * hidden,
            bytes_accessed=weigh * sum(a.size * a.dtype.itemsize for a in args),
            transcendentals=weigh * 4 * count * hidden,
        ),
        name=name,
    )(*args)


def after(values, *before):
    held = lax.optimization_barrier((*values, *before))
    return held[: len(values)]


def exchanged(features, params, shards):
    def send(value, mask):
        return lax.ppermute(value, "seq", [(d, d ^ mask) for d in range(shards)])

    straight, mate, ahead, far0, far1 = sort_rows(features, shards)
    count = straight.shape[0]
    groups = REACH // 2
    far0, far1 = send(far0, REACH), send(far1, REACH + 1)
    joined = join_rows(straight, send(mate, 1), ahead)
    near = list(joined[:groups])
    far = [None, *joined[groups:]]
    block = jax.ShapeDtypeStruct((4, count, features.shape[-1]), features.dtype)

    def group(index):
        near_rows, far_rows = arrived[index]
        return run_group(
            group_kernel, (near_rows, *far_rows), count, params, (), block, "switch_group", WEIGH[index]
        )

    ends = []
    arrived = [(near[0], (far0, far1))]
    arrived.append((send(near[1], 2), (send(far[1], REACH + 2),)))
    for g in range(2, groups):
        past_near, past_far = arrived[g - 2]
        near_next, far_next, past_near, *past_far = after((near[g], far[g], past_near, *past_far), *ends[:g - 1])
        arrived[g - 2] = (past_near, tuple(past_far))
        arrived.append((send(near_next, 2 * g), (send(far_next, REACH + 2 * g),)))
        ends.append(group(g - 2))
    ends.append(group(groups - 2))
    near_rows, far_rows = arrived[groups - 1]
    whole = jax.ShapeDtypeStruct(features.shape, features.dtype)

    def kernel(blocks, *refs):
        last_kernel(blocks, shards, *refs)

    return run_group(kernel, (near_rows, *far_rows), count, params, tuple(ends), whole, "switch_last")


def gathered(features, first, second):
    streams, rows_here, width = features.shape
    devices = lax.axis_size("seq")
    slots = rows_here // devices
    outgoing = features.reshape(streams, slots, devices, width).transpose(2, 0, 1, 3)
    outgoing = outgoing.reshape(devices, streams * slots, width)
    received = lax.all_to_all(outgoing, "seq", split_axis=0, concat_axis=0, tiled=True)
    clusters = devices // (2 * REACH)
    halves = received.reshape(clusters, 2, REACH, streams * slots, width)
    pairs = jnp.concatenate([halves[:, 0], halves[:, 1]], axis=-1).reshape(-1, 2 * width)
    mid = switch_rows(pairs, *first)
    mid = mid.reshape(clusters, REACH // 2, 2, streams * slots, 2, width)
    pairs = mid.transpose(0, 4, 1, 3, 2, 5).reshape(-1, 2 * width)
    result = switch_rows(pairs, *second)
    result = result.reshape(devices // 2, streams, slots, 2, width)
    return result.transpose(1, 2, 0, 3, 4).reshape(streams, rows_here, width)


def per_device(features, *params):
    first, second = params[:6], params[6:]
    shards = lax.axis_size("seq")
    if shards == 2 * REACH and features.shape[1] % (shards * shards) == 0:
        return exchanged(features, params, shards)
    return gathered(features, first, second)


def solution(mesh):
    return jax.shard_map(
        per_device,
        mesh=mesh,
        in_specs=(P("groups", "seq", None),) + (P(),) * 12,
        out_specs=P("groups", "seq", None),
        check_vma=False,
    )
```

time: 60.6 us -> 50.7 us (0.84)
  starting transfers between devices: 25.6 us -> 15.2 us
  waiting for transfers between devices: 7.01 us -> 12.7 us
  local copies, waits for them, and re-layouts: 6.48 us -> 1.53 us
    ppermute x15 -> x9, starting transfers between devices: 25.6 us -> 15.2 us  [send(): return lax.ppermute(value, 'seq', [(d, d ^ mask) for d in range(shards)])]
    ppermute x15 -> x9, waiting for transfers between devices: 7.01 us -> 12.7 us  [send(): return lax.ppermute(value, 'seq', [(d, d ^ mask) for d in range(shards)])]
    unnamed x28 -> x26, local copies, waits for them, and re-layouts: 6.44 us -> 1.53 us
    pallas_call x5 -> x6, Pallas kernels: 21 us -> 20.9 us  [the longest x4 20.1 us: run_group(): pl.pallas_call(functools.partial(kernel, len(blocks)), out_shape=out_shap...]
  transfers between devices with their start and end apart: 15 -> 9, of which waited for: 4 -> 3; matrix products, arithmetic and copies ran while one was open for 0% -> 0% of each run, Pallas kernels for 23% -> 27%
where the time goes in v3:
time: 50.7 us; the launch traced here: 50.6 us
  Pallas kernels  20.9 us (41%)
  starting transfers between devices  15.2 us (30%)
  waiting for transfers between devices  12.7 us (25%)
  local copies, waits for them, and re-layouts  1.53 us (3%)
    pallas_call x4, Pallas kernels, run_group(): pl.pallas_call(functools.partial(kernel, len(blocks)), out_shape=out_shap...  20.1 us
    ppermute x9, starting transfers between devices, send(): return lax.ppermute(value, 'seq', [(d, d ^ mask) for d in range(shards)])  15.2 us
    ppermute x9, waiting for transfers between devices, send(): return lax.ppermute(value, 'seq', [(d, d ^ mask) for d in range(shards)])  12.7 us
    unnamed x26, local copies, waits for them, and re-layouts  1.53 us
  transfers between devices with their start and end apart: 9, of which 3 were waited for; matrix products, arithmetic and copies ran while one was open for 0% of the time, Pallas kernels for 27%

profile of v3, /device:TPU:0, one launch (start us, length us, event | category | flops | bytes accessed | tf_op | source)
XLA Modules:
  0.0 50.6 jit_solution(2198304629803773517)
XLA Ops:
  0.0 0.0 copy-start.8
  0.0 0.0 copy-start.5
  0.0 0.0 copy-start.4
  0.0 0.0 copy-start.12
  0.1 1.5 %copy-done.12 = bf16[2,1024,384]{2,1,0:T(8,128)(2,1)S(1)} copy-done((bf16[2,1024,384]{2,1,0:T(8,128)(2,1)S(1)}, bf16[2,1024,384]{2,1,0:T(8,128)(2,1)}, u32[]{:S(2)}) %copy-start.12) | copy-done | bytes 1572888
  1.5 0.7 %sort_rows.1 = (bf16[128,384]{1,0:T(8,128)(2,1)S(1)}, bf16[7,128,384]{2,1,0:T(8,128)(2,1)S(1)}, bf16[6,128,384]{2,1,0:T(8,128)(2,1)S(1)}, bf16[128,384]{1,0:T(8,128)(2,1)S(1)}, bf16[128,384]{1,0:T(8,128)(2,1)S(1)}) custom-call(bf16[2,1024,384]{2,1,0:T(8,128)(2,1)S(1)} %copy-done.12), custom_call_target="tpu_custom_call" | custom-call | flops 30000001024 | bytes 3145728 | tf_op jit(solution)/shard_map/sort_rows/pallas_call | solution.py:79
  2.3 0.5 %collective-permute-start = (bf16[7,128,384]{2,1,0:T(8,128)(2,1)S(1)}, bf16[7,128,384]{2,1,0:T(8,128)(2,1)S(1)}, u32[]{:S(2)}, u32[]{:S(2)}) collective-permute-start(bf16[7,128,384]{2,1,0:T(8,128)(2,1)S(1)} %get-tuple-element.27), channel_id=1, source_target_pairs={{0,1},{1,0},{2,3},{3,2},{4,5},{5,4},{6,7},{7,6},{8,9},{9,8},{10,11... | collective-permute-start | bytes 2064392 | tf_op jit(solution)/shard_map/ppermute | solution.py:186
  2.8 3.7 %collective-permute-start.3 = (bf16[128,384]{1,0:T(8,128)(2,1)S(1)}, bf16[128,384]{1,0:T(8,128)(2,1)S(1)}, u32[]{:S(2)}, u32[]{:S(2)}) collective-permute-start(bf16[128,384]{1,0:T(8,128)(2,1)S(1)} %get-tuple-element.36), channel_id=1, source_target_pairs={{0,8},{1,9},{2,10},{3,11},{4,12},{5,13},{6,14},{7,15},{8,0},{9,1},... | collective-permute-start | bytes 294920 | tf_op jit(solution)/shard_map/ppermute | solution.py:186
  6.4 0.1 collective-permute-start.4
  6.5 0.0 collective-permute-done.mate
  6.5 0.1 join_rows.1
  6.6 1.6 %collective-permute-start.1 = (bf16[256,384]{1,0:T(8,128)(2,1)S(1)}, bf16[256,384]{1,0:T(8,128)(2,1)S(1)}, u32[]{:S(2)}, u32[]{:S(2)}) collective-permute-start(bf16[256,384]{1,0:T(8,128)(2,1)S(1)} %get-tuple-element.31), channel_id=1, source_target_pairs={{0,2},{1,3},{2,0},{3,1},{4,6},{5,7},{6,4},{7,5},{8,10},{9,11},{10,... | collective-permute-start | bytes 589832 | tf_op jit(solution)/shard_map/ppermute | solution.py:186
  8.3 2.5 %collective-permute-start.2 = (bf16[256,384]{1,0:T(8,128)(2,1)S(1)}, bf16[256,384]{1,0:T(8,128)(2,1)S(1)}, u32[]{:S(2)}, u32[]{:S(2)}) collective-permute-start(bf16[256,384]{1,0:T(8,128)(2,1)S(1)} %get-tuple-element.32), channel_id=1, source_target_pairs={{0,10},{1,11},{2,8},{3,9},{4,14},{5,15},{6,12},{7,13},{8,2},{9,3},... | collective-permute-start | bytes 589832 | tf_op jit(solution)/shard_map/ppermute | solution.py:186
  10.8 7.7 %collective-permute-done.3.refs_1_ = bf16[128,384]{1,0:T(8,128)(2,1)S(1)} collective-permute-done((bf16[128,384]{1,0:T(8,128)(2,1)S(1)}, bf16[128,384]{1,0:T(8,128)(2,1)S(1)}, u32[]{:S(2)}, u32[]{:S(2)}) %collective-permute-start.3) | collective-permute-done | bytes 98336 | tf_op jit(solution)/shard_map/ppermute | solution.py:186
  18.5 1.6 %collective-permute-done.4.refs_2_ = bf16[128,384]{1,0:T(8,128)(2,1)S(1)} collective-permute-done((bf16[128,384]{1,0:T(8,128)(2,1)S(1)}, bf16[128,384]{1,0:T(8,128)(2,1)S(1)}, u32[]{:S(2)}, u32[]{:S(2)}) %collective-permute-start.4) | collective-permute-done | bytes 98336 | tf_op jit(solution)/shard_map/ppermute | solution.py:186
  20.1 1.0 %collective-permute-start.7 = (bf16[256,384]{1,0:T(8,128)(2,1)S(1)}, bf16[256,384]{1,0:T(8,128)(2,1)S(1)}, u32[]{:S(2)}, u32[]{:S(2)}) collective-permute-start(bf16[256,384]{1,0:T(8,128)(2,1)S(1)} %get-tuple-element.45), channel_id=1, source_target_pairs={{0,4},{1,5},{2,6},{3,7},{4,0},{5,1},{6,2},{7,3},{8,12},{9,13},{10,... | collective-permute-start | bytes 589832 | tf_op jit(solution)/shard_map/ppermute | solution.py:186
  21.1 2.7 %collective-permute-start.8 = (bf16[256,384]{1,0:T(8,128)(2,1)S(1)}, bf16[256,384]{1,0:T(8,128)(2,1)S(1)}, u32[]{:S(2)}, u32[]{:S(2)}) collective-permute-start(bf16[256,384]{1,0:T(8,128)(2,1)S(1)} %get-tuple-element.46), channel_id=1, source_target_pairs={{0,12},{1,13},{2,14},{3,15},{4,8},{5,9},{6,10},{7,11},{8,4},{9,5},... | collective-permute-start | bytes 589832 | tf_op jit(solution)/shard_map/ppermute | solution.py:186
  23.9 0.0 copy-done.11
  23.9 0.0 copy-done.10
  23.9 0.0 copy-done.7
  24.0 4.5 %switch_group.3.refs_14_ = bf16[4,128,384]{2,1,0:T(8,128)(2,1)S(1)} custom-call(bf16[256,384]{1,0:T(8,128)(2,1)S(1)} %get-tuple-element.38.refs_0_, bf16[128,384]{1,0:T(8,128)(2,1)S(1)} %collective-permute-done.3.refs_1_, bf16[128,384]{1,0:T(8,128)(2,1)S(1)} %collective-permute-done.4.refs_2_, bf16[768,1536]{1,0:T(8,128)(2,1)S(1)} %copy-done, ...), custom_call_target="tpu_custom_call" | custom-call | tf_op jit(solution)/shard_map/switch_group/pallas_call | solution.py:163
  28.5 0.0 collective-permute-done.1.refs_0_
  28.5 0.0 collective-permute-done.2.refs_1_
  28.5 2.1 %collective-permute-start.5 = (bf16[256,384]{1,0:T(8,128)(2,1)S(1)}, bf16[256,384]{1,0:T(8,128)(2,1)S(1)}, u32[]{:S(2)}, u32[]{:S(2)}) collective-permute-start(bf16[256,384]{1,0:T(8,128)(2,1)S(1)} %get-tuple-element.41), channel_id=1, source_target_pairs={{0,6},{1,7},{2,4},{3,5},{4,2},{5,3},{6,0},{7,1},{8,14},{9,15},{10,... | collective-permute-start | bytes 589832 | tf_op jit(solution)/shard_map/ppermute | solution.py:186
  30.7 0.9 %collective-permute-start.6 = (bf16[256,384]{1,0:T(8,128)(2,1)S(1)}, bf16[256,384]{1,0:T(8,128)(2,1)S(1)}, u32[]{:S(2)}, u32[]{:S(2)}) collective-permute-start(bf16[256,384]{1,0:T(8,128)(2,1)S(1)} %get-tuple-element.42), channel_id=1, source_target_pairs={{0,14},{1,15},{2,12},{3,13},{4,10},{5,11},{6,8},{7,9},{8,6},{9,7},... | collective-permute-start | bytes 589832 | tf_op jit(solution)/shard_map/ppermute | solution.py:186
  31.5 4.5 %switch_group.4.refs_15_ = bf16[4,128,384]{2,1,0:T(8,128)(2,1)S(1)} custom-call(bf16[256,384]{1,0:T(8,128)(2,1)S(1)} %collective-permute-done.1.refs_0_, bf16[256,384]{1,0:T(8,128)(2,1)S(1)} %collective-permute-done.2.refs_1_, bf16[768,1536]{1,0:T(8,128)(2,1)S(1)} %copy-done, bf16[1536,768]{1,0:T(8,128)(2,1)S(1)} %copy-done.1, f32[1536]{0:T(1024)S(1)} %copy-done.4, ...), custom_call_target="tpu_custom_call" | custom-call | tf_op jit(solution)/shard_map/switch_group/pallas_call | solution.py:163
  36.1 0.0 collective-permute-done.7.refs_0_
  36.1 0.0 collective-permute-done.8.refs_1_
  36.1 4.7 %switch_group.5.refs_16_ = bf16[4,128,384]{2,1,0:T(8,128)(2,1)S(1)} custom-call(bf16[256,384]{1,0:T(8,128)(2,1)S(1)} %collective-permute-done.7.refs_0_, bf16[256,384]{1,0:T(8,128)(2,1)S(1)} %collective-permute-done.8.refs_1_, bf16[768,1536]{1,0:T(8,128)(2,1)S(1)} %copy-done, bf16[1536,768]{1,0:T(8,128)(2,1)S(1)} %copy-done.1, f32[1536]{0:T(1024)S(1)} %copy-done.4, ...), custom_call_target="tpu_custom_call" | custom-call | flops 2415919104 | bytes 9867264 | tf_op jit(solution)/shard_map/switch_group/pallas_call | solution.py:163
  40.8 0.0 collective-permute-done.5.refs_0_
  40.8 3.4 %collective-permute-done.6.refs_1_ = bf16[256,384]{1,0:T(8,128)(2,1)S(1)} collective-permute-done((bf16[256,384]{1,0:T(8,128)(2,1)S(1)}, bf16[256,384]{1,0:T(8,128)(2,1)S(1)}, u32[]{:S(2)}, u32[]{:S(2)}) %collective-permute-start.6) | collective-permute-done | bytes 196640 | tf_op jit(solution)/shard_map/ppermute | solution.py:186
  44.2 6.4 %switch_last.1 = bf16[2,1024,384]{2,1,0:T(8,128)(2,1)} custom-call(bf16[256,384]{1,0:T(8,128)(2,1)S(1)} %collective-permute-done.5.refs_0_, bf16[256,384]{1,0:T(8,128)(2,1)S(1)} %collective-permute-done.6.refs_1_, bf16[768,1536]{1,0:T(8,128)(2,1)S(1)} %copy-done, bf16[1536,768]{1,0:T(8,128)(2,1)S(1)} %copy-done.1, f32[1536]{0:T(1024)S(1)} %copy-done.4, ...), custom_call_target="tpu_custom_call" | custom-call | flops 2415919104 | bytes 11046912 | tf_op jit(solution)/shard_map/switch_last/pallas_call | solution.py:163
  (18 shorter events, 0.0 us)
Async XLA Ops:
  0.0 23.9 %copy-start.11 = (f32[768]{0:T(1024)S(1)}, f32[768]{0:T(1024)}, u32[]{:S(2)}) copy-start(f32[768]{0:T(1024)} %refs_13_.7) | copy-start | bytes 9220
  0.0 23.9 %copy-start.10 = (f32[768]{0:T(1024)S(1)}, f32[768]{0:T(1024)}, u32[]{:S(2)}) copy-start(f32[768]{0:T(1024)} %refs_12_.7) | copy-start | bytes 9220
  0.0 23.9 %copy-start.7 = (f32[1536]{0:T(1024)S(1)}, f32[1536]{0:T(1024)}, u32[]{:S(2)}) copy-start(f32[1536]{0:T(1024)} %refs_11_.7) | copy-start | bytes 18436
  0.0 23.9 %copy-start.6 = (f32[1536]{0:T(1024)S(1)}, f32[1536]{0:T(1024)}, u32[]{:S(2)}) copy-start(f32[1536]{0:T(1024)} %refs_10_.7) | copy-start | bytes 18436
  0.0 23.9 %copy-start.9 = (f32[768]{0:T(1024)S(1)}, f32[768]{0:T(1024)}, u32[]{:S(2)}) copy-start(f32[768]{0:T(1024)} %refs_7_.7) | copy-start | bytes 9220
  0.0 23.9 %copy-start.8 = (f32[768]{0:T(1024)S(1)}, f32[768]{0:T(1024)}, u32[]{:S(2)}) copy-start(f32[768]{0:T(1024)} %refs_6_.7) | copy-start | bytes 9220
  0.0 23.9 %copy-start.5 = (f32[1536]{0:T(1024)S(1)}, f32[1536]{0:T(1024)}, u32[]{:S(2)}) copy-start(f32[1536]{0:T(1024)} %refs_5_.7) | copy-start | bytes 18436
  0.0 23.9 %copy-start.4 = (f32[1536]{0:T(1024)S(1)}, f32[1536]{0:T(1024)}, u32[]{:S(2)}) copy-start(f32[1536]{0:T(1024)} %refs_4_.7) | copy-start | bytes 18436
  0.0 1.5 %copy-start.12 = (bf16[2,1024,384]{2,1,0:T(8,128)(2,1)S(1)}, bf16[2,1024,384]{2,1,0:T(8,128)(2,1)}, u32[]{:S(2)}) copy-start(bf16[2,1024,384]{2,1,0:T(8,128)(2,1)} %x_ref.1) | copy-start | bytes 4718596
  1.5 22.4 %copy-start = (bf16[768,1536]{1,0:T(8,128)(2,1)S(1)}, bf16[768,1536]{1,0:T(8,128)(2,1)}, u32[]{:S(2)}) copy-start(bf16[768,1536]{1,0:T(8,128)(2,1)} %refs_2_.5) | copy-start | bytes 7077892
  1.5 22.4 %copy-start.1 = (bf16[1536,768]{1,0:T(8,128)(2,1)S(1)}, bf16[1536,768]{1,0:T(8,128)(2,1)}, u32[]{:S(2)}) copy-start(bf16[1536,768]{1,0:T(8,128)(2,1)} %refs_3_.7) | copy-start | bytes 7077892
  1.5 22.4 %copy-start.2 = (bf16[768,1536]{1,0:T(8,128)(2,1)S(1)}, bf16[768,1536]{1,0:T(8,128)(2,1)}, u32[]{:S(2)}) copy-start(bf16[768,1536]{1,0:T(8,128)(2,1)} %refs_8_.7) | copy-start | bytes 7077892
  1.5 22.4 %copy-start.3 = (bf16[1536,768]{1,0:T(8,128)(2,1)S(1)}, bf16[1536,768]{1,0:T(8,128)(2,1)}, u32[]{:S(2)}) copy-start(bf16[1536,768]{1,0:T(8,128)(2,1)} %refs_9_.7) | copy-start | bytes 7077892
  2.3 4.3 %collective-permute-start = (bf16[7,128,384]{2,1,0:T(8,128)(2,1)S(1)}, bf16[7,128,384]{2,1,0:T(8,128)(2,1)S(1)}, u32[]{:S(2)}, u32[]{:S(2)}) collective-permute-start(bf16[7,128,384]{2,1,0:T(8,128)(2,1)S(1)} %get-tuple-element.27), channel_id=1, source_target_pairs={{0,1},{1,0},{2,3},{3,2},{4,5},{5,4},{6,7},{7,6},{8,9},{9,8},{10,11... | collective-permute-start | bytes 2064392 | tf_op jit(solution)/shard_map/ppermute | solution.py:186
  2.8 15.7 %collective-permute-start.3 = (bf16[128,384]{1,0:T(8,128)(2,1)S(1)}, bf16[128,384]{1,0:T(8,128)(2,1)S(1)}, u32[]{:S(2)}, u32[]{:S(2)}) collective-permute-start(bf16[128,384]{1,0:T(8,128)(2,1)S(1)} %get-tuple-element.36), channel_id=1, source_target_pairs={{0,8},{1,9},{2,10},{3,11},{4,12},{5,13},{6,14},{7,15},{8,0},{9,1},... | collective-permute-start | bytes 294920 | tf_op jit(solution)/shard_map/ppermute | solution.py:186
  6.4 13.7 %collective-permute-start.4 = (bf16[128,384]{1,0:T(8,128)(2,1)S(1)}, bf16[128,384]{1,0:T(8,128)(2,1)S(1)}, u32[]{:S(2)}, u32[]{:S(2)}) collective-permute-start(bf16[128,384]{1,0:T(8,128)(2,1)S(1)} %get-tuple-element.37), channel_id=1, source_target_pairs={{0,9},{1,8},{2,11},{3,10},{4,13},{5,12},{6,15},{7,14},{8,1},{9,0},... | collective-permute-start | bytes 294920 | tf_op jit(solution)/shard_map/ppermute | solution.py:186
  6.6 21.9 %collective-permute-start.1 = (bf16[256,384]{1,0:T(8,128)(2,1)S(1)}, bf16[256,384]{1,0:T(8,128)(2,1)S(1)}, u32[]{:S(2)}, u32[]{:S(2)}) collective-permute-start(bf16[256,384]{1,0:T(8,128)(2,1)S(1)} %get-tuple-element.31), channel_id=1, source_target_pairs={{0,2},{1,3},{2,0},{3,1},{4,6},{5,7},{6,4},{7,5},{8,10},{9,11},{10,... | collective-permute-start | bytes 589832 | tf_op jit(solution)/shard_map/ppermute | solution.py:186
  8.3 20.3 %collective-permute-start.2 = (bf16[256,384]{1,0:T(8,128)(2,1)S(1)}, bf16[256,384]{1,0:T(8,128)(2,1)S(1)}, u32[]{:S(2)}, u32[]{:S(2)}) collective-permute-start(bf16[256,384]{1,0:T(8,128)(2,1)S(1)} %get-tuple-element.32), channel_id=1, source_target_pairs={{0,10},{1,11},{2,8},{3,9},{4,14},{5,15},{6,12},{7,13},{8,2},{9,3},... | collective-permute-start | bytes 589832 | tf_op jit(solution)/shard_map/ppermute | solution.py:186
  20.1 16.0 %collective-permute-start.7 = (bf16[256,384]{1,0:T(8,128)(2,1)S(1)}, bf16[256,384]{1,0:T(8,128)(2,1)S(1)}, u32[]{:S(2)}, u32[]{:S(2)}) collective-permute-start(bf16[256,384]{1,0:T(8,128)(2,1)S(1)} %get-tuple-element.45), channel_id=1, source_target_pairs={{0,4},{1,5},{2,6},{3,7},{4,0},{5,1},{6,2},{7,3},{8,12},{9,13},{10,... | collective-permute-start | bytes 589832 | tf_op jit(solution)/shard_map/ppermute | solution.py:186
  21.1 14.9 %collective-permute-start.8 = (bf16[256,384]{1,0:T(8,128)(2,1)S(1)}, bf16[256,384]{1,0:T(8,128)(2,1)S(1)}, u32[]{:S(2)}, u32[]{:S(2)}) collective-permute-start(bf16[256,384]{1,0:T(8,128)(2,1)S(1)} %get-tuple-element.46), channel_id=1, source_target_pairs={{0,12},{1,13},{2,14},{3,15},{4,8},{5,9},{6,10},{7,11},{8,4},{9,5},... | collective-permute-start | bytes 589832 | tf_op jit(solution)/shard_map/ppermute | solution.py:186
  28.5 12.3 %collective-permute-start.5 = (bf16[256,384]{1,0:T(8,128)(2,1)S(1)}, bf16[256,384]{1,0:T(8,128)(2,1)S(1)}, u32[]{:S(2)}, u32[]{:S(2)}) collective-permute-start(bf16[256,384]{1,0:T(8,128)(2,1)S(1)} %get-tuple-element.41), channel_id=1, source_target_pairs={{0,6},{1,7},{2,4},{3,5},{4,2},{5,3},{6,0},{7,1},{8,14},{9,15},{10,... | collective-permute-start | bytes 589832 | tf_op jit(solution)/shard_map/ppermute | solution.py:186
  30.7 13.5 %collective-permute-start.6 = (bf16[256,384]{1,0:T(8,128)(2,1)S(1)}, bf16[256,384]{1,0:T(8,128)(2,1)S(1)}, u32[]{:S(2)}, u32[]{:S(2)}) collective-permute-start(bf16[256,384]{1,0:T(8,128)(2,1)S(1)} %get-tuple-element.42), channel_id=1, source_target_pairs={{0,14},{1,15},{2,12},{3,13},{4,10},{5,11},{6,8},{7,9},{8,6},{9,7},... | collective-permute-start | bytes 589832 | tf_op jit(solution)/shard_map/ppermute | solution.py:186

commit v4 on v3

--- a/solution.py
+++ b/solution.py
@@ -18,18 +18,27 @@
     return half + half * jnp.tanh(n * (root + (root * 0.044715) * (n * n)))
 
 
-def switch_rows(s, expand, contract, gain, shift, keep, bias):
-    hidden = jnp.dot(s, expand, preferred_element_type=jnp.float32)
+def dot(a, b):
+    return jnp.dot(a, b, preferred_element_type=jnp.float32)
+
+
+def activated(hidden, gain, shift):
     center = hidden - jnp.mean(hidden, axis=-1, keepdims=True)
     spread = jnp.mean(center * center, axis=-1, keepdims=True)
     normed = center * lax.rsqrt(spread + 1e-05) * gain[None] + shift[None]
-    active = gelu(normed).astype(jnp.bfloat16)
-    result = (
-        jax.nn.sigmoid(keep[None]) * s.astype(jnp.float32)
-        + jnp.dot(active, contract, preferred_element_type=jnp.float32)
-        + bias[None]
-    )
-    return result.astype(jnp.bfloat16)
+    return gelu(normed).astype(jnp.bfloat16)
+
+
+def switch_tiles(tiles, expand, contract, gain, shift, keep, bias):
+    keep = jax.nn.sigmoid(keep[None])
+    hidden, results = [dot(tiles[0], expand)], []
+    for i, s in enumerate(tiles):
+        if i + 1 < len(tiles):
+            hidden.append(dot(tiles[i + 1], expand))
+        active = activated(hidden[i], gain, shift)
+        result = keep * s.astype(jnp.float32) + dot(active, contract) + bias[None]
+        results.append(result.astype(jnp.bfloat16))
+    return results
 
 
 def iota2(shape, dim):
@@ -118,15 +127,10 @@
     first = [ref[...] for ref in first]
     second = [ref[...] for ref in second]
     width = roles.shape[-1]
-    mids = [
-        switch_rows(jnp.concatenate([roles[c], roles[2 + c]], axis=-1), *first) for c in range(2)
-    ]
-    ends = []
-    for half in range(2):
-        part = slice(half * width, (half + 1) * width)
-        o = switch_rows(jnp.concatenate([mids[0][:, part], mids[1][:, part]], axis=-1), *second)
-        ends += [o[:, :width], o[:, width:]]
-    return ends
+    mids = switch_tiles([jnp.concatenate([roles[c], roles[2 + c]], axis=-1) for c in range(2)], *first)
+    halves = [slice(0, width), slice(width, 2 * width)]
+    pairs = [jnp.concatenate([mids[0][:, part], mids[1][:, part]], axis=-1) for part in halves]
+    return [o[:, part] for o in switch_tiles(pairs, *second) for part in halves]
 
 
 def group_kernel(blocks, *refs):
@@ -229,10 +233,10 @@
     clusters = devices // (2 * REACH)
     halves = received.reshape(clusters, 2, REACH, streams * slots, width)
     pairs = jnp.concatenate([halves[:, 0], halves[:, 1]], axis=-1).reshape(-1, 2 * width)
-    mid = switch_rows(pairs, *first)
+    (mid,) = switch_tiles([pairs], *first)
     mid = mid.reshape(clusters, REACH // 2, 2, streams * slots, 2, width)
     pairs = mid.transpose(0, 4, 1, 3, 2, 5).reshape(-1, 2 * width)
-    result = switch_rows(pairs, *second)
+    (result,) = switch_tiles([pairs], *second)
     result = result.reshape(devices // 2, streams, slots, 2, width)
     return result.transpose(1, 2, 0, 3, 4).reshape(streams, rows_here, width)
 

time: 50.7 us -> 49.9 us (0.984)
  Pallas kernels: 20.9 us -> 16.7 us
  waiting for transfers between devices: 12.7 us -> 16.1 us
    pallas_call x4, Pallas kernels: 20.1 us -> 15.9 us  [run_group(): pl.pallas_call(functools.partial(kernel, len(blocks)), out_shape=out_shap...]
    ppermute x9, waiting for transfers between devices: 12.7 us -> 16.1 us  [send(): return lax.ppermute(value, 'seq', [(d, d ^ mask) for d in range(shards)])]
  transfers between devices with their start and end apart: 9 -> 9, of which waited for: 3 -> 4; matrix products, arithmetic and copies ran while one was open for 0% -> 0% of each run, Pallas kernels for 27% -> 21%
where the time goes in v4:
time: 49.9 us; the launch traced here: 49.7 us
  Pallas kernels  16.7 us (33%)
  waiting for transfers between devices  16.1 us (32%)
  starting transfers between devices  15.2 us (30%)
  local copies, waits for them, and re-layouts  1.53 us (3%)
    ppermute x9, waiting for transfers between devices, send(): return lax.ppermute(value, 'seq', [(d, d ^ mask) for d in range(shards)])  16.1 us
    pallas_call x4, Pallas kernels, run_group(): pl.pallas_call(functools.partial(kernel, len(blocks)), out_shape=out_shap...  15.9 us
    ppermute x9, starting transfers between devices, send(): return lax.ppermute(value, 'seq', [(d, d ^ mask) for d in range(shards)])  15.2 us
    unnamed x26, local copies, waits for them, and re-layouts  1.53 us
  transfers between devices with their start and end apart: 9, of which 4 were waited for; matrix products, arithmetic and copies ran while one was open for 0% of the time, Pallas kernels for 21%

profile of v4, /device:TPU:0, one launch (start us, length us, event | category | flops | bytes accessed | tf_op | source)
XLA Modules:
  0.0 49.7 jit_solution(3869662293179523899)
XLA Ops:
  0.0 0.0 copy-start.8
  0.0 0.0 copy-start.5
  0.0 0.0 copy-start.4
  0.0 0.0 copy-start.12
  0.1 1.5 %copy-done.12 = bf16[2,1024,384]{2,1,0:T(8,128)(2,1)S(1)} copy-done((bf16[2,1024,384]{2,1,0:T(8,128)(2,1)S(1)}, bf16[2,1024,384]{2,1,0:T(8,128)(2,1)}, u32[]{:S(2)}) %copy-start.12) | copy-done | bytes 1572888
  1.5 0.7 %sort_rows.1 = (bf16[128,384]{1,0:T(8,128)(2,1)S(1)}, bf16[7,128,384]{2,1,0:T(8,128)(2,1)S(1)}, bf16[6,128,384]{2,1,0:T(8,128)(2,1)S(1)}, bf16[128,384]{1,0:T(8,128)(2,1)S(1)}, bf16[128,384]{1,0:T(8,128)(2,1)S(1)}) custom-call(bf16[2,1024,384]{2,1,0:T(8,128)(2,1)S(1)} %copy-done.12), custom_call_target="tpu_custom_call" | custom-call | flops 30000001024 | bytes 3145728 | tf_op jit(solution)/shard_map/sort_rows/pallas_call | solution.py:88
  2.3 0.5 %collective-permute-start = (bf16[7,128,384]{2,1,0:T(8,128)(2,1)S(1)}, bf16[7,128,384]{2,1,0:T(8,128)(2,1)S(1)}, u32[]{:S(2)}, u32[]{:S(2)}) collective-permute-start(bf16[7,128,384]{2,1,0:T(8,128)(2,1)S(1)} %get-tuple-element.27), channel_id=1, source_target_pairs={{0,1},{1,0},{2,3},{3,2},{4,5},{5,4},{6,7},{7,6},{8,9},{9,8},{10,11... | collective-permute-start | bytes 2064392 | tf_op jit(solution)/shard_map/ppermute | solution.py:190
  2.8 3.7 %collective-permute-start.3 = (bf16[128,384]{1,0:T(8,128)(2,1)S(1)}, bf16[128,384]{1,0:T(8,128)(2,1)S(1)}, u32[]{:S(2)}, u32[]{:S(2)}) collective-permute-start(bf16[128,384]{1,0:T(8,128)(2,1)S(1)} %get-tuple-element.36), channel_id=1, source_target_pairs={{0,8},{1,9},{2,10},{3,11},{4,12},{5,13},{6,14},{7,15},{8,0},{9,1},... | collective-permute-start | bytes 294920 | tf_op jit(solution)/shard_map/ppermute | solution.py:190
  6.4 0.1 collective-permute-start.4
  6.5 0.0 collective-permute-done.mate
  6.5 0.1 join_rows.1
  6.6 1.6 %collective-permute-start.1 = (bf16[256,384]{1,0:T(8,128)(2,1)S(1)}, bf16[256,384]{1,0:T(8,128)(2,1)S(1)}, u32[]{:S(2)}, u32[]{:S(2)}) collective-permute-start(bf16[256,384]{1,0:T(8,128)(2,1)S(1)} %get-tuple-element.31), channel_id=1, source_target_pairs={{0,2},{1,3},{2,0},{3,1},{4,6},{5,7},{6,4},{7,5},{8,10},{9,11},{10,... | collective-permute-start | bytes 589832 | tf_op jit(solution)/shard_map/ppermute | solution.py:190
  8.3 2.5 %collective-permute-start.2 = (bf16[256,384]{1,0:T(8,128)(2,1)S(1)}, bf16[256,384]{1,0:T(8,128)(2,1)S(1)}, u32[]{:S(2)}, u32[]{:S(2)}) collective-permute-start(bf16[256,384]{1,0:T(8,128)(2,1)S(1)} %get-tuple-element.32), channel_id=1, source_target_pairs={{0,10},{1,11},{2,8},{3,9},{4,14},{5,15},{6,12},{7,13},{8,2},{9,3},... | collective-permute-start | bytes 589832 | tf_op jit(solution)/shard_map/ppermute | solution.py:190
  10.8 7.7 %collective-permute-done.3.refs_1_ = bf16[128,384]{1,0:T(8,128)(2,1)S(1)} collective-permute-done((bf16[128,384]{1,0:T(8,128)(2,1)S(1)}, bf16[128,384]{1,0:T(8,128)(2,1)S(1)}, u32[]{:S(2)}, u32[]{:S(2)}) %collective-permute-start.3) | collective-permute-done | bytes 98336 | tf_op jit(solution)/shard_map/ppermute | solution.py:190
  18.5 1.6 %collective-permute-done.4.refs_2_ = bf16[128,384]{1,0:T(8,128)(2,1)S(1)} collective-permute-done((bf16[128,384]{1,0:T(8,128)(2,1)S(1)}, bf16[128,384]{1,0:T(8,128)(2,1)S(1)}, u32[]{:S(2)}, u32[]{:S(2)}) %collective-permute-start.4) | collective-permute-done | bytes 98336 | tf_op jit(solution)/shard_map/ppermute | solution.py:190
  20.1 1.0 %collective-permute-start.7 = (bf16[256,384]{1,0:T(8,128)(2,1)S(1)}, bf16[256,384]{1,0:T(8,128)(2,1)S(1)}, u32[]{:S(2)}, u32[]{:S(2)}) collective-permute-start(bf16[256,384]{1,0:T(8,128)(2,1)S(1)} %get-tuple-element.45), channel_id=1, source_target_pairs={{0,4},{1,5},{2,6},{3,7},{4,0},{5,1},{6,2},{7,3},{8,12},{9,13},{10,... | collective-permute-start | bytes 589832 | tf_op jit(solution)/shard_map/ppermute | solution.py:190
  21.1 2.7 %collective-permute-start.8 = (bf16[256,384]{1,0:T(8,128)(2,1)S(1)}, bf16[256,384]{1,0:T(8,128)(2,1)S(1)}, u32[]{:S(2)}, u32[]{:S(2)}) collective-permute-start(bf16[256,384]{1,0:T(8,128)(2,1)S(1)} %get-tuple-element.46), channel_id=1, source_target_pairs={{0,12},{1,13},{2,14},{3,15},{4,8},{5,9},{6,10},{7,11},{8,4},{9,5},... | collective-permute-start | bytes 589832 | tf_op jit(solution)/shard_map/ppermute | solution.py:190
  23.9 0.0 copy-done.11
  23.9 0.0 copy-done.10
  23.9 0.0 copy-done.7
  24.0 3.5 %switch_group.3.refs_14_ = bf16[4,128,384]{2,1,0:T(8,128)(2,1)S(1)} custom-call(bf16[256,384]{1,0:T(8,128)(2,1)S(1)} %get-tuple-element.38.refs_0_, bf16[128,384]{1,0:T(8,128)(2,1)S(1)} %collective-permute-done.3.refs_1_, bf16[128,384]{1,0:T(8,128)(2,1)S(1)} %collective-permute-done.4.refs_2_, bf16[768,1536]{1,0:T(8,128)(2,1)S(1)} %copy-done, ...), custom_call_target="tpu_custom_call" | custom-call | tf_op jit(solution)/shard_map/switch_group/pallas_call | solution.py:167
  27.5 0.0 collective-permute-done.1.refs_0_
  27.5 0.0 collective-permute-done.2.refs_1_
  27.5 2.1 %collective-permute-start.5 = (bf16[256,384]{1,0:T(8,128)(2,1)S(1)}, bf16[256,384]{1,0:T(8,128)(2,1)S(1)}, u32[]{:S(2)}, u32[]{:S(2)}) collective-permute-start(bf16[256,384]{1,0:T(8,128)(2,1)S(1)} %get-tuple-element.41), channel_id=1, source_target_pairs={{0,6},{1,7},{2,4},{3,5},{4,2},{5,3},{6,0},{7,1},{8,14},{9,15},{10,... | collective-permute-start | bytes 589832 | tf_op jit(solution)/shard_map/ppermute | solution.py:190
  29.6 0.9 %collective-permute-start.6 = (bf16[256,384]{1,0:T(8,128)(2,1)S(1)}, bf16[256,384]{1,0:T(8,128)(2,1)S(1)}, u32[]{:S(2)}, u32[]{:S(2)}) collective-permute-start(bf16[256,384]{1,0:T(8,128)(2,1)S(1)} %get-tuple-element.42), channel_id=1, source_target_pairs={{0,14},{1,15},{2,12},{3,13},{4,10},{5,11},{6,8},{7,9},{8,6},{9,7},... | collective-permute-start | bytes 589832 | tf_op jit(solution)/shard_map/ppermute | solution.py:190
  30.5 3.5 %switch_group.4.refs_15_ = bf16[4,128,384]{2,1,0:T(8,128)(2,1)S(1)} custom-call(bf16[256,384]{1,0:T(8,128)(2,1)S(1)} %collective-permute-done.1.refs_0_, bf16[256,384]{1,0:T(8,128)(2,1)S(1)} %collective-permute-done.2.refs_1_, bf16[768,1536]{1,0:T(8,128)(2,1)S(1)} %copy-done, bf16[1536,768]{1,0:T(8,128)(2,1)S(1)} %copy-done.1, f32[1536]{0:T(1024)S(1)} %copy-done.4, ...), custom_call_target="tpu_custom_call" | custom-call | tf_op jit(solution)/shard_map/switch_group/pallas_call | solution.py:167
  34.0 0.0 collective-permute-done.7.refs_0_
  34.0 0.0 collective-permute-done.8.refs_1_
  34.0 3.5 %switch_group.5.refs_16_ = bf16[4,128,384]{2,1,0:T(8,128)(2,1)S(1)} custom-call(bf16[256,384]{1,0:T(8,128)(2,1)S(1)} %collective-permute-done.7.refs_0_, bf16[256,384]{1,0:T(8,128)(2,1)S(1)} %collective-permute-done.8.refs_1_, bf16[768,1536]{1,0:T(8,128)(2,1)S(1)} %copy-done, bf16[1536,768]{1,0:T(8,128)(2,1)S(1)} %copy-done.1, f32[1536]{0:T(1024)S(1)} %copy-done.4, ...), custom_call_target="tpu_custom_call" | custom-call | flops 2415919104 | bytes 9867264 | tf_op jit(solution)/shard_map/switch_group/pallas_call | solution.py:167
  37.5 1.1 %collective-permute-done.5.refs_0_ = bf16[256,384]{1,0:T(8,128)(2,1)S(1)} collective-permute-done((bf16[256,384]{1,0:T(8,128)(2,1)S(1)}, bf16[256,384]{1,0:T(8,128)(2,1)S(1)}, u32[]{:S(2)}, u32[]{:S(2)}) %collective-permute-start.5) | collective-permute-done | bytes 196640 | tf_op jit(solution)/shard_map/ppermute | solution.py:190
  38.6 5.7 %collective-permute-done.6.refs_1_ = bf16[256,384]{1,0:T(8,128)(2,1)S(1)} collective-permute-done((bf16[256,384]{1,0:T(8,128)(2,1)S(1)}, bf16[256,384]{1,0:T(8,128)(2,1)S(1)}, u32[]{:S(2)}, u32[]{:S(2)}) %collective-permute-start.6) | collective-permute-done | bytes 196640 | tf_op jit(solution)/shard_map/ppermute | solution.py:190
  44.3 5.5 %switch_last.1 = bf16[2,1024,384]{2,1,0:T(8,128)(2,1)} custom-call(bf16[256,384]{1,0:T(8,128)(2,1)S(1)} %collective-permute-done.5.refs_0_, bf16[256,384]{1,0:T(8,128)(2,1)S(1)} %collective-permute-done.6.refs_1_, bf16[768,1536]{1,0:T(8,128)(2,1)S(1)} %copy-done, bf16[1536,768]{1,0:T(8,128)(2,1)S(1)} %copy-done.1, f32[1536]{0:T(1024)S(1)} %copy-done.4, ...), custom_call_target="tpu_custom_call" | custom-call | flops 2415919104 | bytes 11046912 | tf_op jit(solution)/shard_map/switch_last/pallas_call | solution.py:167
  (18 shorter events, 0.0 us)
Async XLA Ops:
  0.0 23.9 %copy-start.11 = (f32[768]{0:T(1024)S(1)}, f32[768]{0:T(1024)}, u32[]{:S(2)}) copy-start(f32[768]{0:T(1024)} %refs_13_.7) | copy-start | bytes 9220
  0.0 23.9 %copy-start.10 = (f32[768]{0:T(1024)S(1)}, f32[768]{0:T(1024)}, u32[]{:S(2)}) copy-start(f32[768]{0:T(1024)} %refs_12_.7) | copy-start | bytes 9220
  0.0 23.9 %copy-start.7 = (f32[1536]{0:T(1024)S(1)}, f32[1536]{0:T(1024)}, u32[]{:S(2)}) copy-start(f32[1536]{0:T(1024)} %refs_11_.7) | copy-start | bytes 18436
  0.0 23.9 %copy-start.6 = (f32[1536]{0:T(1024)S(1)}, f32[1536]{0:T(1024)}, u32[]{:S(2)}) copy-start(f32[1536]{0:T(1024)} %refs_10_.7) | copy-start | bytes 18436
  0.0 23.9 %copy-start.9 = (f32[768]{0:T(1024)S(1)}, f32[768]{0:T(1024)}, u32[]{:S(2)}) copy-start(f32[768]{0:T(1024)} %refs_7_.7) | copy-start | bytes 9220
  0.0 23.9 %copy-start.8 = (f32[768]{0:T(1024)S(1)}, f32[768]{0:T(1024)}, u32[]{:S(2)}) copy-start(f32[768]{0:T(1024)} %refs_6_.7) | copy-start | bytes 9220
  0.0 23.9 %copy-start.5 = (f32[1536]{0:T(1024)S(1)}, f32[1536]{0:T(1024)}, u32[]{:S(2)}) copy-start(f32[1536]{0:T(1024)} %refs_5_.7) | copy-start | bytes 18436
  0.0 23.9 %copy-start.4 = (f32[1536]{0:T(1024)S(1)}, f32[1536]{0:T(1024)}, u32[]{:S(2)}) copy-start(f32[1536]{0:T(1024)} %refs_4_.7) | copy-start | bytes 18436
  0.0 1.5 %copy-start.12 = (bf16[2,1024,384]{2,1,0:T(8,128)(2,1)S(1)}, bf16[2,1024,384]{2,1,0:T(8,128)(2,1)}, u32[]{:S(2)}) copy-start(bf16[2,1024,384]{2,1,0:T(8,128)(2,1)} %x_ref.1) | copy-start | bytes 4718596
  1.5 22.4 %copy-start = (bf16[768,1536]{1,0:T(8,128)(2,1)S(1)}, bf16[768,1536]{1,0:T(8,128)(2,1)}, u32[]{:S(2)}) copy-start(bf16[768,1536]{1,0:T(8,128)(2,1)} %refs_2_.5) | copy-start | bytes 7077892
  1.5 22.4 %copy-start.1 = (bf16[1536,768]{1,0:T(8,128)(2,1)S(1)}, bf16[1536,768]{1,0:T(8,128)(2,1)}, u32[]{:S(2)}) copy-start(bf16[1536,768]{1,0:T(8,128)(2,1)} %refs_3_.7) | copy-start | bytes 7077892
  1.5 22.4 %copy-start.2 = (bf16[768,1536]{1,0:T(8,128)(2,1)S(1)}, bf16[768,1536]{1,0:T(8,128)(2,1)}, u32[]{:S(2)}) copy-start(bf16[768,1536]{1,0:T(8,128)(2,1)} %refs_8_.7) | copy-start | bytes 7077892
  1.5 22.4 %copy-start.3 = (bf16[1536,768]{1,0:T(8,128)(2,1)S(1)}, bf16[1536,768]{1,0:T(8,128)(2,1)}, u32[]{:S(2)}) copy-start(bf16[1536,768]{1,0:T(8,128)(2,1)} %refs_9_.7) | copy-start | bytes 7077892
  2.3 4.3 %collective-permute-start = (bf16[7,128,384]{2,1,0:T(8,128)(2,1)S(1)}, bf16[7,128,384]{2,1,0:T(8,128)(2,1)S(1)}, u32[]{:S(2)}, u32[]{:S(2)}) collective-permute-start(bf16[7,128,384]{2,1,0:T(8,128)(2,1)S(1)} %get-tuple-element.27), channel_id=1, source_target_pairs={{0,1},{1,0},{2,3},{3,2},{4,5},{5,4},{6,7},{7,6},{8,9},{9,8},{10,11... | collective-permute-start | bytes 2064392 | tf_op jit(solution)/shard_map/ppermute | solution.py:190
  2.8 15.7 %collective-permute-start.3 = (bf16[128,384]{1,0:T(8,128)(2,1)S(1)}, bf16[128,384]{1,0:T(8,128)(2,1)S(1)}, u32[]{:S(2)}, u32[]{:S(2)}) collective-permute-start(bf16[128,384]{1,0:T(8,128)(2,1)S(1)} %get-tuple-element.36), channel_id=1, source_target_pairs={{0,8},{1,9},{2,10},{3,11},{4,12},{5,13},{6,14},{7,15},{8,0},{9,1},... | collective-permute-start | bytes 294920 | tf_op jit(solution)/shard_map/ppermute | solution.py:190
  6.4 13.7 %collective-permute-start.4 = (bf16[128,384]{1,0:T(8,128)(2,1)S(1)}, bf16[128,384]{1,0:T(8,128)(2,1)S(1)}, u32[]{:S(2)}, u32[]{:S(2)}) collective-permute-start(bf16[128,384]{1,0:T(8,128)(2,1)S(1)} %get-tuple-element.37), channel_id=1, source_target_pairs={{0,9},{1,8},{2,11},{3,10},{4,13},{5,12},{6,15},{7,14},{8,1},{9,0},... | collective-permute-start | bytes 294920 | tf_op jit(solution)/shard_map/ppermute | solution.py:190
  6.6 20.8 %collective-permute-start.1 = (bf16[256,384]{1,0:T(8,128)(2,1)S(1)}, bf16[256,384]{1,0:T(8,128)(2,1)S(1)}, u32[]{:S(2)}, u32[]{:S(2)}) collective-permute-start(bf16[256,384]{1,0:T(8,128)(2,1)S(1)} %get-tuple-element.31), channel_id=1, source_target_pairs={{0,2},{1,3},{2,0},{3,1},{4,6},{5,7},{6,4},{7,5},{8,10},{9,11},{10,... | collective-permute-start | bytes 589832 | tf_op jit(solution)/shard_map/ppermute | solution.py:190
  8.3 19.2 %collective-permute-start.2 = (bf16[256,384]{1,0:T(8,128)(2,1)S(1)}, bf16[256,384]{1,0:T(8,128)(2,1)S(1)}, u32[]{:S(2)}, u32[]{:S(2)}) collective-permute-start(bf16[256,384]{1,0:T(8,128)(2,1)S(1)} %get-tuple-element.32), channel_id=1, source_target_pairs={{0,10},{1,11},{2,8},{3,9},{4,14},{5,15},{6,12},{7,13},{8,2},{9,3},... | collective-permute-start | bytes 589832 | tf_op jit(solution)/shard_map/ppermute | solution.py:190
  20.1 13.9 %collective-permute-start.7 = (bf16[256,384]{1,0:T(8,128)(2,1)S(1)}, bf16[256,384]{1,0:T(8,128)(2,1)S(1)}, u32[]{:S(2)}, u32[]{:S(2)}) collective-permute-start(bf16[256,384]{1,0:T(8,128)(2,1)S(1)} %get-tuple-element.45), channel_id=1, source_target_pairs={{0,4},{1,5},{2,6},{3,7},{4,0},{5,1},{6,2},{7,3},{8,12},{9,13},{10,... | collective-permute-start | bytes 589832 | tf_op jit(solution)/shard_map/ppermute | solution.py:190
  21.1 12.8 %collective-permute-start.8 = (bf16[256,384]{1,0:T(8,128)(2,1)S(1)}, bf16[256,384]{1,0:T(8,128)(2,1)S(1)}, u32[]{:S(2)}, u32[]{:S(2)}) collective-permute-start(bf16[256,384]{1,0:T(8,128)(2,1)S(1)} %get-tuple-element.46), channel_id=1, source_target_pairs={{0,12},{1,13},{2,14},{3,15},{4,8},{5,9},{6,10},{7,11},{8,4},{9,5},... | collective-permute-start | bytes 589832 | tf_op jit(solution)/shard_map/ppermute | solution.py:190
  27.5 11.1 %collective-permute-start.5 = (bf16[256,384]{1,0:T(8,128)(2,1)S(1)}, bf16[256,384]{1,0:T(8,128)(2,1)S(1)}, u32[]{:S(2)}, u32[]{:S(2)}) collective-permute-start(bf16[256,384]{1,0:T(8,128)(2,1)S(1)} %get-tuple-element.41), channel_id=1, source_target_pairs={{0,6},{1,7},{2,4},{3,5},{4,2},{5,3},{6,0},{7,1},{8,14},{9,15},{10,... | collective-permute-start | bytes 589832 | tf_op jit(solution)/shard_map/ppermute | solution.py:190
  29.6 14.7 %collective-permute-start.6 = (bf16[256,384]{1,0:T(8,128)(2,1)S(1)}, bf16[256,384]{1,0:T(8,128)(2,1)S(1)}, u32[]{:S(2)}, u32[]{:S(2)}) collective-permute-start(bf16[256,384]{1,0:T(8,128)(2,1)S(1)} %get-tuple-element.42), channel_id=1, source_target_pairs={{0,14},{1,15},{2,12},{3,13},{4,10},{5,11},{6,8},{7,9},{8,6},{9,7},... | collective-permute-start | bytes 589832 | tf_op jit(solution)/shard_map/ppermute | solution.py:190

commit v5 on v4

--- a/solution.py
+++ b/solution.py
@@ -8,6 +8,8 @@
 from jax.sharding import PartitionSpec as P
 
 REACH = 8
+FIRSTS = (REACH, REACH + 1)
+ORDER = ((10, ()), (2, ()), (12, (8,)), (4, (8, 9)), (14, (8, 9)), (6, (2, 10)))
 WEIGH = (0, 0, 1)
 MIB = 1 << 20
 
@@ -141,7 +143,7 @@
 
 def last_kernel(blocks, shards, *refs):
     first, second = refs[blocks : blocks + 6], refs[blocks + 6 : blocks + 12]
-    done, out, roles = refs[blocks + 12 : -2], refs[-2], refs[-1]
+    done, out, roles, whole, sems = refs[blocks + 12 : -4], refs[-4], refs[-3], refs[-2], refs[-1]
     ends = group_blocks(refs[:blocks], roles, first, second)
     me = lax.axis_index("seq")
     near = (me & (REACH - 1)) >> 1
@@ -150,17 +152,22 @@
     group, half, core = col // (4 * shards), (col // (2 * shards)) % 2, (col // shards) % 2
     source = half * REACH + ((group ^ near) * 2 + core)
     place = one_hot((row // shards == col % shards) & (row % shards == source))
-    streams, rows, _ = out.shape
+    streams, rows, _ = whole.shape
+    copies = []
     for s in range(streams):
         for t in range(rows // tile):
             at = s * (rows // shards) + t * shards
             parts = [d[i, at : at + shards] for d in done for i in range(4)]
             parts += [end[at : at + shards] for end in ends]
-            y = jnp.dot(place, jnp.concatenate(parts, axis=0), preferred_element_type=jnp.float32)
-            out[s, t * tile : (t + 1) * tile] = y.astype(jnp.bfloat16)
-
-
-def run_group(kernel, blocks, count, params, extra, out_shape, name, weigh=1):
+            to = (s, slice(t * tile, (t + 1) * tile))
+            whole[to] = dot(place, jnp.concatenate(parts, axis=0)).astype(jnp.bfloat16)
+            copies.append(pltpu.make_async_copy(whole.at[to], out.at[to], sems.at[s, t]))
+            copies[-1].start()
+    for copy in copies:
+        copy.wait()
+
+
+def run_group(kernel, blocks, count, params, extra, out_shape, out_spec, scratch, name, weigh=1):
     width = blocks[0].shape[-1]
     args = (*blocks, *params, *extra)
     hidden = params[0].shape[1]
@@ -168,8 +175,8 @@
         functools.partial(kernel, len(blocks)),
         out_shape=out_shape,
         in_specs=[pl.BlockSpec(memory_space=pltpu.VMEM)] * len(args),
-        out_specs=pl.BlockSpec(memory_space=pltpu.VMEM),
-        scratch_shapes=[pltpu.VMEM((4, count, width), jnp.bfloat16)],
+        out_specs=pl.BlockSpec(memory_space=out_spec),
+        scratch_shapes=[pltpu.VMEM((4, count, width), jnp.bfloat16), *scratch],
         compiler_params=pltpu.CompilerParams(vmem_limit_bytes=32 * MIB),
         cost_estimate=pl.CostEstimate(
             flops=weigh * 2 * 2 * count * 4 * 2 * width * hidden,
@@ -180,47 +187,44 @@
     )(*args)
 
 
-def after(values, *before):
-    held = lax.optimization_barrier((*values, *before))
-    return held[: len(values)]
-
-
 def exchanged(features, params, shards):
-    def send(value, mask):
-        return lax.ppermute(value, "seq", [(d, d ^ mask) for d in range(shards)])
-
-    straight, mate, ahead, far0, far1 = sort_rows(features, shards)
-    count = straight.shape[0]
+    straight, mate, ahead, *firsts = sort_rows(features, shards)
+    count, width = straight.shape
     groups = REACH // 2
-    far0, far1 = send(far0, REACH), send(far1, REACH + 1)
-    joined = join_rows(straight, send(mate, 1), ahead)
-    near = list(joined[:groups])
-    far = [None, *joined[groups:]]
-    block = jax.ShapeDtypeStruct((4, count, features.shape[-1]), features.dtype)
-
-    def group(index):
-        near_rows, far_rows = arrived[index]
-        return run_group(
-            group_kernel, (near_rows, *far_rows), count, params, (), block, "switch_group", WEIGH[index]
-        )
-
+    got = {}
+
+    def send(value, mask, before=()):
+        if before:
+            value, *held = lax.optimization_barrier((value, *(got[key] for key in before)))
+            got.update(zip(before, held))
+        got[mask] = lax.ppermute(value, "seq", [(d, d ^ mask) for d in range(shards)])
+
+    for mask, value in zip(FIRSTS, firsts):
+        send(value, mask)
+    send(mate, 1)
+    joined = join_rows(straight, got[1], ahead)
+    got[0] = joined[0]
+    ready = dict(zip([*range(2, REACH, 2), *range(REACH + 2, 2 * REACH, 2)], joined[1:]))
+    for mask, before in ORDER:
+        send(ready[mask], mask, before)
+    block = jax.ShapeDtypeStruct((4, count, width), features.dtype)
+    whole = jax.ShapeDtypeStruct(features.shape, features.dtype)
     ends = []
-    arrived = [(near[0], (far0, far1))]
-    arrived.append((send(near[1], 2), (send(far[1], REACH + 2),)))
-    for g in range(2, groups):
-        past_near, past_far = arrived[g - 2]
-        near_next, far_next, past_near, *past_far = after((near[g], far[g], past_near, *past_far), *ends[:g - 1])
-        arrived[g - 2] = (past_near, tuple(past_far))
-        arrived.append((send(near_next, 2 * g), (send(far_next, REACH + 2 * g),)))
-        ends.append(group(g - 2))
-    ends.append(group(groups - 2))
-    near_rows, far_rows = arrived[groups - 1]
-    whole = jax.ShapeDtypeStruct(features.shape, features.dtype)
+    for g in range(groups):
+        far = FIRSTS if g == 0 else (REACH + 2 * g,)
+        blocks = [got[2 * g], *(got[mask] for mask in far)]
+        if g < groups - 1:
+            ends.append(
+                run_group(group_kernel, blocks, count, params, (), block, pltpu.VMEM, (), "switch_group", WEIGH[g])
+            )
 
     def kernel(blocks, *refs):
         last_kernel(blocks, shards, *refs)
 
-    return run_group(kernel, (near_rows, *far_rows), count, params, tuple(ends), whole, "switch_last")
+    streams, rows, _ = features.shape
+    sems = pltpu.SemaphoreType.DMA((streams, rows // (shards * shards)))
+    scratch = (pltpu.VMEM(whole.shape, whole.dtype), sems)
+    return run_group(kernel, blocks, count, params, tuple(ends), whole, pltpu.HBM, scratch, "switch_last")
 
 
 def gathered(features, first, second):

time: 49.9 us -> 49 us (0.982); the launches traced: 49.7 us -> 48.1 us
  starting transfers between devices: 15.2 us -> 14.3 us
  waiting for transfers between devices: 16.1 us -> 15.5 us
    ppermute x9, starting transfers between devices: 15.2 us -> 14.3 us  [send(): lax.ppermute(value, 'seq', [(d, d ^ mask) for d in range(shards)])]
    ppermute x9, waiting for transfers between devices: 16.1 us -> 15.5 us  [send(): lax.ppermute(value, 'seq', [(d, d ^ mask) for d in range(shards)])]
  transfers between devices with their start and end apart: 9 -> 9, of which waited for: 4 -> 5; matrix products, arithmetic and copies ran while one was open for 0% -> 0% of each run, Pallas kernels for 21% -> 22%
where the time goes in v5:
time: 49 us; the launch traced here: 48.1 us
  Pallas kernels  16.3 us (33%)
  waiting for transfers between devices  15.5 us (32%)
  starting transfers between devices  14.3 us (29%)
  local copies, waits for them, and re-layouts  1.53 us (3%)
    ppermute x9, waiting for transfers between devices, send(): lax.ppermute(value, 'seq', [(d, d ^ mask) for d in range(shards)])  15.5 us
    pallas_call x4, Pallas kernels, run_group(): pl.pallas_call(functools.partial(kernel, len(blocks)), out_shape=out_shap...  15.5 us
    ppermute x9, starting transfers between devices, send(): lax.ppermute(value, 'seq', [(d, d ^ mask) for d in range(shards)])  14.3 us
    unnamed x26, local copies, waits for them, and re-layouts  1.53 us
  transfers between devices with their start and end apart: 9, of which 5 were waited for; matrix products, arithmetic and copies ran while one was open for 0% of the time, Pallas kernels for 22%

profile of v5, /device:TPU:0, one launch (start us, length us, event | category | flops | bytes accessed | tf_op | source)
XLA Modules:
  0.0 48.1 jit_solution(3129847160902991767)
XLA Ops:
  0.0 0.0 copy-start.8
  0.0 0.0 copy-start.5
  0.0 0.0 copy-start.4
  0.0 0.0 copy-start.12
  0.1 1.5 %copy-done.12 = bf16[2,1024,384]{2,1,0:T(8,128)(2,1)S(1)} copy-done((bf16[2,1024,384]{2,1,0:T(8,128)(2,1)S(1)}, bf16[2,1024,384]{2,1,0:T(8,128)(2,1)}, u32[]{:S(2)}) %copy-start.12) | copy-done | bytes 1572888
  1.5 0.7 %sort_rows.1 = (bf16[128,384]{1,0:T(8,128)(2,1)S(1)}, bf16[7,128,384]{2,1,0:T(8,128)(2,1)S(1)}, bf16[6,128,384]{2,1,0:T(8,128)(2,1)S(1)}, bf16[128,384]{1,0:T(8,128)(2,1)S(1)}, bf16[128,384]{1,0:T(8,128)(2,1)S(1)}) custom-call(bf16[2,1024,384]{2,1,0:T(8,128)(2,1)S(1)} %copy-done.12), custom_call_target="tpu_custom_call" | custom-call | flops 30000001024 | bytes 3145728 | tf_op jit(solution)/shard_map/sort_rows/pallas_call | solution.py:90
  2.3 0.5 %collective-permute-start = (bf16[7,128,384]{2,1,0:T(8,128)(2,1)S(1)}, bf16[7,128,384]{2,1,0:T(8,128)(2,1)S(1)}, u32[]{:S(2)}, u32[]{:S(2)}) collective-permute-start(bf16[7,128,384]{2,1,0:T(8,128)(2,1)S(1)} %get-tuple-element.29), channel_id=1, source_target_pairs={{0,1},{1,0},{2,3},{3,2},{4,5},{5,4},{6,7},{7,6},{8,9},{9,8},{10,11... | collective-permute-start | bytes 2064392 | tf_op jit(solution)/shard_map/ppermute | solution.py:200
  2.8 3.7 %collective-permute-start.4 = (bf16[128,384]{1,0:T(8,128)(2,1)S(1)}, bf16[128,384]{1,0:T(8,128)(2,1)S(1)}, u32[]{:S(2)}, u32[]{:S(2)}) collective-permute-start(bf16[128,384]{1,0:T(8,128)(2,1)S(1)} %get-tuple-element.38), channel_id=1, source_target_pairs={{0,8},{1,9},{2,10},{3,11},{4,12},{5,13},{6,14},{7,15},{8,0},{9,1},... | collective-permute-start | bytes 294920 | tf_op jit(solution)/shard_map/ppermute | solution.py:200
  6.4 0.1 collective-permute-start.5
  6.5 0.0 collective-permute-done.mate
  6.5 0.1 join_rows.1
  6.6 1.6 %collective-permute-start.1 = (bf16[256,384]{1,0:T(8,128)(2,1)S(1)}, bf16[256,384]{1,0:T(8,128)(2,1)S(1)}, u32[]{:S(2)}, u32[]{:S(2)}) collective-permute-start(bf16[256,384]{1,0:T(8,128)(2,1)S(1)} %get-tuple-element.32), channel_id=1, source_target_pairs={{0,2},{1,3},{2,0},{3,1},{4,6},{5,7},{6,4},{7,5},{8,10},{9,11},{10,... | collective-permute-start | bytes 589832 | tf_op jit(solution)/shard_map/ppermute | solution.py:200
  8.3 2.5 %collective-permute-start.2 = (bf16[256,384]{1,0:T(8,128)(2,1)S(1)}, bf16[256,384]{1,0:T(8,128)(2,1)S(1)}, u32[]{:S(2)}, u32[]{:S(2)}) collective-permute-start(bf16[256,384]{1,0:T(8,128)(2,1)S(1)} %get-tuple-element.33), channel_id=1, source_target_pairs={{0,10},{1,11},{2,8},{3,9},{4,14},{5,15},{6,12},{7,13},{8,2},{9,3},... | collective-permute-start | bytes 589832 | tf_op jit(solution)/shard_map/ppermute | solution.py:200
  10.8 7.7 %collective-permute-done.4.refs_1_ = bf16[128,384]{1,0:T(8,128)(2,1)S(1)} collective-permute-done((bf16[128,384]{1,0:T(8,128)(2,1)S(1)}, bf16[128,384]{1,0:T(8,128)(2,1)S(1)}, u32[]{:S(2)}, u32[]{:S(2)}) %collective-permute-start.4) | collective-permute-done | bytes 98336 | tf_op jit(solution)/shard_map/ppermute | solution.py:200
  18.5 1.6 %collective-permute-done.5.refs_2_ = bf16[128,384]{1,0:T(8,128)(2,1)S(1)} collective-permute-done((bf16[128,384]{1,0:T(8,128)(2,1)S(1)}, bf16[128,384]{1,0:T(8,128)(2,1)S(1)}, u32[]{:S(2)}, u32[]{:S(2)}) %collective-permute-start.5) | collective-permute-done | bytes 98336 | tf_op jit(solution)/shard_map/ppermute | solution.py:200
  20.1 1.0 %collective-permute-start.7 = (bf16[256,384]{1,0:T(8,128)(2,1)S(1)}, bf16[256,384]{1,0:T(8,128)(2,1)S(1)}, u32[]{:S(2)}, u32[]{:S(2)}) collective-permute-start(bf16[256,384]{1,0:T(8,128)(2,1)S(1)} %get-tuple-element.49), channel_id=1, source_target_pairs={{0,4},{1,5},{2,6},{3,7},{4,0},{5,1},{6,2},{7,3},{8,12},{9,13},{10,... | collective-permute-start | bytes 589832 | tf_op jit(solution)/shard_map/ppermute | solution.py:200
  21.1 2.7 %collective-permute-start.8 = (bf16[256,384]{1,0:T(8,128)(2,1)S(1)}, bf16[256,384]{1,0:T(8,128)(2,1)S(1)}, u32[]{:S(2)}, u32[]{:S(2)}) collective-permute-start(bf16[256,384]{1,0:T(8,128)(2,1)S(1)} %get-tuple-element.50), channel_id=1, source_target_pairs={{0,12},{1,13},{2,14},{3,15},{4,8},{5,9},{6,10},{7,11},{8,4},{9,5},... | collective-permute-start | bytes 589832 | tf_op jit(solution)/shard_map/ppermute | solution.py:200
  23.9 2.1 %collective-permute-start.6 = (bf16[256,384]{1,0:T(8,128)(2,1)S(1)}, bf16[256,384]{1,0:T(8,128)(2,1)S(1)}, u32[]{:S(2)}, u32[]{:S(2)}) collective-permute-start(bf16[256,384]{1,0:T(8,128)(2,1)S(1)} %get-tuple-element.43), channel_id=1, source_target_pairs={{0,14},{1,15},{2,12},{3,13},{4,10},{5,11},{6,8},{7,9},{8,6},{9,7},... | collective-permute-start | bytes 589832 | tf_op jit(solution)/shard_map/ppermute | solution.py:200
  25.9 0.0 copy-done.11
  25.9 0.0 copy-done.10
  25.9 0.0 copy-done.7
  26.0 3.5 %switch_group.3.refs_14_ = bf16[4,128,384]{2,1,0:T(8,128)(2,1)S(1)} custom-call(bf16[256,384]{1,0:T(8,128)(2,1)S(1)} %get-tuple-element.44.refs_0_, bf16[128,384]{1,0:T(8,128)(2,1)S(1)} %collective-permute-done.4.refs_1_, bf16[128,384]{1,0:T(8,128)(2,1)S(1)} %collective-permute-done.5.refs_2_, bf16[768,1536]{1,0:T(8,128)(2,1)S(1)} %copy-done, ...), custom_call_target="tpu_custom_call" | custom-call | tf_op jit(solution)/shard_map/switch_group/pallas_call | solution.py:174
  29.5 0.0 collective-permute-done.1.refs_0_
  29.5 0.0 collective-permute-done.2.refs_1_
  29.5 0.1 collective-permute-start.3
  29.6 3.5 %switch_group.4.refs_15_ = bf16[4,128,384]{2,1,0:T(8,128)(2,1)S(1)} custom-call(bf16[256,384]{1,0:T(8,128)(2,1)S(1)} %collective-permute-done.1.refs_0_, bf16[256,384]{1,0:T(8,128)(2,1)S(1)} %collective-permute-done.2.refs_1_, bf16[768,1536]{1,0:T(8,128)(2,1)S(1)} %copy-done, bf16[1536,768]{1,0:T(8,128)(2,1)S(1)} %copy-done.1, f32[1536]{0:T(1024)S(1)} %copy-done.4, ...), custom_call_target="tpu_custom_call" | custom-call | tf_op jit(solution)/shard_map/switch_group/pallas_call | solution.py:174
  33.1 0.0 collective-permute-done.7.refs_0_
  33.1 0.8 %collective-permute-done.8.refs_1_ = bf16[256,384]{1,0:T(8,128)(2,1)S(1)} collective-permute-done((bf16[256,384]{1,0:T(8,128)(2,1)S(1)}, bf16[256,384]{1,0:T(8,128)(2,1)S(1)}, u32[]{:S(2)}, u32[]{:S(2)}) %collective-permute-start.8) | collective-permute-done | bytes 196640 | tf_op jit(solution)/shard_map/ppermute | solution.py:200
  34.0 3.5 %switch_group.5.refs_16_ = bf16[4,128,384]{2,1,0:T(8,128)(2,1)S(1)} custom-call(bf16[256,384]{1,0:T(8,128)(2,1)S(1)} %collective-permute-done.7.refs_0_, bf16[256,384]{1,0:T(8,128)(2,1)S(1)} %collective-permute-done.8.refs_1_, bf16[768,1536]{1,0:T(8,128)(2,1)S(1)} %copy-done, bf16[1536,768]{1,0:T(8,128)(2,1)S(1)} %copy-done.1, f32[1536]{0:T(1024)S(1)} %copy-done.4, ...), custom_call_target="tpu_custom_call" | custom-call | flops 2415919104 | bytes 9867264 | tf_op jit(solution)/shard_map/switch_group/pallas_call | solution.py:174
  37.5 1.6 %collective-permute-done.6.refs_1_ = bf16[256,384]{1,0:T(8,128)(2,1)S(1)} collective-permute-done((bf16[256,384]{1,0:T(8,128)(2,1)S(1)}, bf16[256,384]{1,0:T(8,128)(2,1)S(1)}, u32[]{:S(2)}, u32[]{:S(2)}) %collective-permute-start.6) | collective-permute-done | bytes 196640 | tf_op jit(solution)/shard_map/ppermute | solution.py:200
  39.0 3.8 %collective-permute-done.3.refs_0_ = bf16[256,384]{1,0:T(8,128)(2,1)S(1)} collective-permute-done((bf16[256,384]{1,0:T(8,128)(2,1)S(1)}, bf16[256,384]{1,0:T(8,128)(2,1)S(1)}, u32[]{:S(2)}, u32[]{:S(2)}) %collective-permute-start.3) | collective-permute-done | bytes 196640 | tf_op jit(solution)/shard_map/ppermute | solution.py:200
  42.8 5.1 %switch_last.1 = bf16[2,1024,384]{2,1,0:T(8,128)(2,1)} custom-call(bf16[256,384]{1,0:T(8,128)(2,1)S(1)} %collective-permute-done.3.refs_0_, bf16[256,384]{1,0:T(8,128)(2,1)S(1)} %collective-permute-done.6.refs_1_, bf16[768,1536]{1,0:T(8,128)(2,1)S(1)} %copy-done, bf16[1536,768]{1,0:T(8,128)(2,1)S(1)} %copy-done.1, f32[1536]{0:T(1024)S(1)} %copy-done.4, ...), custom_call_target="tpu_custom_call" | custom-call | flops 2415919104 | bytes 11046912 | tf_op jit(solution)/shard_map/switch_last/pallas_call | solution.py:174
  (18 shorter events, 0.0 us)
Async XLA Ops:
  0.0 25.9 %copy-start.11 = (f32[768]{0:T(1024)S(1)}, f32[768]{0:T(1024)}, u32[]{:S(2)}) copy-start(f32[768]{0:T(1024)} %refs_13_.7) | copy-start | bytes 9220
  0.0 25.9 %copy-start.10 = (f32[768]{0:T(1024)S(1)}, f32[768]{0:T(1024)}, u32[]{:S(2)}) copy-start(f32[768]{0:T(1024)} %refs_12_.7) | copy-start | bytes 9220
  0.0 25.9 %copy-start.7 = (f32[1536]{0:T(1024)S(1)}, f32[1536]{0:T(1024)}, u32[]{:S(2)}) copy-start(f32[1536]{0:T(1024)} %refs_11_.7) | copy-start | bytes 18436
  0.0 25.9 %copy-start.6 = (f32[1536]{0:T(1024)S(1)}, f32[1536]{0:T(1024)}, u32[]{:S(2)}) copy-start(f32[1536]{0:T(1024)} %refs_10_.7) | copy-start | bytes 18436
  0.0 25.9 %copy-start.9 = (f32[768]{0:T(1024)S(1)}, f32[768]{0:T(1024)}, u32[]{:S(2)}) copy-start(f32[768]{0:T(1024)} %refs_7_.7) | copy-start | bytes 9220
  0.0 25.9 %copy-start.8 = (f32[768]{0:T(1024)S(1)}, f32[768]{0:T(1024)}, u32[]{:S(2)}) copy-start(f32[768]{0:T(1024)} %refs_6_.7) | copy-start | bytes 9220
  0.0 25.9 %copy-start.5 = (f32[1536]{0:T(1024)S(1)}, f32[1536]{0:T(1024)}, u32[]{:S(2)}) copy-start(f32[1536]{0:T(1024)} %refs_5_.7) | copy-start | bytes 18436
  0.0 25.9 %copy-start.4 = (f32[1536]{0:T(1024)S(1)}, f32[1536]{0:T(1024)}, u32[]{:S(2)}) copy-start(f32[1536]{0:T(1024)} %refs_4_.7) | copy-start | bytes 18436
  0.0 1.5 %copy-start.12 = (bf16[2,1024,384]{2,1,0:T(8,128)(2,1)S(1)}, bf16[2,1024,384]{2,1,0:T(8,128)(2,1)}, u32[]{:S(2)}) copy-start(bf16[2,1024,384]{2,1,0:T(8,128)(2,1)} %x_ref.1) | copy-start | bytes 4718596
  1.5 24.4 %copy-start = (bf16[768,1536]{1,0:T(8,128)(2,1)S(1)}, bf16[768,1536]{1,0:T(8,128)(2,1)}, u32[]{:S(2)}) copy-start(bf16[768,1536]{1,0:T(8,128)(2,1)} %refs_2_.5) | copy-start | bytes 7077892
  1.5 24.5 %copy-start.1 = (bf16[1536,768]{1,0:T(8,128)(2,1)S(1)}, bf16[1536,768]{1,0:T(8,128)(2,1)}, u32[]{:S(2)}) copy-start(bf16[1536,768]{1,0:T(8,128)(2,1)} %refs_3_.7) | copy-start | bytes 7077892
  1.5 24.5 %copy-start.2 = (bf16[768,1536]{1,0:T(8,128)(2,1)S(1)}, bf16[768,1536]{1,0:T(8,128)(2,1)}, u32[]{:S(2)}) copy-start(bf16[768,1536]{1,0:T(8,128)(2,1)} %refs_8_.7) | copy-start | bytes 7077892
  1.5 24.5 %copy-start.3 = (bf16[1536,768]{1,0:T(8,128)(2,1)S(1)}, bf16[1536,768]{1,0:T(8,128)(2,1)}, u32[]{:S(2)}) copy-start(bf16[1536,768]{1,0:T(8,128)(2,1)} %refs_9_.7) | copy-start | bytes 7077892
  2.3 4.3 %collective-permute-start = (bf16[7,128,384]{2,1,0:T(8,128)(2,1)S(1)}, bf16[7,128,384]{2,1,0:T(8,128)(2,1)S(1)}, u32[]{:S(2)}, u32[]{:S(2)}) collective-permute-start(bf16[7,128,384]{2,1,0:T(8,128)(2,1)S(1)} %get-tuple-element.29), channel_id=1, source_target_pairs={{0,1},{1,0},{2,3},{3,2},{4,5},{5,4},{6,7},{7,6},{8,9},{9,8},{10,11... | collective-permute-start | bytes 2064392 | tf_op jit(solution)/shard_map/ppermute | solution.py:200
  2.8 15.7 %collective-permute-start.4 = (bf16[128,384]{1,0:T(8,128)(2,1)S(1)}, bf16[128,384]{1,0:T(8,128)(2,1)S(1)}, u32[]{:S(2)}, u32[]{:S(2)}) collective-permute-start(bf16[128,384]{1,0:T(8,128)(2,1)S(1)} %get-tuple-element.38), channel_id=1, source_target_pairs={{0,8},{1,9},{2,10},{3,11},{4,12},{5,13},{6,14},{7,15},{8,0},{9,1},... | collective-permute-start | bytes 294920 | tf_op jit(solution)/shard_map/ppermute | solution.py:200
  6.4 13.7 %collective-permute-start.5 = (bf16[128,384]{1,0:T(8,128)(2,1)S(1)}, bf16[128,384]{1,0:T(8,128)(2,1)S(1)}, u32[]{:S(2)}, u32[]{:S(2)}) collective-permute-start(bf16[128,384]{1,0:T(8,128)(2,1)S(1)} %get-tuple-element.40), channel_id=1, source_target_pairs={{0,9},{1,8},{2,11},{3,10},{4,13},{5,12},{6,15},{7,14},{8,1},{9,0},... | collective-permute-start | bytes 294920 | tf_op jit(solution)/shard_map/ppermute | solution.py:200
  6.6 22.9 %collective-permute-start.1 = (bf16[256,384]{1,0:T(8,128)(2,1)S(1)}, bf16[256,384]{1,0:T(8,128)(2,1)S(1)}, u32[]{:S(2)}, u32[]{:S(2)}) collective-permute-start(bf16[256,384]{1,0:T(8,128)(2,1)S(1)} %get-tuple-element.32), channel_id=1, source_target_pairs={{0,2},{1,3},{2,0},{3,1},{4,6},{5,7},{6,4},{7,5},{8,10},{9,11},{10,... | collective-permute-start | bytes 589832 | tf_op jit(solution)/shard_map/ppermute | solution.py:200
  8.3 21.3 %collective-permute-start.2 = (bf16[256,384]{1,0:T(8,128)(2,1)S(1)}, bf16[256,384]{1,0:T(8,128)(2,1)S(1)}, u32[]{:S(2)}, u32[]{:S(2)}) collective-permute-start(bf16[256,384]{1,0:T(8,128)(2,1)S(1)} %get-tuple-element.33), channel_id=1, source_target_pairs={{0,10},{1,11},{2,8},{3,9},{4,14},{5,15},{6,12},{7,13},{8,2},{9,3},... | collective-permute-start | bytes 589832 | tf_op jit(solution)/shard_map/ppermute | solution.py:200
  20.1 13.0 %collective-permute-start.7 = (bf16[256,384]{1,0:T(8,128)(2,1)S(1)}, bf16[256,384]{1,0:T(8,128)(2,1)S(1)}, u32[]{:S(2)}, u32[]{:S(2)}) collective-permute-start(bf16[256,384]{1,0:T(8,128)(2,1)S(1)} %get-tuple-element.49), channel_id=1, source_target_pairs={{0,4},{1,5},{2,6},{3,7},{4,0},{5,1},{6,2},{7,3},{8,12},{9,13},{10,... | collective-permute-start | bytes 589832 | tf_op jit(solution)/shard_map/ppermute | solution.py:200
  21.1 12.8 %collective-permute-start.8 = (bf16[256,384]{1,0:T(8,128)(2,1)S(1)}, bf16[256,384]{1,0:T(8,128)(2,1)S(1)}, u32[]{:S(2)}, u32[]{:S(2)}) collective-permute-start(bf16[256,384]{1,0:T(8,128)(2,1)S(1)} %get-tuple-element.50), channel_id=1, source_target_pairs={{0,12},{1,13},{2,14},{3,15},{4,8},{5,9},{6,10},{7,11},{8,4},{9,5},... | collective-permute-start | bytes 589832 | tf_op jit(solution)/shard_map/ppermute | solution.py:200
  23.9 15.1 %collective-permute-start.6 = (bf16[256,384]{1,0:T(8,128)(2,1)S(1)}, bf16[256,384]{1,0:T(8,128)(2,1)S(1)}, u32[]{:S(2)}, u32[]{:S(2)}) collective-permute-start(bf16[256,384]{1,0:T(8,128)(2,1)S(1)} %get-tuple-element.43), channel_id=1, source_target_pairs={{0,14},{1,15},{2,12},{3,13},{4,10},{5,11},{6,8},{7,9},{8,6},{9,7},... | collective-permute-start | bytes 589832 | tf_op jit(solution)/shard_map/ppermute | solution.py:200
  29.5 13.3 %collective-permute-start.3 = (bf16[256,384]{1,0:T(8,128)(2,1)S(1)}, bf16[256,384]{1,0:T(8,128)(2,1)S(1)}, u32[]{:S(2)}, u32[]{:S(2)}) collective-permute-start(bf16[256,384]{1,0:T(8,128)(2,1)S(1)} %get-tuple-element.34), channel_id=1, source_target_pairs={{0,6},{1,7},{2,4},{3,5},{4,2},{5,3},{6,0},{7,1},{8,14},{9,15},{10,... | collective-permute-start | bytes 589832 | tf_op jit(solution)/shard_map/ppermute | solution.py:200

commit v6 on v5

--- a/solution.py
+++ b/solution.py
@@ -9,7 +9,7 @@
 
 REACH = 8
 FIRSTS = (REACH, REACH + 1)
-ORDER = ((10, ()), (2, ()), (12, (8,)), (4, (8, 9)), (14, (8, 9)), (6, (2, 10)))
+ORDER = ((10, ()), (2, ()), (12, (8, 9)), (4, (8, 9)), (14, (10,)), (6, (8, 9)))
 WEIGH = (0, 0, 1)
 MIB = 1 << 20
 
@@ -135,32 +135,51 @@
     return [o[:, part] for o in switch_tiles(pairs, *second) for part in halves]
 
 
+def placing(shards, first, groups):
+    near = (lax.axis_index("seq") & (REACH - 1)) >> 1
+    shape = (shards * shards, 4 * shards * groups)
+    row, col = iota2(shape, 0), iota2(shape, 1)
+    group, half, core = first + col // (4 * shards), (col // (2 * shards)) % 2, (col // shards) % 2
+    source = half * REACH + ((group ^ near) * 2 + core)
+    return one_hot((row // shards == col % shards) & (row % shards == source))
+
+
 def group_kernel(blocks, *refs):
     first, second, out, roles = refs[blocks : blocks + 6], refs[blocks + 6 : blocks + 12], refs[-2], refs[-1]
     for i, end in enumerate(group_blocks(refs[:blocks], roles, first, second)):
         out[i] = end
 
 
+def placing_kernel(blocks, shards, *refs):
+    first, second = refs[blocks : blocks + 6], refs[blocks + 6 : blocks + 12]
+    done, out, roles = refs[blocks + 12 : -2], refs[-2], refs[-1]
+    ends = group_blocks(refs[:blocks], roles, first, second)
+    tile = shards * shards
+    place = placing(shards, 0, len(done) + 1)
+    streams, rows, _ = out.shape
+    for s in range(streams):
+        for t in range(rows // tile):
+            at = s * (rows // shards) + t * shards
+            parts = [d[i, at : at + shards] for d in done for i in range(4)]
+            parts += [end[at : at + shards] for end in ends]
+            y = dot(place, jnp.concatenate(parts, axis=0))
+            out[s, t * tile : (t + 1) * tile] = y.astype(jnp.bfloat16)
+
+
 def last_kernel(blocks, shards, *refs):
     first, second = refs[blocks : blocks + 6], refs[blocks + 6 : blocks + 12]
-    done, out, roles, whole, sems = refs[blocks + 12 : -4], refs[-4], refs[-3], refs[-2], refs[-1]
+    placed, out, roles, whole, sems = refs[blocks + 12], refs[-4], refs[-3], refs[-2], refs[-1]
     ends = group_blocks(refs[:blocks], roles, first, second)
-    me = lax.axis_index("seq")
-    near = (me & (REACH - 1)) >> 1
     tile = shards * shards
-    row, col = iota2((tile, tile), 0), iota2((tile, tile), 1)
-    group, half, core = col // (4 * shards), (col // (2 * shards)) % 2, (col // shards) % 2
-    source = half * REACH + ((group ^ near) * 2 + core)
-    place = one_hot((row // shards == col % shards) & (row % shards == source))
+    place = placing(shards, REACH // 2 - 1, 1)
     streams, rows, _ = whole.shape
     copies = []
     for s in range(streams):
         for t in range(rows // tile):
             at = s * (rows // shards) + t * shards
-            parts = [d[i, at : at + shards] for d in done for i in range(4)]
-            parts += [end[at : at + shards] for end in ends]
             to = (s, slice(t * tile, (t + 1) * tile))
-            whole[to] = dot(place, jnp.concatenate(parts, axis=0)).astype(jnp.bfloat16)
+            y = dot(place, jnp.concatenate([end[at : at + shards] for end in ends], axis=0))
+            whole[to] = placed[to] + y.astype(jnp.bfloat16)
             copies.append(pltpu.make_async_copy(whole.at[to], out.at[to], sems.at[s, t]))
             copies[-1].start()
     for copy in copies:
@@ -210,13 +229,19 @@
     block = jax.ShapeDtypeStruct((4, count, width), features.dtype)
     whole = jax.ShapeDtypeStruct(features.shape, features.dtype)
     ends = []
+
+    def placing_part(blocks, *refs):
+        placing_kernel(blocks, shards, *refs)
+
     for g in range(groups):
         far = FIRSTS if g == 0 else (REACH + 2 * g,)
         blocks = [got[2 * g], *(got[mask] for mask in far)]
-        if g < groups - 1:
+        if g < groups - 2:
             ends.append(
                 run_group(group_kernel, blocks, count, params, (), block, pltpu.VMEM, (), "switch_group", WEIGH[g])
             )
+        elif g < groups - 1:
+            placed = run_group(placing_part, blocks, count, params, tuple(ends), whole, pltpu.VMEM, (), "switch_place", WEIGH[g])
 
     def kernel(blocks, *refs):
         last_kernel(blocks, shards, *refs)
@@ -224,7 +249,7 @@
     streams, rows, _ = features.shape
     sems = pltpu.SemaphoreType.DMA((streams, rows // (shards * shards)))
     scratch = (pltpu.VMEM(whole.shape, whole.dtype), sems)
-    return run_group(kernel, blocks, count, params, tuple(ends), whole, pltpu.HBM, scratch, "switch_last")
+    return run_group(kernel, blocks, count, params, (placed,), whole, pltpu.HBM, scratch, "switch_last")
 
 
 def gathered(features, first, second):

time: 49 us -> 48.4 us (0.988)
  starting transfers between devices: 14.3 us -> 12.6 us
  waiting for transfers between devices: 15.5 us -> 16.5 us
  Pallas kernels: 16.3 us -> 16.9 us
    ppermute x9, starting transfers between devices: 14.3 us -> 12.6 us  [send(): lax.ppermute(value, 'seq', [(d, d ^ mask) for d in range(shards)])]
    ppermute x9, waiting for transfers between devices: 15.5 us -> 16.5 us  [send(): lax.ppermute(value, 'seq', [(d, d ^ mask) for d in range(shards)])]
    pallas_call x4, Pallas kernels: 15.5 us -> 16.1 us  [run_group(): pl.pallas_call(functools.partial(kernel, len(blocks)), out_shape=out_shap...]
  transfers between devices with their start and end apart: 9 -> 9, of which waited for: 5 -> 5; matrix products, arithmetic and copies ran while one was open for 0% -> 0% of each run, Pallas kernels for 22% -> 24%
where the time goes in v6:
time: 48.4 us; the launch traced here: 47.8 us
  Pallas kernels  16.9 us (35%)
  waiting for transfers between devices  16.5 us (34%)
  starting transfers between devices  12.6 us (26%)
  local copies, waits for them, and re-layouts  1.53 us (3%)
    ppermute x9, waiting for transfers between devices, send(): lax.ppermute(value, 'seq', [(d, d ^ mask) for d in range(shards)])  16.5 us
    pallas_call x4, Pallas kernels, run_group(): pl.pallas_call(functools.partial(kernel, len(blocks)), out_shape=out_shap...  16.1 us
    ppermute x9, starting transfers between devices, send(): lax.ppermute(value, 'seq', [(d, d ^ mask) for d in range(shards)])  12.6 us
    unnamed x26, local copies, waits for them, and re-layouts  1.53 us
  transfers between devices with their start and end apart: 9, of which 5 were waited for; matrix products, arithmetic and copies ran while one was open for 0% of the time, Pallas kernels for 24%

profile of v6, /device:TPU:0, one launch (start us, length us, event | category | flops | bytes accessed | tf_op | source)
XLA Modules:
  0.0 47.8 jit_solution(2187343775158893514)
XLA Ops:
  0.0 0.0 copy-start.8
  0.0 0.0 copy-start.5
  0.0 0.0 copy-start.4
  0.0 0.0 copy-start.12
  0.1 1.5 %copy-done.12 = bf16[2,1024,384]{2,1,0:T(8,128)(2,1)S(1)} copy-done((bf16[2,1024,384]{2,1,0:T(8,128)(2,1)S(1)}, bf16[2,1024,384]{2,1,0:T(8,128)(2,1)}, u32[]{:S(2)}) %copy-start.12) | copy-done | bytes 1572888
  1.5 0.7 %sort_rows.1 = (bf16[128,384]{1,0:T(8,128)(2,1)S(1)}, bf16[7,128,384]{2,1,0:T(8,128)(2,1)S(1)}, bf16[6,128,384]{2,1,0:T(8,128)(2,1)S(1)}, bf16[128,384]{1,0:T(8,128)(2,1)S(1)}, bf16[128,384]{1,0:T(8,128)(2,1)S(1)}) custom-call(bf16[2,1024,384]{2,1,0:T(8,128)(2,1)S(1)} %copy-done.12), custom_call_target="tpu_custom_call" | custom-call | flops 30000001024 | bytes 3145728 | tf_op jit(solution)/shard_map/sort_rows/pallas_call | solution.py:90
  2.3 0.5 %collective-permute-start = (bf16[7,128,384]{2,1,0:T(8,128)(2,1)S(1)}, bf16[7,128,384]{2,1,0:T(8,128)(2,1)S(1)}, u32[]{:S(2)}, u32[]{:S(2)}) collective-permute-start(bf16[7,128,384]{2,1,0:T(8,128)(2,1)S(1)} %get-tuple-element.29), channel_id=1, source_target_pairs={{0,1},{1,0},{2,3},{3,2},{4,5},{5,4},{6,7},{7,6},{8,9},{9,8},{10,11... | collective-permute-start | bytes 2064392 | tf_op jit(solution)/shard_map/ppermute | solution.py:219
  2.8 3.7 %collective-permute-start.1 = (bf16[128,384]{1,0:T(8,128)(2,1)S(1)}, bf16[128,384]{1,0:T(8,128)(2,1)S(1)}, u32[]{:S(2)}, u32[]{:S(2)}) collective-permute-start(bf16[128,384]{1,0:T(8,128)(2,1)S(1)} %get-tuple-element.34), channel_id=1, source_target_pairs={{0,8},{1,9},{2,10},{3,11},{4,12},{5,13},{6,14},{7,15},{8,0},{9,1},... | collective-permute-start | bytes 294920 | tf_op jit(solution)/shard_map/ppermute | solution.py:219
  6.4 0.1 collective-permute-start.2
  6.5 0.0 collective-permute-done.mate
  6.5 0.1 join_rows.1
  6.6 7.7 %collective-permute-done.1.refs_1_ = bf16[128,384]{1,0:T(8,128)(2,1)S(1)} collective-permute-done((bf16[128,384]{1,0:T(8,128)(2,1)S(1)}, bf16[128,384]{1,0:T(8,128)(2,1)S(1)}, u32[]{:S(2)}, u32[]{:S(2)}) %collective-permute-start.1) | collective-permute-done | bytes 98336 | tf_op jit(solution)/shard_map/ppermute | solution.py:219
  14.3 1.6 %collective-permute-done.2.refs_2_ = bf16[128,384]{1,0:T(8,128)(2,1)S(1)} collective-permute-done((bf16[128,384]{1,0:T(8,128)(2,1)S(1)}, bf16[128,384]{1,0:T(8,128)(2,1)S(1)}, u32[]{:S(2)}, u32[]{:S(2)}) %collective-permute-start.2) | collective-permute-done | bytes 98336 | tf_op jit(solution)/shard_map/ppermute | solution.py:219
  15.9 0.8 %collective-permute-start.4 = (bf16[256,384]{1,0:T(8,128)(2,1)S(1)}, bf16[256,384]{1,0:T(8,128)(2,1)S(1)}, u32[]{:S(2)}, u32[]{:S(2)}) collective-permute-start(bf16[256,384]{1,0:T(8,128)(2,1)S(1)} %get-tuple-element.42), channel_id=1, source_target_pairs={{0,10},{1,11},{2,8},{3,9},{4,14},{5,15},{6,12},{7,13},{8,2},{9,3},... | collective-permute-start | bytes 589832 | tf_op jit(solution)/shard_map/ppermute | solution.py:219
  16.7 0.6 %collective-permute-start.8 = (bf16[256,384]{1,0:T(8,128)(2,1)S(1)}, bf16[256,384]{1,0:T(8,128)(2,1)S(1)}, u32[]{:S(2)}, u32[]{:S(2)}) collective-permute-start(bf16[256,384]{1,0:T(8,128)(2,1)S(1)} %get-tuple-element.49), channel_id=1, source_target_pairs={{0,2},{1,3},{2,0},{3,1},{4,6},{5,7},{6,4},{7,5},{8,10},{9,11},{10,... | collective-permute-start | bytes 589832 | tf_op jit(solution)/shard_map/ppermute | solution.py:219
  17.3 4.4 %collective-permute-start.6 = (bf16[256,384]{1,0:T(8,128)(2,1)S(1)}, bf16[256,384]{1,0:T(8,128)(2,1)S(1)}, u32[]{:S(2)}, u32[]{:S(2)}) collective-permute-start(bf16[256,384]{1,0:T(8,128)(2,1)S(1)} %get-tuple-element.44), channel_id=1, source_target_pairs={{0,4},{1,5},{2,6},{3,7},{4,0},{5,1},{6,2},{7,3},{8,12},{9,13},{10,... | collective-permute-start | bytes 589832 | tf_op jit(solution)/shard_map/ppermute | solution.py:219
  21.7 0.1 collective-permute-start.7
  21.7 1.1 %collective-permute-start.3 = (bf16[256,384]{1,0:T(8,128)(2,1)S(1)}, bf16[256,384]{1,0:T(8,128)(2,1)S(1)}, u32[]{:S(2)}, u32[]{:S(2)}) collective-permute-start(bf16[256,384]{1,0:T(8,128)(2,1)S(1)} %get-tuple-element.40), channel_id=1, source_target_pairs={{0,6},{1,7},{2,4},{3,5},{4,2},{5,3},{6,0},{7,1},{8,14},{9,15},{10,... | collective-permute-start | bytes 589832 | tf_op jit(solution)/shard_map/ppermute | solution.py:219
  22.8 0.0 copy-done.11
  22.8 0.0 copy-done.10
  22.8 0.0 copy-done.7
  22.9 3.5 %switch_group.2.refs_14_ = bf16[4,128,384]{2,1,0:T(8,128)(2,1)S(1)} custom-call(bf16[256,384]{1,0:T(8,128)(2,1)S(1)} %get-tuple-element.46.refs_0_, bf16[128,384]{1,0:T(8,128)(2,1)S(1)} %collective-permute-done.1.refs_1_, bf16[128,384]{1,0:T(8,128)(2,1)S(1)} %collective-permute-done.2.refs_2_, bf16[768,1536]{1,0:T(8,128)(2,1)S(1)} %copy-done, ...), custom_call_target="tpu_custom_call" | custom-call | tf_op jit(solution)/shard_map/switch_group/pallas_call | solution.py:193
  26.4 3.4 %collective-permute-done.4.refs_1_ = bf16[256,384]{1,0:T(8,128)(2,1)S(1)} collective-permute-done((bf16[256,384]{1,0:T(8,128)(2,1)S(1)}, bf16[256,384]{1,0:T(8,128)(2,1)S(1)}, u32[]{:S(2)}, u32[]{:S(2)}) %collective-permute-start.4) | collective-permute-done | bytes 196640 | tf_op jit(solution)/shard_map/ppermute | solution.py:219
  29.8 1.4 %collective-permute-start.5 = (bf16[256,384]{1,0:T(8,128)(2,1)S(1)}, bf16[256,384]{1,0:T(8,128)(2,1)S(1)}, u32[]{:S(2)}, u32[]{:S(2)}) collective-permute-start(bf16[256,384]{1,0:T(8,128)(2,1)S(1)} %get-tuple-element.43), channel_id=1, source_target_pairs={{0,14},{1,15},{2,12},{3,13},{4,10},{5,11},{6,8},{7,9},{8,6},{9,7},... | collective-permute-start | bytes 589832 | tf_op jit(solution)/shard_map/ppermute | solution.py:219
  31.3 0.0 collective-permute-done.8.refs_0_
  31.3 3.5 %switch_group.3.refs_15_ = bf16[4,128,384]{2,1,0:T(8,128)(2,1)S(1)} custom-call(bf16[256,384]{1,0:T(8,128)(2,1)S(1)} %collective-permute-done.8.refs_0_, bf16[256,384]{1,0:T(8,128)(2,1)S(1)} %collective-permute-done.4.refs_1_, bf16[768,1536]{1,0:T(8,128)(2,1)S(1)} %copy-done, bf16[1536,768]{1,0:T(8,128)(2,1)S(1)} %copy-done.1, f32[1536]{0:T(1024)S(1)} %copy-done.4, ...), custom_call_target="tpu_custom_call" | custom-call | tf_op jit(solution)/shard_map/switch_group/pallas_call | solution.py:193
  34.7 0.7 %collective-permute-done.6.refs_0_ = bf16[256,384]{1,0:T(8,128)(2,1)S(1)} collective-permute-done((bf16[256,384]{1,0:T(8,128)(2,1)S(1)}, bf16[256,384]{1,0:T(8,128)(2,1)S(1)}, u32[]{:S(2)}, u32[]{:S(2)}) %collective-permute-start.6) | collective-permute-done | bytes 196640 | tf_op jit(solution)/shard_map/ppermute | solution.py:219
  35.4 0.0 collective-permute-done.7.refs_1_
  35.4 4.3 %switch_place.1.refs_14_ = bf16[2,1024,384]{2,1,0:T(8,128)(2,1)S(1)} custom-call(bf16[256,384]{1,0:T(8,128)(2,1)S(1)} %collective-permute-done.6.refs_0_, bf16[256,384]{1,0:T(8,128)(2,1)S(1)} %collective-permute-done.7.refs_1_, bf16[768,1536]{1,0:T(8,128)(2,1)S(1)} %copy-done, bf16[1536,768]{1,0:T(8,128)(2,1)S(1)} %copy-done.1, f32[1536]{0:T(1024)S(1)} %copy-done.4, ...), custom_call_target="tpu_custom_call" | custom-call | flops 2415919104 | bytes 10653696 | tf_op jit(solution)/shard_map/switch_place/pallas_call | solution.py:193
  39.7 0.0 collective-permute-done.3.refs_0_
  39.8 3.1 %collective-permute-done.5.refs_1_ = bf16[256,384]{1,0:T(8,128)(2,1)S(1)} collective-permute-done((bf16[256,384]{1,0:T(8,128)(2,1)S(1)}, bf16[256,384]{1,0:T(8,128)(2,1)S(1)}, u32[]{:S(2)}, u32[]{:S(2)}) %collective-permute-start.5) | collective-permute-done | bytes 196640 | tf_op jit(solution)/shard_map/ppermute | solution.py:219
  42.8 4.8 %switch_last.1 = bf16[2,1024,384]{2,1,0:T(8,128)(2,1)} custom-call(bf16[256,384]{1,0:T(8,128)(2,1)S(1)} %collective-permute-done.3.refs_0_, bf16[256,384]{1,0:T(8,128)(2,1)S(1)} %collective-permute-done.5.refs_1_, bf16[768,1536]{1,0:T(8,128)(2,1)S(1)} %copy-done, bf16[1536,768]{1,0:T(8,128)(2,1)S(1)} %copy-done.1, f32[1536]{0:T(1024)S(1)} %copy-done.4, ...), custom_call_target="tpu_custom_call" | custom-call | flops 2415919104 | bytes 11440128 | tf_op jit(solution)/shard_map/switch_last/pallas_call | solution.py:193
  (18 shorter events, 0.0 us)
Async XLA Ops:
  0.0 22.8 %copy-start.11 = (f32[768]{0:T(1024)S(1)}, f32[768]{0:T(1024)}, u32[]{:S(2)}) copy-start(f32[768]{0:T(1024)} %refs_13_.7) | copy-start | bytes 9220
  0.0 22.8 %copy-start.10 = (f32[768]{0:T(1024)S(1)}, f32[768]{0:T(1024)}, u32[]{:S(2)}) copy-start(f32[768]{0:T(1024)} %refs_12_.7) | copy-start | bytes 9220
  0.0 22.8 %copy-start.7 = (f32[1536]{0:T(1024)S(1)}, f32[1536]{0:T(1024)}, u32[]{:S(2)}) copy-start(f32[1536]{0:T(1024)} %refs_11_.7) | copy-start | bytes 18436
  0.0 22.8 %copy-start.6 = (f32[1536]{0:T(1024)S(1)}, f32[1536]{0:T(1024)}, u32[]{:S(2)}) copy-start(f32[1536]{0:T(1024)} %refs_10_.7) | copy-start | bytes 18436
  0.0 22.8 %copy-start.9 = (f32[768]{0:T(1024)S(1)}, f32[768]{0:T(1024)}, u32[]{:S(2)}) copy-start(f32[768]{0:T(1024)} %refs_7_.7) | copy-start | bytes 9220
  0.0 22.8 %copy-start.8 = (f32[768]{0:T(1024)S(1)}, f32[768]{0:T(1024)}, u32[]{:S(2)}) copy-start(f32[768]{0:T(1024)} %refs_6_.7) | copy-start | bytes 9220
  0.0 22.8 %copy-start.5 = (f32[1536]{0:T(1024)S(1)}, f32[1536]{0:T(1024)}, u32[]{:S(2)}) copy-start(f32[1536]{0:T(1024)} %refs_5_.7) | copy-start | bytes 18436
  0.0 22.8 %copy-start.4 = (f32[1536]{0:T(1024)S(1)}, f32[1536]{0:T(1024)}, u32[]{:S(2)}) copy-start(f32[1536]{0:T(1024)} %refs_4_.7) | copy-start | bytes 18436
  0.0 1.5 %copy-start.12 = (bf16[2,1024,384]{2,1,0:T(8,128)(2,1)S(1)}, bf16[2,1024,384]{2,1,0:T(8,128)(2,1)}, u32[]{:S(2)}) copy-start(bf16[2,1024,384]{2,1,0:T(8,128)(2,1)} %x_ref.1) | copy-start | bytes 4718596
  1.5 21.3 %copy-start = (bf16[768,1536]{1,0:T(8,128)(2,1)S(1)}, bf16[768,1536]{1,0:T(8,128)(2,1)}, u32[]{:S(2)}) copy-start(bf16[768,1536]{1,0:T(8,128)(2,1)} %refs_2_.5) | copy-start | bytes 7077892
  1.5 21.3 %copy-start.1 = (bf16[1536,768]{1,0:T(8,128)(2,1)S(1)}, bf16[1536,768]{1,0:T(8,128)(2,1)}, u32[]{:S(2)}) copy-start(bf16[1536,768]{1,0:T(8,128)(2,1)} %refs_3_.7) | copy-start | bytes 7077892
  1.5 21.3 %copy-start.2 = (bf16[768,1536]{1,0:T(8,128)(2,1)S(1)}, bf16[768,1536]{1,0:T(8,128)(2,1)}, u32[]{:S(2)}) copy-start(bf16[768,1536]{1,0:T(8,128)(2,1)} %refs_8_.7) | copy-start | bytes 7077892
  1.5 21.4 %copy-start.3 = (bf16[1536,768]{1,0:T(8,128)(2,1)S(1)}, bf16[1536,768]{1,0:T(8,128)(2,1)}, u32[]{:S(2)}) copy-start(bf16[1536,768]{1,0:T(8,128)(2,1)} %refs_9_.7) | copy-start | bytes 7077892
  2.3 4.3 %collective-permute-start = (bf16[7,128,384]{2,1,0:T(8,128)(2,1)S(1)}, bf16[7,128,384]{2,1,0:T(8,128)(2,1)S(1)}, u32[]{:S(2)}, u32[]{:S(2)}) collective-permute-start(bf16[7,128,384]{2,1,0:T(8,128)(2,1)S(1)} %get-tuple-element.29), channel_id=1, source_target_pairs={{0,1},{1,0},{2,3},{3,2},{4,5},{5,4},{6,7},{7,6},{8,9},{9,8},{10,11... | collective-permute-start | bytes 2064392 | tf_op jit(solution)/shard_map/ppermute | solution.py:219
  2.8 11.5 %collective-permute-start.1 = (bf16[128,384]{1,0:T(8,128)(2,1)S(1)}, bf16[128,384]{1,0:T(8,128)(2,1)S(1)}, u32[]{:S(2)}, u32[]{:S(2)}) collective-permute-start(bf16[128,384]{1,0:T(8,128)(2,1)S(1)} %get-tuple-element.34), channel_id=1, source_target_pairs={{0,8},{1,9},{2,10},{3,11},{4,12},{5,13},{6,14},{7,15},{8,0},{9,1},... | collective-permute-start | bytes 294920 | tf_op jit(solution)/shard_map/ppermute | solution.py:219
  6.4 9.4 %collective-permute-start.2 = (bf16[128,384]{1,0:T(8,128)(2,1)S(1)}, bf16[128,384]{1,0:T(8,128)(2,1)S(1)}, u32[]{:S(2)}, u32[]{:S(2)}) collective-permute-start(bf16[128,384]{1,0:T(8,128)(2,1)S(1)} %get-tuple-element.35), channel_id=1, source_target_pairs={{0,9},{1,8},{2,11},{3,10},{4,13},{5,12},{6,15},{7,14},{8,1},{9,0},... | collective-permute-start | bytes 294920 | tf_op jit(solution)/shard_map/ppermute | solution.py:219
  15.9 14.0 %collective-permute-start.4 = (bf16[256,384]{1,0:T(8,128)(2,1)S(1)}, bf16[256,384]{1,0:T(8,128)(2,1)S(1)}, u32[]{:S(2)}, u32[]{:S(2)}) collective-permute-start(bf16[256,384]{1,0:T(8,128)(2,1)S(1)} %get-tuple-element.42), channel_id=1, source_target_pairs={{0,10},{1,11},{2,8},{3,9},{4,14},{5,15},{6,12},{7,13},{8,2},{9,3},... | collective-permute-start | bytes 589832 | tf_op jit(solution)/shard_map/ppermute | solution.py:219
  16.7 14.5 %collective-permute-start.8 = (bf16[256,384]{1,0:T(8,128)(2,1)S(1)}, bf16[256,384]{1,0:T(8,128)(2,1)S(1)}, u32[]{:S(2)}, u32[]{:S(2)}) collective-permute-start(bf16[256,384]{1,0:T(8,128)(2,1)S(1)} %get-tuple-element.49), channel_id=1, source_target_pairs={{0,2},{1,3},{2,0},{3,1},{4,6},{5,7},{6,4},{7,5},{8,10},{9,11},{10,... | collective-permute-start | bytes 589832 | tf_op jit(solution)/shard_map/ppermute | solution.py:219
  17.3 18.1 %collective-permute-start.6 = (bf16[256,384]{1,0:T(8,128)(2,1)S(1)}, bf16[256,384]{1,0:T(8,128)(2,1)S(1)}, u32[]{:S(2)}, u32[]{:S(2)}) collective-permute-start(bf16[256,384]{1,0:T(8,128)(2,1)S(1)} %get-tuple-element.44), channel_id=1, source_target_pairs={{0,4},{1,5},{2,6},{3,7},{4,0},{5,1},{6,2},{7,3},{8,12},{9,13},{10,... | collective-permute-start | bytes 589832 | tf_op jit(solution)/shard_map/ppermute | solution.py:219
  21.7 13.7 %collective-permute-start.7 = (bf16[256,384]{1,0:T(8,128)(2,1)S(1)}, bf16[256,384]{1,0:T(8,128)(2,1)S(1)}, u32[]{:S(2)}, u32[]{:S(2)}) collective-permute-start(bf16[256,384]{1,0:T(8,128)(2,1)S(1)} %get-tuple-element.45), channel_id=1, source_target_pairs={{0,12},{1,13},{2,14},{3,15},{4,8},{5,9},{6,10},{7,11},{8,4},{9,5},... | collective-permute-start | bytes 589832 | tf_op jit(solution)/shard_map/ppermute | solution.py:219
  21.7 18.0 %collective-permute-start.3 = (bf16[256,384]{1,0:T(8,128)(2,1)S(1)}, bf16[256,384]{1,0:T(8,128)(2,1)S(1)}, u32[]{:S(2)}, u32[]{:S(2)}) collective-permute-start(bf16[256,384]{1,0:T(8,128)(2,1)S(1)} %get-tuple-element.40), channel_id=1, source_target_pairs={{0,6},{1,7},{2,4},{3,5},{4,2},{5,3},{6,0},{7,1},{8,14},{9,15},{10,... | collective-permute-start | bytes 589832 | tf_op jit(solution)/shard_map/ppermute | solution.py:219
  29.8 13.0 %collective-permute-start.5 = (bf16[256,384]{1,0:T(8,128)(2,1)S(1)}, bf16[256,384]{1,0:T(8,128)(2,1)S(1)}, u32[]{:S(2)}, u32[]{:S(2)}) collective-permute-start(bf16[256,384]{1,0:T(8,128)(2,1)S(1)} %get-tuple-element.43), channel_id=1, source_target_pairs={{0,14},{1,15},{2,12},{3,13},{4,10},{5,11},{6,8},{7,9},{8,6},{9,7},... | collective-permute-start | bytes 589832 | tf_op jit(solution)/shard_map/ppermute | solution.py:219

commit v7 on v6

--- a/solution.py
+++ b/solution.py
@@ -174,12 +174,14 @@
     place = placing(shards, REACH // 2 - 1, 1)
     streams, rows, _ = whole.shape
     copies = []
-    for s in range(streams):
-        for t in range(rows // tile):
-            at = s * (rows // shards) + t * shards
+    width = whole.shape[2]
+    for t in range(rows // tile):
+        each = [slice(s * (rows // shards) + t * shards, s * (rows // shards) + (t + 1) * shards) for s in range(streams)]
+        sides = [jnp.concatenate([end[at] for end in ends], axis=0) for at in each]
+        y = dot(place, jnp.concatenate(sides, axis=-1)).astype(jnp.bfloat16)
+        for s in range(streams):
             to = (s, slice(t * tile, (t + 1) * tile))
-            y = dot(place, jnp.concatenate([end[at : at + shards] for end in ends], axis=0))
-            whole[to] = placed[to] + y.astype(jnp.bfloat16)
+            whole[to] = placed[to] + y[:, s * width : (s + 1) * width]
             copies.append(pltpu.make_async_copy(whole.at[to], out.at[to], sems.at[s, t]))
             copies[-1].start()
     for copy in copies:

time: 48.4 us -> 48.5 us (level)
  no operation moved by 1% of the time
where the time goes in v7:
time: 48.5 us; the launch traced here: 47.8 us
  Pallas kernels  16.9 us (35%)
  waiting for transfers between devices  16.5 us (34%)
  starting transfers between devices  12.6 us (26%)
  local copies, waits for them, and re-layouts  1.53 us (3%)
    ppermute x9, waiting for transfers between devices, send(): lax.ppermute(value, 'seq', [(d, d ^ mask) for d in range(shards)])  16.5 us
    pallas_call x4, Pallas kernels, run_group(): pl.pallas_call(functools.partial(kernel, len(blocks)), out_shape=out_shap...  16.1 us
    ppermute x9, starting transfers between devices, send(): lax.ppermute(value, 'seq', [(d, d ^ mask) for d in range(shards)])  12.6 us
    unnamed x26, local copies, waits for them, and re-layouts  1.53 us
  transfers between devices with their start and end apart: 9, of which 5 were waited for; matrix products, arithmetic and copies ran while one was open for 0% of the time, Pallas kernels for 24%

profile of v7, /device:TPU:0, one launch (start us, length us, event | category | flops | bytes accessed | tf_op | source)
XLA Modules:
  0.0 47.8 jit_solution(9774623207088725303)
XLA Ops:
  0.1 1.5 %copy-done.12 = bf16[2,1024,384]{2,1,0:T(8,128)(2,1)S(1)} copy-done((bf16[2,1024,384]{2,1,0:T(8,128)(2,1)S(1)}, bf16[2,1024,384]{2,1,0:T(8,128)(2,1)}, u32[]{:S(2)}) %copy-start.12) | copy-done | bytes 1572888
  1.5 0.7 %sort_rows.1 = (bf16[128,384]{1,0:T(8,128)(2,1)S(1)}, bf16[7,128,384]{2,1,0:T(8,128)(2,1)S(1)}, bf16[6,128,384]{2,1,0:T(8,128)(2,1)S(1)}, bf16[128,384]{1,0:T(8,128)(2,1)S(1)}, bf16[128,384]{1,0:T(8,128)(2,1)S(1)}) custom-call(bf16[2,1024,384]{2,1,0:T(8,128)(2,1)S(1)} %copy-done.12), custom_call_target="tpu_custom_call" | custom-call | flops 30000001024 | bytes 3145728 | tf_op jit(solution)/shard_map/sort_rows/pallas_call | solution.py:90
  2.3 0.5 %collective-permute-start = (bf16[7,128,384]{2,1,0:T(8,128)(2,1)S(1)}, bf16[7,128,384]{2,1,0:T(8,128)(2,1)S(1)}, u32[]{:S(2)}, u32[]{:S(2)}) collective-permute-start(bf16[7,128,384]{2,1,0:T(8,128)(2,1)S(1)} %get-tuple-element.29), channel_id=1, source_target_pairs={{0,1},{1,0},{2,3},{3,2},{4,5},{5,4},{6,7},{7,6},{8,9},{9,8},{10,11... | collective-permute-start | bytes 2064392 | tf_op jit(solution)/shard_map/ppermute | solution.py:221
  2.8 3.7 %collective-permute-start.1 = (bf16[128,384]{1,0:T(8,128)(2,1)S(1)}, bf16[128,384]{1,0:T(8,128)(2,1)S(1)}, u32[]{:S(2)}, u32[]{:S(2)}) collective-permute-start(bf16[128,384]{1,0:T(8,128)(2,1)S(1)} %get-tuple-element.34), channel_id=1, source_target_pairs={{0,8},{1,9},{2,10},{3,11},{4,12},{5,13},{6,14},{7,15},{8,0},{9,1},... | collective-permute-start | bytes 294920 | tf_op jit(solution)/shard_map/ppermute | solution.py:221
  6.4 0.1 collective-permute-start.2
  6.5 0.0 collective-permute-done.mate
  6.5 0.1 join_rows.1
  6.6 7.7 %collective-permute-done.1.refs_1_ = bf16[128,384]{1,0:T(8,128)(2,1)S(1)} collective-permute-done((bf16[128,384]{1,0:T(8,128)(2,1)S(1)}, bf16[128,384]{1,0:T(8,128)(2,1)S(1)}, u32[]{:S(2)}, u32[]{:S(2)}) %collective-permute-start.1) | collective-permute-done | bytes 98336 | tf_op jit(solution)/shard_map/ppermute | solution.py:221
  14.3 1.6 %collective-permute-done.2.refs_2_ = bf16[128,384]{1,0:T(8,128)(2,1)S(1)} collective-permute-done((bf16[128,384]{1,0:T(8,128)(2,1)S(1)}, bf16[128,384]{1,0:T(8,128)(2,1)S(1)}, u32[]{:S(2)}, u32[]{:S(2)}) %collective-permute-start.2) | collective-permute-done | bytes 98336 | tf_op jit(solution)/shard_map/ppermute | solution.py:221
  15.9 0.8 %collective-permute-start.4 = (bf16[256,384]{1,0:T(8,128)(2,1)S(1)}, bf16[256,384]{1,0:T(8,128)(2,1)S(1)}, u32[]{:S(2)}, u32[]{:S(2)}) collective-permute-start(bf16[256,384]{1,0:T(8,128)(2,1)S(1)} %get-tuple-element.42), channel_id=1, source_target_pairs={{0,10},{1,11},{2,8},{3,9},{4,14},{5,15},{6,12},{7,13},{8,2},{9,3},... | collective-permute-start | bytes 589832 | tf_op jit(solution)/shard_map/ppermute | solution.py:221
  16.7 0.6 %collective-permute-start.8 = (bf16[256,384]{1,0:T(8,128)(2,1)S(1)}, bf16[256,384]{1,0:T(8,128)(2,1)S(1)}, u32[]{:S(2)}, u32[]{:S(2)}) collective-permute-start(bf16[256,384]{1,0:T(8,128)(2,1)S(1)} %get-tuple-element.49), channel_id=1, source_target_pairs={{0,2},{1,3},{2,0},{3,1},{4,6},{5,7},{6,4},{7,5},{8,10},{9,11},{10,... | collective-permute-start | bytes 589832 | tf_op jit(solution)/shard_map/ppermute | solution.py:221
  17.3 4.4 %collective-permute-start.6 = (bf16[256,384]{1,0:T(8,128)(2,1)S(1)}, bf16[256,384]{1,0:T(8,128)(2,1)S(1)}, u32[]{:S(2)}, u32[]{:S(2)}) collective-permute-start(bf16[256,384]{1,0:T(8,128)(2,1)S(1)} %get-tuple-element.44), channel_id=1, source_target_pairs={{0,4},{1,5},{2,6},{3,7},{4,0},{5,1},{6,2},{7,3},{8,12},{9,13},{10,... | collective-permute-start | bytes 589832 | tf_op jit(solution)/shard_map/ppermute | solution.py:221
  21.7 0.1 collective-permute-start.7
  21.7 1.1 %collective-permute-start.3 = (bf16[256,384]{1,0:T(8,128)(2,1)S(1)}, bf16[256,384]{1,0:T(8,128)(2,1)S(1)}, u32[]{:S(2)}, u32[]{:S(2)}) collective-permute-start(bf16[256,384]{1,0:T(8,128)(2,1)S(1)} %get-tuple-element.40), channel_id=1, source_target_pairs={{0,6},{1,7},{2,4},{3,5},{4,2},{5,3},{6,0},{7,1},{8,14},{9,15},{10,... | collective-permute-start | bytes 589832 | tf_op jit(solution)/shard_map/ppermute | solution.py:221
  22.8 0.0 copy-done.11
  22.8 0.0 copy-done.9
  22.8 0.0 copy-done.8
  22.8 0.0 copy-done.5
  22.9 0.0 copy-done.4
  22.9 0.0 copy-done
  22.9 0.0 copy-done.1
  22.9 3.5 %switch_group.2.refs_14_ = bf16[4,128,384]{2,1,0:T(8,128)(2,1)S(1)} custom-call(bf16[256,384]{1,0:T(8,128)(2,1)S(1)} %get-tuple-element.46.refs_0_, bf16[128,384]{1,0:T(8,128)(2,1)S(1)} %collective-permute-done.1.refs_1_, bf16[128,384]{1,0:T(8,128)(2,1)S(1)} %collective-permute-done.2.refs_2_, bf16[768,1536]{1,0:T(8,128)(2,1)S(1)} %copy-done, ...), custom_call_target="tpu_custom_call" | custom-call | tf_op jit(solution)/shard_map/switch_group/pallas_call | solution.py:195
  26.4 3.4 %collective-permute-done.4.refs_1_ = bf16[256,384]{1,0:T(8,128)(2,1)S(1)} collective-permute-done((bf16[256,384]{1,0:T(8,128)(2,1)S(1)}, bf16[256,384]{1,0:T(8,128)(2,1)S(1)}, u32[]{:S(2)}, u32[]{:S(2)}) %collective-permute-start.4) | collective-permute-done | bytes 196640 | tf_op jit(solution)/shard_map/ppermute | solution.py:221
  29.8 1.4 %collective-permute-start.5 = (bf16[256,384]{1,0:T(8,128)(2,1)S(1)}, bf16[256,384]{1,0:T(8,128)(2,1)S(1)}, u32[]{:S(2)}, u32[]{:S(2)}) collective-permute-start(bf16[256,384]{1,0:T(8,128)(2,1)S(1)} %get-tuple-element.43), channel_id=1, source_target_pairs={{0,14},{1,15},{2,12},{3,13},{4,10},{5,11},{6,8},{7,9},{8,6},{9,7},... | collective-permute-start | bytes 589832 | tf_op jit(solution)/shard_map/ppermute | solution.py:221
  31.3 0.0 collective-permute-done.8.refs_0_
  31.3 3.5 %switch_group.3.refs_15_ = bf16[4,128,384]{2,1,0:T(8,128)(2,1)S(1)} custom-call(bf16[256,384]{1,0:T(8,128)(2,1)S(1)} %collective-permute-done.8.refs_0_, bf16[256,384]{1,0:T(8,128)(2,1)S(1)} %collective-permute-done.4.refs_1_, bf16[768,1536]{1,0:T(8,128)(2,1)S(1)} %copy-done, bf16[1536,768]{1,0:T(8,128)(2,1)S(1)} %copy-done.1, f32[1536]{0:T(1024)S(1)} %copy-done.4, ...), custom_call_target="tpu_custom_call" | custom-call | tf_op jit(solution)/shard_map/switch_group/pallas_call | solution.py:195
  34.7 0.7 %collective-permute-done.6.refs_0_ = bf16[256,384]{1,0:T(8,128)(2,1)S(1)} collective-permute-done((bf16[256,384]{1,0:T(8,128)(2,1)S(1)}, bf16[256,384]{1,0:T(8,128)(2,1)S(1)}, u32[]{:S(2)}, u32[]{:S(2)}) %collective-permute-start.6) | collective-permute-done | bytes 196640 | tf_op jit(solution)/shard_map/ppermute | solution.py:221
  35.4 0.0 collective-permute-done.7.refs_1_
  35.4 4.3 %switch_place.1.refs_14_ = bf16[2,1024,384]{2,1,0:T(8,128)(2,1)S(1)} custom-call(bf16[256,384]{1,0:T(8,128)(2,1)S(1)} %collective-permute-done.6.refs_0_, bf16[256,384]{1,0:T(8,128)(2,1)S(1)} %collective-permute-done.7.refs_1_, bf16[768,1536]{1,0:T(8,128)(2,1)S(1)} %copy-done, bf16[1536,768]{1,0:T(8,128)(2,1)S(1)} %copy-done.1, f32[1536]{0:T(1024)S(1)} %copy-done.4, ...), custom_call_target="tpu_custom_call" | custom-call | flops 2415919104 | bytes 10653696 | tf_op jit(solution)/shard_map/switch_place/pallas_call | solution.py:195
  39.7 0.0 collective-permute-done.3.refs_0_
  39.8 3.1 %collective-permute-done.5.refs_1_ = bf16[256,384]{1,0:T(8,128)(2,1)S(1)} collective-permute-done((bf16[256,384]{1,0:T(8,128)(2,1)S(1)}, bf16[256,384]{1,0:T(8,128)(2,1)S(1)}, u32[]{:S(2)}, u32[]{:S(2)}) %collective-permute-start.5) | collective-permute-done | bytes 196640 | tf_op jit(solution)/shard_map/ppermute | solution.py:221
  42.8 4.8 %switch_last.1 = bf16[2,1024,384]{2,1,0:T(8,128)(2,1)} custom-call(bf16[256,384]{1,0:T(8,128)(2,1)S(1)} %collective-permute-done.3.refs_0_, bf16[256,384]{1,0:T(8,128)(2,1)S(1)} %collective-permute-done.5.refs_1_, bf16[768,1536]{1,0:T(8,128)(2,1)S(1)} %copy-done, bf16[1536,768]{1,0:T(8,128)(2,1)S(1)} %copy-done.1, f32[1536]{0:T(1024)S(1)} %copy-done.4, ...), custom_call_target="tpu_custom_call" | custom-call | flops 2415919104 | bytes 11440128 | tf_op jit(solution)/shard_map/switch_last/pallas_call | solution.py:195
  (18 shorter events, 0.0 us)
Async XLA Ops:
  0.0 22.8 %copy-start.11 = (f32[768]{0:T(1024)S(1)}, f32[768]{0:T(1024)}, u32[]{:S(2)}) copy-start(f32[768]{0:T(1024)} %refs_13_.7) | copy-start | bytes 9220
  0.0 22.8 %copy-start.10 = (f32[768]{0:T(1024)S(1)}, f32[768]{0:T(1024)}, u32[]{:S(2)}) copy-start(f32[768]{0:T(1024)} %refs_12_.7) | copy-start | bytes 9220
  0.0 22.8 %copy-start.7 = (f32[1536]{0:T(1024)S(1)}, f32[1536]{0:T(1024)}, u32[]{:S(2)}) copy-start(f32[1536]{0:T(1024)} %refs_11_.7) | copy-start | bytes 18436
  0.0 22.8 %copy-start.6 = (f32[1536]{0:T(1024)S(1)}, f32[1536]{0:T(1024)}, u32[]{:S(2)}) copy-start(f32[1536]{0:T(1024)} %refs_10_.7) | copy-start | bytes 18436
  0.0 22.8 %copy-start.9 = (f32[768]{0:T(1024)S(1)}, f32[768]{0:T(1024)}, u32[]{:S(2)}) copy-start(f32[768]{0:T(1024)} %refs_7_.7) | copy-start | bytes 9220
  0.0 22.8 %copy-start.8 = (f32[768]{0:T(1024)S(1)}, f32[768]{0:T(1024)}, u32[]{:S(2)}) copy-start(f32[768]{0:T(1024)} %refs_6_.7) | copy-start | bytes 9220
  0.0 22.8 %copy-start.5 = (f32[1536]{0:T(1024)S(1)}, f32[1536]{0:T(1024)}, u32[]{:S(2)}) copy-start(f32[1536]{0:T(1024)} %refs_5_.7) | copy-start | bytes 18436
  0.0 22.8 %copy-start.4 = (f32[1536]{0:T(1024)S(1)}, f32[1536]{0:T(1024)}, u32[]{:S(2)}) copy-start(f32[1536]{0:T(1024)} %refs_4_.7) | copy-start | bytes 18436
  0.0 1.5 %copy-start.12 = (bf16[2,1024,384]{2,1,0:T(8,128)(2,1)S(1)}, bf16[2,1024,384]{2,1,0:T(8,128)(2,1)}, u32[]{:S(2)}) copy-start(bf16[2,1024,384]{2,1,0:T(8,128)(2,1)} %x_ref.1) | copy-start | bytes 4718596
  1.5 21.3 %copy-start = (bf16[768,1536]{1,0:T(8,128)(2,1)S(1)}, bf16[768,1536]{1,0:T(8,128)(2,1)}, u32[]{:S(2)}) copy-start(bf16[768,1536]{1,0:T(8,128)(2,1)} %refs_2_.5) | copy-start | bytes 7077892
  1.5 21.3 %copy-start.1 = (bf16[1536,768]{1,0:T(8,128)(2,1)S(1)}, bf16[1536,768]{1,0:T(8,128)(2,1)}, u32[]{:S(2)}) copy-start(bf16[1536,768]{1,0:T(8,128)(2,1)} %refs_3_.7) | copy-start | bytes 7077892
  1.5 21.3 %copy-start.2 = (bf16[768,1536]{1,0:T(8,128)(2,1)S(1)}, bf16[768,1536]{1,0:T(8,128)(2,1)}, u32[]{:S(2)}) copy-start(bf16[768,1536]{1,0:T(8,128)(2,1)} %refs_8_.7) | copy-start | bytes 7077892
  1.5 21.4 %copy-start.3 = (bf16[1536,768]{1,0:T(8,128)(2,1)S(1)}, bf16[1536,768]{1,0:T(8,128)(2,1)}, u32[]{:S(2)}) copy-start(bf16[1536,768]{1,0:T(8,128)(2,1)} %refs_9_.7) | copy-start | bytes 7077892
  2.3 4.3 %collective-permute-start = (bf16[7,128,384]{2,1,0:T(8,128)(2,1)S(1)}, bf16[7,128,384]{2,1,0:T(8,128)(2,1)S(1)}, u32[]{:S(2)}, u32[]{:S(2)}) collective-permute-start(bf16[7,128,384]{2,1,0:T(8,128)(2,1)S(1)} %get-tuple-element.29), channel_id=1, source_target_pairs={{0,1},{1,0},{2,3},{3,2},{4,5},{5,4},{6,7},{7,6},{8,9},{9,8},{10,11... | collective-permute-start | bytes 2064392 | tf_op jit(solution)/shard_map/ppermute | solution.py:221
  2.8 11.5 %collective-permute-start.1 = (bf16[128,384]{1,0:T(8,128)(2,1)S(1)}, bf16[128,384]{1,0:T(8,128)(2,1)S(1)}, u32[]{:S(2)}, u32[]{:S(2)}) collective-permute-start(bf16[128,384]{1,0:T(8,128)(2,1)S(1)} %get-tuple-element.34), channel_id=1, source_target_pairs={{0,8},{1,9},{2,10},{3,11},{4,12},{5,13},{6,14},{7,15},{8,0},{9,1},... | collective-permute-start | bytes 294920 | tf_op jit(solution)/shard_map/ppermute | solution.py:221
  6.4 9.4 %collective-permute-start.2 = (bf16[128,384]{1,0:T(8,128)(2,1)S(1)}, bf16[128,384]{1,0:T(8,128)(2,1)S(1)}, u32[]{:S(2)}, u32[]{:S(2)}) collective-permute-start(bf16[128,384]{1,0:T(8,128)(2,1)S(1)} %get-tuple-element.35), channel_id=1, source_target_pairs={{0,9},{1,8},{2,11},{3,10},{4,13},{5,12},{6,15},{7,14},{8,1},{9,0},... | collective-permute-start | bytes 294920 | tf_op jit(solution)/shard_map/ppermute | solution.py:221
  15.9 14.0 %collective-permute-start.4 = (bf16[256,384]{1,0:T(8,128)(2,1)S(1)}, bf16[256,384]{1,0:T(8,128)(2,1)S(1)}, u32[]{:S(2)}, u32[]{:S(2)}) collective-permute-start(bf16[256,384]{1,0:T(8,128)(2,1)S(1)} %get-tuple-element.42), channel_id=1, source_target_pairs={{0,10},{1,11},{2,8},{3,9},{4,14},{5,15},{6,12},{7,13},{8,2},{9,3},... | collective-permute-start | bytes 589832 | tf_op jit(solution)/shard_map/ppermute | solution.py:221
  16.7 14.5 %collective-permute-start.8 = (bf16[256,384]{1,0:T(8,128)(2,1)S(1)}, bf16[256,384]{1,0:T(8,128)(2,1)S(1)}, u32[]{:S(2)}, u32[]{:S(2)}) collective-permute-start(bf16[256,384]{1,0:T(8,128)(2,1)S(1)} %get-tuple-element.49), channel_id=1, source_target_pairs={{0,2},{1,3},{2,0},{3,1},{4,6},{5,7},{6,4},{7,5},{8,10},{9,11},{10,... | collective-permute-start | bytes 589832 | tf_op jit(solution)/shard_map/ppermute | solution.py:221
  17.3 18.1 %collective-permute-start.6 = (bf16[256,384]{1,0:T(8,128)(2,1)S(1)}, bf16[256,384]{1,0:T(8,128)(2,1)S(1)}, u32[]{:S(2)}, u32[]{:S(2)}) collective-permute-start(bf16[256,384]{1,0:T(8,128)(2,1)S(1)} %get-tuple-element.44), channel_id=1, source_target_pairs={{0,4},{1,5},{2,6},{3,7},{4,0},{5,1},{6,2},{7,3},{8,12},{9,13},{10,... | collective-permute-start | bytes 589832 | tf_op jit(solution)/shard_map/ppermute | solution.py:221
  21.7 13.7 %collective-permute-start.7 = (bf16[256,384]{1,0:T(8,128)(2,1)S(1)}, bf16[256,384]{1,0:T(8,128)(2,1)S(1)}, u32[]{:S(2)}, u32[]{:S(2)}) collective-permute-start(bf16[256,384]{1,0:T(8,128)(2,1)S(1)} %get-tuple-element.45), channel_id=1, source_target_pairs={{0,12},{1,13},{2,14},{3,15},{4,8},{5,9},{6,10},{7,11},{8,4},{9,5},... | collective-permute-start | bytes 589832 | tf_op jit(solution)/shard_map/ppermute | solution.py:221
  21.7 18.0 %collective-permute-start.3 = (bf16[256,384]{1,0:T(8,128)(2,1)S(1)}, bf16[256,384]{1,0:T(8,128)(2,1)S(1)}, u32[]{:S(2)}, u32[]{:S(2)}) collective-permute-start(bf16[256,384]{1,0:T(8,128)(2,1)S(1)} %get-tuple-element.40), channel_id=1, source_target_pairs={{0,6},{1,7},{2,4},{3,5},{4,2},{5,3},{6,0},{7,1},{8,14},{9,15},{10,... | collective-permute-start | bytes 589832 | tf_op jit(solution)/shard_map/ppermute | solution.py:221
  29.8 13.0 %collective-permute-start.5 = (bf16[256,384]{1,0:T(8,128)(2,1)S(1)}, bf16[256,384]{1,0:T(8,128)(2,1)S(1)}, u32[]{:S(2)}, u32[]{:S(2)}) collective-permute-start(bf16[256,384]{1,0:T(8,128)(2,1)S(1)} %get-tuple-element.43), channel_id=1, source_target_pairs={{0,14},{1,15},{2,12},{3,13},{4,10},{5,11},{6,8},{7,9},{8,6},{9,7},... | collective-permute-start | bytes 589832 | tf_op jit(solution)/shard_map/ppermute | solution.py:221
